TPU v7x, 512 devices: a whole 4x4x16 slice. The times are simulated.
512 devices in a mesh: dom: 128 (over x, z, core), blk: 4 (over y).
Axes of the slice: x: 4, y: 4, z: 16, core: 2. Of those that a mesh axis runs over, the one named last changes fastest.
Arguments:
- degree: int32 [1024], P('dom'), may hold values from 1 to 3
- face_elem: int32 [4096], P('dom'), may hold values from 0 to 7
- face_side: int32 [4096], P('dom'), may hold values from 0 to 8, as said below
- face_peer: int32 [4096], P('dom'), may hold values from 0 to 7
- coupling: bfloat16 [4096, 320, 320], P('dom', 'blk'), may hold values from -0.078125 to 0.078125
- inv_diag: float32 [1024, 320], P('dom', 'blk'), may hold values from 0.5 to 2
- inv_off: bfloat16 [1024, 320, 320], P('dom', 'blk'), may hold values from -0.109375 to 0.109375
- source: float32 [1024, 320], P('dom', 'blk'), may hold values from -6 to 6
- residual: float32 [1024, 320], P('dom', 'blk'), may hold values from -0.6 to 0.6
Outputs:
- adjoint: float32 [1024, 320], P('dom', 'blk')
- indicator: float32 [1024], P('dom')
Inputs may be any that keep to these rules, and one draw needn't show every extreme that they name: `face_side`: among the 32 faces of one partition (aligned blocks of 32 rows) each side from 1 to 8 is named by at least 2 and at most 4 faces, and one side by exactly 4; the remaining faces have side 0.
All inputs are finite; a program needn't handle non-finite values.
Results may differ from a plain program's by a relative error of at most 0.004.
Values may be sent and summed in bfloat16 or wider, within the bound.
No kernel may reach another device: no remote copies, remote signals or barrier semaphores. Data moves between devices by JAX's collectives and lax.ppermute only.
A program may use at most 64 MiB of HBM per device.

v0:
```python
import jax
import jax.numpy as jnp
from jax import lax
from jax.sharding import PartitionSpec as P

MODES = 64
SWEEPS = 2
NEIGH = 8


def from_behind(block, axis, distance):
    devices = range(lax.axis_size(axis))
    route = [((i - distance) % len(devices), i) for i in devices]
    return lax.ppermute(block, axis, route)


def full_rows(values):
    return lax.all_gather(values, "blk", axis=1, tiled=True)


def local(degree, face_elem, face_side, face_peer, coupling, inv_diag, inv_off, source, residual):
    width = coupling.shape[2]
    quarter = source.shape[1]
    elements = source.shape[0]
    faces = coupling.shape[0]
    neigh = NEIGH
    half_count = neigh // 2
    capacity = faces // neigh
    offsets = [step_size for step_size in range(1, half_count + 1)] + [
        -step_size for step_size in range(1, half_count + 1)
    ]
    first_row = lax.axis_index("blk") * quarter
    limit = (degree + 1) ** 3 * MODES // 64
    modes = jnp.arange(width, dtype=jnp.int32) % MODES
    mask_full = (modes[None, :] < limit[:, None]).astype(jnp.float32)
    mask_rows = lax.dynamic_slice_in_dim(mask_full, first_row, quarter, 1)
    codes = jnp.arange(neigh + 1, dtype=jnp.int32)
    onehot = (face_side[:, None] == codes[None, :]).astype(jnp.int32)
    before = jnp.cumsum(onehot, axis=0) - onehot
    slot_index = jnp.sum(before * onehot, axis=1)
    crossing = face_side > 0
    inner = jnp.where(crossing, 0.0, 1.0).astype(jnp.float32)
    position = jnp.where(crossing, (face_side - 1) * capacity + slot_index, neigh * capacity)
    safe_position = jnp.minimum(position, neigh * capacity - 1)
    wanted = (
        jnp.zeros((neigh * capacity,), jnp.int32)
        .at[position]
        .set(face_peer, mode="drop")
        .reshape(neigh, capacity)
    )
    requested = jnp.stack(
        [from_behind(wanted[side_num], "dom", offsets[side_num]) for side_num in range(neigh)]
    )
    requested_flat = requested.reshape(-1)

    def invert(values_full):
        own_part = lax.dynamic_slice_in_dim(values_full, first_row, quarter, 1)
        product = jnp.einsum("eij,ej->ei", inv_off, values_full, preferred_element_type=jnp.float32)
        return inv_diag * own_part.astype(jnp.float32) + product

    source_half = (source * mask_rows).astype(jnp.bfloat16)
    base_state = invert(full_rows(source_half)) * mask_rows
    adjoint = base_state
    for sweep_index in range(SWEEPS):
        state_rows = adjoint.astype(jnp.bfloat16)
        state_full = full_rows(state_rows)
        outgoing = state_full[requested]
        incoming = jnp.stack(
            [
                from_behind(outgoing[side_num], "dom", -offsets[side_num])
                for side_num in range(neigh)
            ]
        ).reshape(-1, width)
        peer_state = jnp.where(crossing[:, None], incoming[safe_position], state_full[face_peer])
        elem_state = state_rows[face_elem]
        local_terms = jnp.einsum(
            "fij,fj->fi", coupling, peer_state, preferred_element_type=jnp.float32
        )
        transposed = jnp.einsum(
            "fij,fi->fj", coupling, elem_state, preferred_element_type=jnp.float32
        )
        own_terms = jnp.zeros((elements, quarter), jnp.float32).at[face_elem].add(local_terms)
        partial_value = (
            jnp.zeros((elements, width), jnp.float32).at[face_peer].add(transposed * inner[:, None])
        )
        outbound = (
            jnp.zeros((neigh * capacity, width), jnp.float32)
            .at[position]
            .set(transposed, mode="drop")
            .reshape(neigh, capacity, width)
        )
        returned = jnp.stack(
            [from_behind(outbound[side_num], "dom", offsets[side_num]) for side_num in range(neigh)]
        ).reshape(-1, width)
        partial_value = partial_value.at[requested_flat].add(returned)
        middle = lax.dynamic_slice_in_dim(partial_value, first_row, quarter, 1) + own_terms
        partial_value = lax.dynamic_update_slice_in_dim(partial_value, middle, first_row, 1)
        summed = lax.psum(partial_value, "blk")
        coupled_half = (summed * mask_full).astype(jnp.bfloat16)
        adjoint = (base_state - invert(coupled_half)) * mask_rows
    weights = jnp.sum(adjoint * residual * mask_rows, axis=1)
    indicator = lax.psum(weights, "blk")
    return (adjoint, indicator)


def solution(mesh):
    in_specs = (
        P("dom"),
        P("dom"),
        P("dom"),
        P("dom"),
        P("dom", "blk", None),
        P("dom", "blk"),
        P("dom", "blk", None),
        P("dom", "blk"),
        P("dom", "blk"),
    )
    out_specs = (P("dom", "blk"), P("dom"))
    return jax.shard_map(local, mesh=mesh, in_specs=in_specs, out_specs=out_specs, check_vma=False)
```

profile of v0, /device:TPU:96, one launch (start us, length us, event | category | flops | bytes accessed | tf_op | source)
XLA Modules:
  0.0 313.0 jit_solution(9358824529545259234)
XLA Ops:
  5.9 5.0 %collective-permute-start.1 = (s32[4]{0:T(128)S(1)}, s32[4]{0:T(128)S(1)}, u32[]{:S(2)}, u32[]{:S(2)}) collective-permute-start(s32[4]{0:T(128)S(1)} %get-tuple-element.44), channel_id=1, source_target_pairs={{504,0},{508,4},{0,8},{4,12},{8,16},{12,20},{16,24},{20,28},{24,32... | collective-permute-start | bytes 56 | tf_op jit(solution)/shard_map/ppermute | solution.py:14
  10.9 5.2 %collective-permute-start.2 = (s32[4]{0:T(128)S(1)}, s32[4]{0:T(128)S(1)}, u32[]{:S(2)}, u32[]{:S(2)}) collective-permute-start(s32[4]{0:T(128)S(1)} %get-tuple-element.43), channel_id=1, source_target_pairs={{500,0},{504,4},{508,8},{0,12},{4,16},{8,20},{12,24},{16,28},{20,3... | collective-permute-start | bytes 56 | tf_op jit(solution)/shard_map/ppermute | solution.py:14
  16.1 6.4 %collective-permute-start.3 = (s32[4]{0:T(128)S(1)}, s32[4]{0:T(128)S(1)}, u32[]{:S(2)}, u32[]{:S(2)}) collective-permute-start(s32[4]{0:T(128)S(1)} %get-tuple-element.42), channel_id=1, source_target_pairs={{496,0},{500,4},{504,8},{508,12},{0,16},{4,20},{8,24},{12,28},{16,... | collective-permute-start | bytes 56 | tf_op jit(solution)/shard_map/ppermute | solution.py:14
  22.5 1.9 collective-permute-start.4
  27.9 11.3 %all-gather = bf16[4,80,8]{1,2,0:T(8,128)(2,1)S(1)} all-gather(bf16[1,80,8]{1,2,0:T(8,128)(2,1)S(1)} %fusion.36), channel_id=1, replica_groups=mesh['dom'=128,'blk'=4] {'blk'}, dimensions={0}, use_global_device_ids=true | all-gather | bytes 6400 | tf_op jit(solution)/shard_map/all_gather | solution.py:18
  44.7 10.4 %all-gather.1 = bf16[4,80,8]{1,2,0:T(8,128)(2,1)S(1)} all-gather(bf16[1,80,8]{1,2,0:T(8,128)(2,1)S(1)} %bitcast.165), channel_id=1, replica_groups=mesh['dom'=128,'blk'=4] {'blk'}, dimensions={0}, use_global_device_ids=true | all-gather | bytes 6400 | tf_op jit(solution)/shard_map/all_gather | solution.py:18
  55.9 1.9 collective-permute-start.5
  57.9 1.9 collective-permute-start.6
  59.8 3.3 %collective-permute-start.7 = (s32[4]{0:T(128)S(1)}, s32[4]{0:T(128)S(1)}, u32[]{:S(2)}, u32[]{:S(2)}) collective-permute-start(s32[4]{0:T(128)S(1)} %get-tuple-element.38), channel_id=1, source_target_pairs={{16,0},{20,4},{24,8},{28,12},{32,16},{36,20},{40,24},{44,28},{48,3... | collective-permute-start | bytes 56 | tf_op jit(solution)/shard_map/ppermute | solution.py:14
  63.1 2.7 collective-permute-start.8
  65.8 4.2 %collective-permute-start.9 = (f32[4,320]{1,0:T(4,128)S(1)}, f32[4,320]{1,0:T(4,128)S(1)}, u32[]{:S(2)}, u32[]{:S(2)}) collective-permute-start(f32[4,320]{1,0:T(4,128)S(1)} %get-tuple-element.20), channel_id=1, source_target_pairs={{504,0},{508,4},{0,8},{4,12},{8,16},{12,20},{16,24},{20,28},{24,32... | collective-permute-start | bytes 15368 | tf_op jit(solution)/shard_map/ppermute | solution.py:14
  70.0 3.6 %collective-permute-start.10 = (f32[4,320]{1,0:T(4,128)S(1)}, f32[4,320]{1,0:T(4,128)S(1)}, u32[]{:S(2)}, u32[]{:S(2)}) collective-permute-start(f32[4,320]{1,0:T(4,128)S(1)} %get-tuple-element.19), channel_id=1, source_target_pairs={{500,0},{504,4},{508,8},{0,12},{4,16},{8,20},{12,24},{16,28},{20,3... | collective-permute-start | bytes 15368 | tf_op jit(solution)/shard_map/ppermute | solution.py:14
  73.7 3.8 %collective-permute-start.11 = (f32[4,320]{1,0:T(4,128)S(1)}, f32[4,320]{1,0:T(4,128)S(1)}, u32[]{:S(2)}, u32[]{:S(2)}) collective-permute-start(f32[4,320]{1,0:T(4,128)S(1)} %get-tuple-element.18), channel_id=1, source_target_pairs={{496,0},{500,4},{504,8},{508,12},{0,16},{4,20},{8,24},{12,28},{16,... | collective-permute-start | bytes 15368 | tf_op jit(solution)/shard_map/ppermute | solution.py:14
  78.5 2.9 collective-permute-start.16
  85.0 5.0 %collective-permute-done.17 = bf16[4,320]{1,0:T(4,128)(2,1)S(1)} collective-permute-done((bf16[4,320]{1,0:T(4,128)(2,1)S(1)}, bf16[4,320]{1,0:T(4,128)(2,1)S(1)}, u32[]{:S(2)}, u32[]{:S(2)}) %collective-permute-start.17) | collective-permute-done | bytes 2592 | tf_op jit(solution)/shard_map/ppermute | solution.py:14
  91.9 4.2 %collective-permute-done.18 = bf16[4,320]{1,0:T(4,128)(2,1)S(1)} collective-permute-done((bf16[4,320]{1,0:T(4,128)(2,1)S(1)}, bf16[4,320]{1,0:T(4,128)(2,1)S(1)}, u32[]{:S(2)}, u32[]{:S(2)}) %collective-permute-start.18) | collective-permute-done | bytes 2592 | tf_op jit(solution)/shard_map/ppermute | solution.py:14
  96.1 8.5 %collective-permute-start.19 = (bf16[4,320]{1,0:T(4,128)(2,1)S(1)}, bf16[4,320]{1,0:T(4,128)(2,1)S(1)}, u32[]{:S(2)}, u32[]{:S(2)}) collective-permute-start(bf16[4,320]{1,0:T(4,128)(2,1)S(1)} %get-tuple-element.34), channel_id=1, source_target_pairs={{16,0},{20,4},{24,8},{28,12},{32,16},{36,20},{40,24},{44,28},{48,3... | collective-permute-start | bytes 7688 | tf_op jit(solution)/shard_map/ppermute | solution.py:14
  107.8 3.0 collective-permute-done.20
  110.8 2.7 collective-permute-start.21
  113.5 4.6 %collective-permute-done.21 = bf16[4,320]{1,0:T(4,128)(2,1)S(1)} collective-permute-done((bf16[4,320]{1,0:T(4,128)(2,1)S(1)}, bf16[4,320]{1,0:T(4,128)(2,1)S(1)}, u32[]{:S(2)}, u32[]{:S(2)}) %collective-permute-start.21) | collective-permute-done | bytes 2592 | tf_op jit(solution)/shard_map/ppermute | solution.py:14
  120.1 3.9 %collective-permute-done.22 = bf16[4,320]{1,0:T(4,128)(2,1)S(1)} collective-permute-done((bf16[4,320]{1,0:T(4,128)(2,1)S(1)}, bf16[4,320]{1,0:T(4,128)(2,1)S(1)}, u32[]{:S(2)}, u32[]{:S(2)}) %collective-permute-start.22) | collective-permute-done | bytes 2592 | tf_op jit(solution)/shard_map/ppermute | solution.py:14
  125.9 11.1 %collective-permute-done.23 = bf16[4,320]{1,0:T(4,128)(2,1)S(1)} collective-permute-done((bf16[4,320]{1,0:T(4,128)(2,1)S(1)}, bf16[4,320]{1,0:T(4,128)(2,1)S(1)}, u32[]{:S(2)}, u32[]{:S(2)}) %collective-permute-start.23) | collective-permute-done | bytes 2592 | tf_op jit(solution)/shard_map/ppermute | solution.py:14
  140.4 7.3 %collective-permute-start.13 = (f32[4,320]{1,0:T(4,128)S(1)}, f32[4,320]{1,0:T(4,128)S(1)}, u32[]{:S(2)}, u32[]{:S(2)}) collective-permute-start(f32[4,320]{1,0:T(4,128)S(1)} %get-tuple-element.16), channel_id=1, source_target_pairs={{8,0},{12,4},{16,8},{20,12},{24,16},{28,20},{32,24},{36,28},{40,32... | collective-permute-start | bytes 15368 | tf_op jit(solution)/shard_map/ppermute | solution.py:14
  147.7 8.0 %collective-permute-start.14 = (f32[4,320]{1,0:T(4,128)S(1)}, f32[4,320]{1,0:T(4,128)S(1)}, u32[]{:S(2)}, u32[]{:S(2)}) collective-permute-start(f32[4,320]{1,0:T(4,128)S(1)} %get-tuple-element.15), channel_id=1, source_target_pairs={{12,0},{16,4},{20,8},{24,12},{28,16},{32,20},{36,24},{40,28},{44,3... | collective-permute-start | bytes 15368 | tf_op jit(solution)/shard_map/ppermute | solution.py:14
  155.7 2.1 collective-permute-start.15
  157.9 5.4 %collective-permute-done.15 = f32[4,320]{1,0:T(4,128)S(1)} collective-permute-done((f32[4,320]{1,0:T(4,128)S(1)}, f32[4,320]{1,0:T(4,128)S(1)}, u32[]{:S(2)}, u32[]{:S(2)}) %collective-permute-start.15) | collective-permute-done | bytes 5152 | tf_op jit(solution)/shard_map/ppermute | solution.py:14
  165.2 15.8 %psum.21 = bf16[8,320]{1,0:T(8,128)(2,1)S(1)} all-reduce(f32[8,320]{1,0:T(8,128)S(1)} %dynamic_update_slice.6), channel_id=1, replica_groups=mesh['dom'=128,'blk'=4] {'blk'}, use_global_device_ids=true, to_apply=%region_7.8 | all-reduce | flops 2560 | bytes 15360 | tf_op jit(solution)/shard_map/psum | solution.py:98
  183.3 10.4 %all-gather.2 = bf16[4,80,8]{1,2,0:T(8,128)(2,1)S(1)} all-gather(bf16[1,80,8]{1,2,0:T(8,128)(2,1)S(1)} %bitcast.166), channel_id=1, replica_groups=mesh['dom'=128,'blk'=4] {'blk'}, dimensions={0}, use_global_device_ids=true | all-gather | bytes 6400 | tf_op jit(solution)/shard_map/all_gather | solution.py:18
  194.4 1.9 collective-permute-start.32
  197.9 2.4 collective-permute-start.24
  200.3 1.9 collective-permute-start.25
  202.2 1.9 collective-permute-start.26
  204.1 1.9 collective-permute-start.27
  206.1 3.9 %collective-permute-start.33 = (bf16[4,320]{1,0:T(4,128)(2,1)S(1)}, bf16[4,320]{1,0:T(4,128)(2,1)S(1)}, u32[]{:S(2)}, u32[]{:S(2)}) collective-permute-start(bf16[4,320]{1,0:T(4,128)(2,1)S(1)} %get-tuple-element.28), channel_id=1, source_target_pairs={{8,0},{12,4},{16,8},{20,12},{24,16},{28,20},{32,24},{36,28},{40,32... | collective-permute-start | bytes 7688 | tf_op jit(solution)/shard_map/ppermute | solution.py:14
  210.0 2.8 collective-permute-done.33
  212.8 2.2 collective-permute-start.34
  215.0 3.9 %collective-permute-done.34 = bf16[4,320]{1,0:T(4,128)(2,1)S(1)} collective-permute-done((bf16[4,320]{1,0:T(4,128)(2,1)S(1)}, bf16[4,320]{1,0:T(4,128)(2,1)S(1)}, u32[]{:S(2)}, u32[]{:S(2)}) %collective-permute-start.34) | collective-permute-done | bytes 2592 | tf_op jit(solution)/shard_map/ppermute | solution.py:14
  218.9 8.5 %collective-permute-start.35 = (bf16[4,320]{1,0:T(4,128)(2,1)S(1)}, bf16[4,320]{1,0:T(4,128)(2,1)S(1)}, u32[]{:S(2)}, u32[]{:S(2)}) collective-permute-start(bf16[4,320]{1,0:T(4,128)(2,1)S(1)} %get-tuple-element.26), channel_id=1, source_target_pairs={{16,0},{20,4},{24,8},{28,12},{32,16},{36,20},{40,24},{44,28},{48,3... | collective-permute-start | bytes 7688 | tf_op jit(solution)/shard_map/ppermute | solution.py:14
  230.6 3.0 collective-permute-done.36
  235.6 5.4 %collective-permute-done.37 = bf16[4,320]{1,0:T(4,128)(2,1)S(1)} collective-permute-done((bf16[4,320]{1,0:T(4,128)(2,1)S(1)}, bf16[4,320]{1,0:T(4,128)(2,1)S(1)}, u32[]{:S(2)}, u32[]{:S(2)}) %collective-permute-start.37) | collective-permute-done | bytes 2592 | tf_op jit(solution)/shard_map/ppermute | solution.py:14
  242.9 3.9 %collective-permute-done.38 = bf16[4,320]{1,0:T(4,128)(2,1)S(1)} collective-permute-done((bf16[4,320]{1,0:T(4,128)(2,1)S(1)}, bf16[4,320]{1,0:T(4,128)(2,1)S(1)}, u32[]{:S(2)}, u32[]{:S(2)}) %collective-permute-start.38) | collective-permute-done | bytes 2592 | tf_op jit(solution)/shard_map/ppermute | solution.py:14
  248.7 11.1 %collective-permute-done.39 = bf16[4,320]{1,0:T(4,128)(2,1)S(1)} collective-permute-done((bf16[4,320]{1,0:T(4,128)(2,1)S(1)}, bf16[4,320]{1,0:T(4,128)(2,1)S(1)}, u32[]{:S(2)}, u32[]{:S(2)}) %collective-permute-start.39) | collective-permute-done | bytes 2592 | tf_op jit(solution)/shard_map/ppermute | solution.py:14
  263.2 7.3 %collective-permute-start.29 = (f32[4,320]{1,0:T(4,128)S(1)}, f32[4,320]{1,0:T(4,128)S(1)}, u32[]{:S(2)}, u32[]{:S(2)}) collective-permute-start(f32[4,320]{1,0:T(4,128)S(1)} %get-tuple-element.8), channel_id=1, source_target_pairs={{8,0},{12,4},{16,8},{20,12},{24,16},{28,20},{32,24},{36,28},{40,32... | collective-permute-start | bytes 15368 | tf_op jit(solution)/shard_map/ppermute | solution.py:14
  270.5 8.0 %collective-permute-start.30 = (f32[4,320]{1,0:T(4,128)S(1)}, f32[4,320]{1,0:T(4,128)S(1)}, u32[]{:S(2)}, u32[]{:S(2)}) collective-permute-start(f32[4,320]{1,0:T(4,128)S(1)} %get-tuple-element.7), channel_id=1, source_target_pairs={{12,0},{16,4},{20,8},{24,12},{28,16},{32,20},{36,24},{40,28},{44,3... | collective-permute-start | bytes 15368 | tf_op jit(solution)/shard_map/ppermute | solution.py:14
  278.5 2.1 collective-permute-start.31
  280.7 5.4 %collective-permute-done.31 = f32[4,320]{1,0:T(4,128)S(1)} collective-permute-done((f32[4,320]{1,0:T(4,128)S(1)}, f32[4,320]{1,0:T(4,128)S(1)}, u32[]{:S(2)}, u32[]{:S(2)}) %collective-permute-start.31) | collective-permute-done | bytes 5152 | tf_op jit(solution)/shard_map/ppermute | solution.py:14
  288.0 14.3 %psum.22 = bf16[8,320]{1,0:T(8,128)(2,1)S(1)} all-reduce(f32[8,320]{1,0:T(8,128)S(1)} %dynamic_update_slice.7), channel_id=1, replica_groups=mesh['dom'=128,'blk'=4] {'blk'}, use_global_device_ids=true, to_apply=%region_12.13 | all-reduce | flops 2560 | bytes 15360 | tf_op jit(solution)/shard_map/psum | solution.py:98
  303.5 9.5 %psum.23 = f32[8]{0:T(128)} all-reduce(f32[8]{0:T(128)S(1)} %get-tuple-element.2), channel_id=1, replica_groups=mesh['dom'=128,'blk'=4] {'blk'}, use_global_device_ids=true, to_apply=%region_14.15 | all-reduce | flops 8 | bytes 64 | tf_op jit(solution)/shard_map/psum | solution.py:102
  (160 shorter events, 53.8 us)
Async XLA Ops:
  0.6 42.1 %copy-start = (bf16[32,80,320]{2,1,0:T(8,128)(2,1)S(1)}, bf16[32,80,320]{2,1,0:T(8,128)(2,1)}, u32[]{:S(2)}) copy-start(bf16[32,80,320]{2,1,0:T(8,128)(2,1)} %param.13) | copy-start | bytes 4915204
  4.0 51.9 %collective-permute-start = (s32[4]{0:T(128)S(1)}, s32[4]{0:T(128)S(1)}, u32[]{:S(2)}, u32[]{:S(2)}) collective-permute-start(s32[4]{0:T(128)S(1)} %get-tuple-element.45), channel_id=1, source_target_pairs={{508,0},{0,4},{4,8},{8,12},{12,16},{16,20},{20,24},{24,28},{28,32}... | collective-permute-start | bytes 56 | tf_op jit(solution)/shard_map/ppermute | solution.py:14
  5.9 52.0 %collective-permute-start.1 = (s32[4]{0:T(128)S(1)}, s32[4]{0:T(128)S(1)}, u32[]{:S(2)}, u32[]{:S(2)}) collective-permute-start(s32[4]{0:T(128)S(1)} %get-tuple-element.44), channel_id=1, source_target_pairs={{504,0},{508,4},{0,8},{4,12},{8,16},{12,20},{16,24},{20,28},{24,32... | collective-permute-start | bytes 56 | tf_op jit(solution)/shard_map/ppermute | solution.py:14
  10.9 48.9 %collective-permute-start.2 = (s32[4]{0:T(128)S(1)}, s32[4]{0:T(128)S(1)}, u32[]{:S(2)}, u32[]{:S(2)}) collective-permute-start(s32[4]{0:T(128)S(1)} %get-tuple-element.43), channel_id=1, source_target_pairs={{500,0},{504,4},{508,8},{0,12},{4,16},{8,20},{12,24},{16,28},{20,3... | collective-permute-start | bytes 56 | tf_op jit(solution)/shard_map/ppermute | solution.py:14
  16.1 47.0 %collective-permute-start.3 = (s32[4]{0:T(128)S(1)}, s32[4]{0:T(128)S(1)}, u32[]{:S(2)}, u32[]{:S(2)}) collective-permute-start(s32[4]{0:T(128)S(1)} %get-tuple-element.42), channel_id=1, source_target_pairs={{496,0},{500,4},{504,8},{508,12},{0,16},{4,20},{8,24},{12,28},{16,... | collective-permute-start | bytes 56 | tf_op jit(solution)/shard_map/ppermute | solution.py:14
  22.5 43.3 %collective-permute-start.4 = (s32[4]{0:T(128)S(1)}, s32[4]{0:T(128)S(1)}, u32[]{:S(2)}, u32[]{:S(2)}) collective-permute-start(s32[4]{0:T(128)S(1)} %get-tuple-element.41), channel_id=1, source_target_pairs={{4,0},{8,4},{12,8},{16,12},{20,16},{24,20},{28,24},{32,28},{36,32}... | collective-permute-start | bytes 56 | tf_op jit(solution)/shard_map/ppermute | solution.py:14
  55.9 14.1 %collective-permute-start.5 = (s32[4]{0:T(128)S(1)}, s32[4]{0:T(128)S(1)}, u32[]{:S(2)}, u32[]{:S(2)}) collective-permute-start(s32[4]{0:T(128)S(1)} %get-tuple-element.40), channel_id=1, source_target_pairs={{8,0},{12,4},{16,8},{20,12},{24,16},{28,20},{32,24},{36,28},{40,32... | collective-permute-start | bytes 56 | tf_op jit(solution)/shard_map/ppermute | solution.py:14
  57.9 15.8 %collective-permute-start.6 = (s32[4]{0:T(128)S(1)}, s32[4]{0:T(128)S(1)}, u32[]{:S(2)}, u32[]{:S(2)}) collective-permute-start(s32[4]{0:T(128)S(1)} %get-tuple-element.39), channel_id=1, source_target_pairs={{12,0},{16,4},{20,8},{24,12},{28,16},{32,20},{36,24},{40,28},{44,3... | collective-permute-start | bytes 56 | tf_op jit(solution)/shard_map/ppermute | solution.py:14
  59.8 17.7 %collective-permute-start.7 = (s32[4]{0:T(128)S(1)}, s32[4]{0:T(128)S(1)}, u32[]{:S(2)}, u32[]{:S(2)}) collective-permute-start(s32[4]{0:T(128)S(1)} %get-tuple-element.38), channel_id=1, source_target_pairs={{16,0},{20,4},{24,8},{28,12},{32,16},{36,20},{40,24},{44,28},{48,3... | collective-permute-start | bytes 56 | tf_op jit(solution)/shard_map/ppermute | solution.py:14
  63.1 77.3 %collective-permute-start.8 = (f32[4,320]{1,0:T(4,128)S(1)}, f32[4,320]{1,0:T(4,128)S(1)}, u32[]{:S(2)}, u32[]{:S(2)}) collective-permute-start(f32[4,320]{1,0:T(4,128)S(1)} %get-tuple-element.21), channel_id=1, source_target_pairs={{508,0},{0,4},{4,8},{8,12},{12,16},{16,20},{20,24},{24,28},{28,32}... | collective-permute-start | bytes 15368 | tf_op jit(solution)/shard_map/ppermute | solution.py:14
  65.8 81.9 %collective-permute-start.9 = (f32[4,320]{1,0:T(4,128)S(1)}, f32[4,320]{1,0:T(4,128)S(1)}, u32[]{:S(2)}, u32[]{:S(2)}) collective-permute-start(f32[4,320]{1,0:T(4,128)S(1)} %get-tuple-element.20), channel_id=1, source_target_pairs={{504,0},{508,4},{0,8},{4,12},{8,16},{12,20},{16,24},{20,28},{24,32... | collective-permute-start | bytes 15368 | tf_op jit(solution)/shard_map/ppermute | solution.py:14
  70.0 85.6 %collective-permute-start.10 = (f32[4,320]{1,0:T(4,128)S(1)}, f32[4,320]{1,0:T(4,128)S(1)}, u32[]{:S(2)}, u32[]{:S(2)}) collective-permute-start(f32[4,320]{1,0:T(4,128)S(1)} %get-tuple-element.19), channel_id=1, source_target_pairs={{500,0},{504,4},{508,8},{0,12},{4,16},{8,20},{12,24},{16,28},{20,3... | collective-permute-start | bytes 15368 | tf_op jit(solution)/shard_map/ppermute | solution.py:14
  73.7 84.1 %collective-permute-start.11 = (f32[4,320]{1,0:T(4,128)S(1)}, f32[4,320]{1,0:T(4,128)S(1)}, u32[]{:S(2)}, u32[]{:S(2)}) collective-permute-start(f32[4,320]{1,0:T(4,128)S(1)} %get-tuple-element.18), channel_id=1, source_target_pairs={{496,0},{500,4},{504,8},{508,12},{0,16},{4,20},{8,24},{12,28},{16,... | collective-permute-start | bytes 15368 | tf_op jit(solution)/shard_map/ppermute | solution.py:14
  78.4 102.7 %copy-start.3 = (bf16[8,80,320]{2,1,0:T(8,128)(2,1)S(1)}, bf16[8,80,320]{2,1,0:T(8,128)(2,1)}, u32[]{:S(2)}) copy-start(bf16[8,80,320]{2,1,0:T(8,128)(2,1)} %param.15) | copy-start | bytes 1228804
  78.5 4.6 %collective-permute-start.16 = (bf16[4,320]{1,0:T(4,128)(2,1)S(1)}, bf16[4,320]{1,0:T(4,128)(2,1)S(1)}, u32[]{:S(2)}, u32[]{:S(2)}) collective-permute-start(bf16[4,320]{1,0:T(4,128)(2,1)S(1)} %get-tuple-element.37), channel_id=1, source_target_pairs={{4,0},{8,4},{12,8},{16,12},{20,16},{24,20},{28,24},{32,28},{36,32}... | collective-permute-start | bytes 7688 | tf_op jit(solution)/shard_map/ppermute | solution.py:14
  83.0 7.0 %collective-permute-start.17 = (bf16[4,320]{1,0:T(4,128)(2,1)S(1)}, bf16[4,320]{1,0:T(4,128)(2,1)S(1)}, u32[]{:S(2)}, u32[]{:S(2)}) collective-permute-start(bf16[4,320]{1,0:T(4,128)(2,1)S(1)} %get-tuple-element.36), channel_id=1, source_target_pairs={{8,0},{12,4},{16,8},{20,12},{24,16},{28,20},{32,24},{36,28},{40,32... | collective-permute-start | bytes 7688 | tf_op jit(solution)/shard_map/ppermute | solution.py:14
  90.0 6.1 %collective-permute-start.18 = (bf16[4,320]{1,0:T(4,128)(2,1)S(1)}, bf16[4,320]{1,0:T(4,128)(2,1)S(1)}, u32[]{:S(2)}, u32[]{:S(2)}) collective-permute-start(bf16[4,320]{1,0:T(4,128)(2,1)S(1)} %get-tuple-element.35), channel_id=1, source_target_pairs={{12,0},{16,4},{20,8},{24,12},{28,16},{32,20},{36,24},{40,28},{44,3... | collective-permute-start | bytes 7688 | tf_op jit(solution)/shard_map/ppermute | solution.py:14
  96.1 9.8 %collective-permute-start.19 = (bf16[4,320]{1,0:T(4,128)(2,1)S(1)}, bf16[4,320]{1,0:T(4,128)(2,1)S(1)}, u32[]{:S(2)}, u32[]{:S(2)}) collective-permute-start(bf16[4,320]{1,0:T(4,128)(2,1)S(1)} %get-tuple-element.34), channel_id=1, source_target_pairs={{16,0},{20,4},{24,8},{28,12},{32,16},{36,20},{40,24},{44,28},{48,3... | collective-permute-start | bytes 7688 | tf_op jit(solution)/shard_map/ppermute | solution.py:14
  105.9 4.9 %collective-permute-start.20 = (bf16[4,320]{1,0:T(4,128)(2,1)S(1)}, bf16[4,320]{1,0:T(4,128)(2,1)S(1)}, u32[]{:S(2)}, u32[]{:S(2)}) collective-permute-start(bf16[4,320]{1,0:T(4,128)(2,1)S(1)} %get-tuple-element.33), channel_id=1, source_target_pairs={{508,0},{0,4},{4,8},{8,12},{12,16},{16,20},{20,24},{24,28},{28,32}... | collective-permute-start | bytes 7688 | tf_op jit(solution)/shard_map/ppermute | solution.py:14
  110.8 7.4 %collective-permute-start.21 = (bf16[4,320]{1,0:T(4,128)(2,1)S(1)}, bf16[4,320]{1,0:T(4,128)(2,1)S(1)}, u32[]{:S(2)}, u32[]{:S(2)}) collective-permute-start(bf16[4,320]{1,0:T(4,128)(2,1)S(1)} %get-tuple-element.32), channel_id=1, source_target_pairs={{504,0},{508,4},{0,8},{4,12},{8,16},{12,20},{16,24},{20,28},{24,32... | collective-permute-start | bytes 7688 | tf_op jit(solution)/shard_map/ppermute | solution.py:14
  118.2 5.8 %collective-permute-start.22 = (bf16[4,320]{1,0:T(4,128)(2,1)S(1)}, bf16[4,320]{1,0:T(4,128)(2,1)S(1)}, u32[]{:S(2)}, u32[]{:S(2)}) collective-permute-start(bf16[4,320]{1,0:T(4,128)(2,1)S(1)} %get-tuple-element.31), channel_id=1, source_target_pairs={{500,0},{504,4},{508,8},{0,12},{4,16},{8,20},{12,24},{16,28},{20,3... | collective-permute-start | bytes 7688 | tf_op jit(solution)/shard_map/ppermute | solution.py:14
  124.0 13.0 %collective-permute-start.23 = (bf16[4,320]{1,0:T(4,128)(2,1)S(1)}, bf16[4,320]{1,0:T(4,128)(2,1)S(1)}, u32[]{:S(2)}, u32[]{:S(2)}) collective-permute-start(bf16[4,320]{1,0:T(4,128)(2,1)S(1)} %get-tuple-element.30), channel_id=1, source_target_pairs={{496,0},{500,4},{504,8},{508,12},{0,16},{4,20},{8,24},{12,28},{16,... | collective-permute-start | bytes 7688 | tf_op jit(solution)/shard_map/ppermute | solution.py:14
  136.9 20.9 %collective-permute-start.12 = (f32[4,320]{1,0:T(4,128)S(1)}, f32[4,320]{1,0:T(4,128)S(1)}, u32[]{:S(2)}, u32[]{:S(2)}) collective-permute-start(f32[4,320]{1,0:T(4,128)S(1)} %get-tuple-element.17), channel_id=1, source_target_pairs={{4,0},{8,4},{12,8},{16,12},{20,16},{24,20},{28,24},{32,28},{36,32}... | collective-permute-start | bytes 15368 | tf_op jit(solution)/shard_map/ppermute | solution.py:14
  139.6 41.8 %copy-start.1 = (f32[8,80]{1,0:T(8,128)S(1)}, f32[8,80]{1,0:T(8,128)}, u32[]{:S(2)}) copy-start(f32[8,80]{1,0:T(8,128)} %param.14) | copy-start | bytes 7684
  140.4 17.4 %collective-permute-start.13 = (f32[4,320]{1,0:T(4,128)S(1)}, f32[4,320]{1,0:T(4,128)S(1)}, u32[]{:S(2)}, u32[]{:S(2)}) collective-permute-start(f32[4,320]{1,0:T(4,128)S(1)} %get-tuple-element.16), channel_id=1, source_target_pairs={{8,0},{12,4},{16,8},{20,12},{24,16},{28,20},{32,24},{36,28},{40,32... | collective-permute-start | bytes 15368 | tf_op jit(solution)/shard_map/ppermute | solution.py:14
  147.7 10.2 %collective-permute-start.14 = (f32[4,320]{1,0:T(4,128)S(1)}, f32[4,320]{1,0:T(4,128)S(1)}, u32[]{:S(2)}, u32[]{:S(2)}) collective-permute-start(f32[4,320]{1,0:T(4,128)S(1)} %get-tuple-element.15), channel_id=1, source_target_pairs={{12,0},{16,4},{20,8},{24,12},{28,16},{32,20},{36,24},{40,28},{44,3... | collective-permute-start | bytes 15368 | tf_op jit(solution)/shard_map/ppermute | solution.py:14
  155.7 7.6 %collective-permute-start.15 = (f32[4,320]{1,0:T(4,128)S(1)}, f32[4,320]{1,0:T(4,128)S(1)}, u32[]{:S(2)}, u32[]{:S(2)}) collective-permute-start(f32[4,320]{1,0:T(4,128)S(1)} %get-tuple-element.14), channel_id=1, source_target_pairs={{16,0},{20,4},{24,8},{28,12},{32,16},{36,20},{40,24},{44,28},{48,3... | collective-permute-start | bytes 15368 | tf_op jit(solution)/shard_map/ppermute | solution.py:14
  194.4 11.6 %collective-permute-start.32 = (bf16[4,320]{1,0:T(4,128)(2,1)S(1)}, bf16[4,320]{1,0:T(4,128)(2,1)S(1)}, u32[]{:S(2)}, u32[]{:S(2)}) collective-permute-start(bf16[4,320]{1,0:T(4,128)(2,1)S(1)} %get-tuple-element.29), channel_id=1, source_target_pairs={{4,0},{8,4},{12,8},{16,12},{20,16},{24,20},{28,24},{32,28},{36,32}... | collective-permute-start | bytes 7688 | tf_op jit(solution)/shard_map/ppermute | solution.py:14
  197.9 65.4 %collective-permute-start.24 = (f32[4,320]{1,0:T(4,128)S(1)}, f32[4,320]{1,0:T(4,128)S(1)}, u32[]{:S(2)}, u32[]{:S(2)}) collective-permute-start(f32[4,320]{1,0:T(4,128)S(1)} %get-tuple-element.13), channel_id=1, source_target_pairs={{508,0},{0,4},{4,8},{8,12},{12,16},{16,20},{20,24},{24,28},{28,32}... | collective-permute-start | bytes 15368 | tf_op jit(solution)/shard_map/ppermute | solution.py:14
  200.3 70.2 %collective-permute-start.25 = (f32[4,320]{1,0:T(4,128)S(1)}, f32[4,320]{1,0:T(4,128)S(1)}, u32[]{:S(2)}, u32[]{:S(2)}) collective-permute-start(f32[4,320]{1,0:T(4,128)S(1)} %get-tuple-element.12), channel_id=1, source_target_pairs={{504,0},{508,4},{0,8},{4,12},{8,16},{12,20},{16,24},{20,28},{24,32... | collective-permute-start | bytes 15368 | tf_op jit(solution)/shard_map/ppermute | solution.py:14
  202.2 76.3 %collective-permute-start.26 = (f32[4,320]{1,0:T(4,128)S(1)}, f32[4,320]{1,0:T(4,128)S(1)}, u32[]{:S(2)}, u32[]{:S(2)}) collective-permute-start(f32[4,320]{1,0:T(4,128)S(1)} %get-tuple-element.11), channel_id=1, source_target_pairs={{500,0},{504,4},{508,8},{0,12},{4,16},{8,20},{12,24},{16,28},{20,3... | collective-permute-start | bytes 15368 | tf_op jit(solution)/shard_map/ppermute | solution.py:14
  204.1 76.5 %collective-permute-start.27 = (f32[4,320]{1,0:T(4,128)S(1)}, f32[4,320]{1,0:T(4,128)S(1)}, u32[]{:S(2)}, u32[]{:S(2)}) collective-permute-start(f32[4,320]{1,0:T(4,128)S(1)} %get-tuple-element.10), channel_id=1, source_target_pairs={{496,0},{500,4},{504,8},{508,12},{0,16},{4,20},{8,24},{12,28},{16,... | collective-permute-start | bytes 15368 | tf_op jit(solution)/shard_map/ppermute | solution.py:14
  206.1 6.7 %collective-permute-start.33 = (bf16[4,320]{1,0:T(4,128)(2,1)S(1)}, bf16[4,320]{1,0:T(4,128)(2,1)S(1)}, u32[]{:S(2)}, u32[]{:S(2)}) collective-permute-start(bf16[4,320]{1,0:T(4,128)(2,1)S(1)} %get-tuple-element.28), channel_id=1, source_target_pairs={{8,0},{12,4},{16,8},{20,12},{24,16},{28,20},{32,24},{36,28},{40,32... | collective-permute-start | bytes 7688 | tf_op jit(solution)/shard_map/ppermute | solution.py:14
  212.8 6.1 %collective-permute-start.34 = (bf16[4,320]{1,0:T(4,128)(2,1)S(1)}, bf16[4,320]{1,0:T(4,128)(2,1)S(1)}, u32[]{:S(2)}, u32[]{:S(2)}) collective-permute-start(bf16[4,320]{1,0:T(4,128)(2,1)S(1)} %get-tuple-element.27), channel_id=1, source_target_pairs={{12,0},{16,4},{20,8},{24,12},{28,16},{32,20},{36,24},{40,28},{44,3... | collective-permute-start | bytes 7688 | tf_op jit(solution)/shard_map/ppermute | solution.py:14
  218.9 9.8 %collective-permute-start.35 = (bf16[4,320]{1,0:T(4,128)(2,1)S(1)}, bf16[4,320]{1,0:T(4,128)(2,1)S(1)}, u32[]{:S(2)}, u32[]{:S(2)}) collective-permute-start(bf16[4,320]{1,0:T(4,128)(2,1)S(1)} %get-tuple-element.26), channel_id=1, source_target_pairs={{16,0},{20,4},{24,8},{28,12},{32,16},{36,20},{40,24},{44,28},{48,3... | collective-permute-start | bytes 7688 | tf_op jit(solution)/shard_map/ppermute | solution.py:14
  228.7 4.9 %collective-permute-start.36 = (bf16[4,320]{1,0:T(4,128)(2,1)S(1)}, bf16[4,320]{1,0:T(4,128)(2,1)S(1)}, u32[]{:S(2)}, u32[]{:S(2)}) collective-permute-start(bf16[4,320]{1,0:T(4,128)(2,1)S(1)} %get-tuple-element.25), channel_id=1, source_target_pairs={{508,0},{0,4},{4,8},{8,12},{12,16},{16,20},{20,24},{24,28},{28,32}... | collective-permute-start | bytes 7688 | tf_op jit(solution)/shard_map/ppermute | solution.py:14
  233.6 7.4 %collective-permute-start.37 = (bf16[4,320]{1,0:T(4,128)(2,1)S(1)}, bf16[4,320]{1,0:T(4,128)(2,1)S(1)}, u32[]{:S(2)}, u32[]{:S(2)}) collective-permute-start(bf16[4,320]{1,0:T(4,128)(2,1)S(1)} %get-tuple-element.24), channel_id=1, source_target_pairs={{504,0},{508,4},{0,8},{4,12},{8,16},{12,20},{16,24},{20,28},{24,32... | collective-permute-start | bytes 7688 | tf_op jit(solution)/shard_map/ppermute | solution.py:14
  241.0 5.8 %collective-permute-start.38 = (bf16[4,320]{1,0:T(4,128)(2,1)S(1)}, bf16[4,320]{1,0:T(4,128)(2,1)S(1)}, u32[]{:S(2)}, u32[]{:S(2)}) collective-permute-start(bf16[4,320]{1,0:T(4,128)(2,1)S(1)} %get-tuple-element.23), channel_id=1, source_target_pairs={{500,0},{504,4},{508,8},{0,12},{4,16},{8,20},{12,24},{16,28},{20,3... | collective-permute-start | bytes 7688 | tf_op jit(solution)/shard_map/ppermute | solution.py:14
  246.8 13.0 %collective-permute-start.39 = (bf16[4,320]{1,0:T(4,128)(2,1)S(1)}, bf16[4,320]{1,0:T(4,128)(2,1)S(1)}, u32[]{:S(2)}, u32[]{:S(2)}) collective-permute-start(bf16[4,320]{1,0:T(4,128)(2,1)S(1)} %get-tuple-element.22), channel_id=1, source_target_pairs={{496,0},{500,4},{504,8},{508,12},{0,16},{4,20},{8,24},{12,28},{16,... | collective-permute-start | bytes 7688 | tf_op jit(solution)/shard_map/ppermute | solution.py:14
  259.8 20.9 %collective-permute-start.28 = (f32[4,320]{1,0:T(4,128)S(1)}, f32[4,320]{1,0:T(4,128)S(1)}, u32[]{:S(2)}, u32[]{:S(2)}) collective-permute-start(f32[4,320]{1,0:T(4,128)S(1)} %get-tuple-element.9), channel_id=1, source_target_pairs={{4,0},{8,4},{12,8},{16,12},{20,16},{24,20},{28,24},{32,28},{36,32}... | collective-permute-start | bytes 15368 | tf_op jit(solution)/shard_map/ppermute | solution.py:14
  262.4 40.3 %copy-start.2 = (f32[8,80]{1,0:T(8,128)S(1)}, f32[8,80]{1,0:T(8,128)}, u32[]{:S(2)}) copy-start(f32[8,80]{1,0:T(8,128)} %param.17) | copy-start | bytes 7684
  263.2 17.4 %collective-permute-start.29 = (f32[4,320]{1,0:T(4,128)S(1)}, f32[4,320]{1,0:T(4,128)S(1)}, u32[]{:S(2)}, u32[]{:S(2)}) collective-permute-start(f32[4,320]{1,0:T(4,128)S(1)} %get-tuple-element.8), channel_id=1, source_target_pairs={{8,0},{12,4},{16,8},{20,12},{24,16},{28,20},{32,24},{36,28},{40,32... | collective-permute-start | bytes 15368 | tf_op jit(solution)/shard_map/ppermute | solution.py:14
  270.5 10.2 %collective-permute-start.30 = (f32[4,320]{1,0:T(4,128)S(1)}, f32[4,320]{1,0:T(4,128)S(1)}, u32[]{:S(2)}, u32[]{:S(2)}) collective-permute-start(f32[4,320]{1,0:T(4,128)S(1)} %get-tuple-element.7), channel_id=1, source_target_pairs={{12,0},{16,4},{20,8},{24,12},{28,16},{32,20},{36,24},{40,28},{44,3... | collective-permute-start | bytes 15368 | tf_op jit(solution)/shard_map/ppermute | solution.py:14
  278.5 7.6 %collective-permute-start.31 = (f32[4,320]{1,0:T(4,128)S(1)}, f32[4,320]{1,0:T(4,128)S(1)}, u32[]{:S(2)}, u32[]{:S(2)}) collective-permute-start(f32[4,320]{1,0:T(4,128)S(1)} %get-tuple-element.6), channel_id=1, source_target_pairs={{16,0},{20,4},{24,8},{28,12},{32,16},{36,20},{40,24},{44,28},{48,3... | collective-permute-start | bytes 15368 | tf_op jit(solution)/shard_map/ppermute | solution.py:14
where the time goes:
time: 315 us; the launch traced here: 313 us
  starting transfers between devices  136 us (43%)
  waiting for transfers between devices  76.9 us (24%)
  blocking collectives  71.8 us (23%)
  other arithmetic  13.5 us (4%)
  local copies, waits for them, and re-layouts  8.94 us (3%)
  matrix products  4.21 us (1%)
    ppermute x40, starting transfers between devices, from_behind(): return lax.ppermute(block, axis, route)  136 us
    ppermute x40, waiting for transfers between devices, from_behind(): return lax.ppermute(block, axis, route)  76.9 us
    all_gather x3, blocking collectives, full_rows(): return lax.all_gather(values, 'blk', axis=1, tiled=True)  32.2 us
    psum x2, blocking collectives, local(): summed = lax.psum(partial_value, 'blk')  30.1 us
    psum x1, blocking collectives, local(): indicator = lax.psum(weights, 'blk')  9.47 us
  transfers between devices with their start and end apart: 40, of which 17 were waited for; matrix products, arithmetic and copies ran while one was open for 5% of the time, Pallas kernels for 0%

commit v1 on v0

v1 whole, which is shorter than its diff:
```python
import functools

import jax
import jax.numpy as jnp
from jax import lax
from jax.experimental import pallas as pl
from jax.experimental.pallas import tpu as pltpu
from jax.sharding import PartitionSpec as P

MODES = 64
SWEEPS = 2
NEIGH = 8
HALF = NEIGH // 2
F32 = jnp.float32
BF16 = jnp.bfloat16
NT = (((1,), (1,)), ((), ()))


def dot(a, b):
    return jnp.dot(a, b, preferred_element_type=F32)


def dot_nt(a, b):
    return lax.dot_general(a, b, NT, preferred_element_type=F32)


def two_parts(x):
    hi = x.astype(BF16)
    lo = (x - hi.astype(F32)).astype(BF16)
    return jnp.concatenate([hi.astype(F32), lo.astype(F32)], axis=0).astype(BF16)


def column(row, count):
    i = lax.broadcasted_iota(jnp.int32, (count, count), 0)
    j = lax.broadcasted_iota(jnp.int32, (count, count), 1)
    return jnp.sum(jnp.where(i == j, jnp.broadcast_to(row, (count, count)), 0.0), axis=1, keepdims=True)


def as_row(col, count):
    i = lax.broadcasted_iota(jnp.int32, (count, count), 0)
    j = lax.broadcasted_iota(jnp.int32, (count, count), 1)
    return jnp.sum(jnp.where(i == j, jnp.broadcast_to(col, (count, count)), 0.0), axis=0, keepdims=True)


def mask_of(degree, width, first):
    elements = degree.shape[1]
    order = degree.astype(F32) + 1.0
    limit = column(order * order * order * (MODES / 64), elements)
    modes = (lax.broadcasted_iota(jnp.int32, (elements, width), 1) + first) % MODES
    return jnp.where(modes.astype(F32) < limit, 1.0, 0.0)


def lane_tables(quarter, faces):
    lanes = quarter * faces
    lane = lax.broadcasted_iota(jnp.int32, (1, lanes), 1).astype(F32)
    face = jnp.floor((lane + 0.5) * (1.0 / quarter))
    inside = lane - face * quarter
    row = lax.broadcasted_iota(jnp.int32, (quarter, lanes), 0).astype(F32)
    fold = jnp.where(row == inside, 1.0, 0.0).astype(BF16)
    return face, fold


def per_lane(face, values):
    faces = values.shape[1]
    lanes = face.shape[1]
    row = lax.broadcasted_iota(jnp.int32, (faces, lanes), 0).astype(F32)
    pick = jnp.where(row == face, 1.0, 0.0).astype(BF16)
    wide = jnp.broadcast_to(values, (8, faces)).astype(BF16)
    return dot(wide, pick)[0:1]


def targets(side, peer, slot, elements):
    offset = jnp.where(side > HALF, HALF - side, side)
    return ((HALF + slot + offset) * elements + peer).astype(F32)


def block_apply(inv_off, vector, elements, quarter):
    row = lax.broadcasted_iota(jnp.int32, (elements, quarter), 0)
    total = jnp.zeros((elements, quarter), F32)
    for e in range(elements):
        part = dot_nt(vector, inv_off[e * quarter : (e + 1) * quarter, :])
        total = jnp.where(row == e, part, total)
    return total


def put_transposed(out, coupling, state, owner, target, elements, quarter, faces):
    face, fold = lane_tables(quarter, faces)
    own_lane = per_lane(face, owner.astype(F32))
    target_lane = per_lane(face, target)
    lanes = quarter * faces
    repeated = dot(state.astype(BF16), fold)
    rows = lax.broadcasted_iota(jnp.int32, (elements, lanes), 0).astype(F32)
    spread = jnp.sum(jnp.where(rows == own_lane, repeated, 0.0), axis=0, keepdims=True)
    count = 3 * HALF * elements
    places = lax.broadcasted_iota(jnp.int32, (count, lanes), 0).astype(F32)
    chosen = jnp.where(places == target_lane, spread, 0.0).astype(BF16)
    transposed = dot(chosen, coupling)
    for q in range(4):
        part = transposed[:, q * quarter : (q + 1) * quarter]
        for r in range(HALF):
            for s in range(3):
                at = (s * HALF + r) * elements
                out[r * 4 + q, s * elements : (s + 1) * elements, 0:quarter] = part[at : at + elements]
            out[r * 4 + q, 3 * elements : 4 * elements, 0:quarter] = state


def first_kernel(degree, source, out):
    elements, quarter = source.shape
    first = lax.axis_index("blk") * quarter
    half = (source[...] * mask_of(degree[...], quarter, first)).astype(BF16).astype(F32)
    for q in range(4):
        out[q, :, 0:quarter] = half


def base_kernel(
    degree, owner, side, peer, coupling, inv_diag, inv_off, source, residual, gathered,
    out, base_out, weight_out, wide,
):
    elements, quarter = source.shape
    faces = owner.shape[1]
    width = 4 * quarter
    slot = lax.axis_index("dom") % HALF
    blk = lax.axis_index("blk")
    mask = mask_of(degree[...], quarter, blk * quarter)
    for q in range(4):
        wide[:, q * quarter : (q + 1) * quarter] = gathered[q, :, 0:quarter]
    own = (source[...] * mask).astype(BF16).astype(F32)
    product = block_apply(inv_off, wide[...].astype(BF16), elements, quarter)
    base = (inv_diag[...] * own + product) * mask
    base_out[...] = base
    state = base.astype(BF16).astype(F32)
    target = targets(side[...], peer[...], slot, elements)
    put_transposed(out, coupling[...], state, owner[...], target, elements, quarter, faces)
    weighted = residual[...] * mask
    parts = two_parts(weighted)
    row = lax.broadcasted_iota(jnp.int32, (elements, width), 0)
    total = jnp.zeros((elements, width), F32)
    for e in range(elements):
        both = dot(parts, inv_off[e * quarter : (e + 1) * quarter, :])
        total = jnp.where(row == e, both[0:elements] + both[elements : 2 * elements], total)
    wide[...] = total
    diagonal = inv_diag[...] * weighted
    for q in range(4):
        at = slice(q * quarter, (q + 1) * quarter)
        wide[:, at] = wide[:, at] + jnp.where(blk == q, diagonal, 0.0)
    weight_out[:, 0:width] = wide[...]
    weight_out[:, 384:512] = jnp.broadcast_to(
        jnp.sum(weighted * base, axis=1, keepdims=True), (elements, 128)
    )


def merge_kernel(message, ahead, behind, kept):
    elements, quarter = kept.shape
    total = message[0, 0 : 3 * elements, 0:quarter]
    for i in range(1, 16):
        total = total + message[i, 0 : 3 * elements, 0:quarter]
    behind[HALF * elements :, 0:quarter] = total[0:elements]
    kept[...] = total[elements : 2 * elements]
    ahead[HALF * elements :, 0:quarter] = total[2 * elements : 3 * elements]
    for r in range(HALF):
        for q in range(4):
            state = message[r * 4 + q, 3 * elements : 4 * elements, 0:quarter]
            rows = slice(r * elements, (r + 1) * elements)
            ahead[rows, q * quarter : (q + 1) * quarter] = state
            behind[rows, q * quarter : (q + 1) * quarter] = state


def couple_kernel(degree, owner, side, peer, coupling, left, middle, right, kept, *rest):
    out = rest[-1]
    elements, quarter = kept.shape
    faces = owner.shape[1]
    width = 4 * quarter
    lanes = quarter * faces
    slot = lax.axis_index("dom") % HALF
    mask = mask_of(degree[...], quarter, lax.axis_index("blk") * quarter)
    rows = HALF * elements
    states = jnp.concatenate(
        [left[0:rows, 0:width], middle[0:rows, 0:width], right[0:rows, 0:width]], axis=0
    ).astype(BF16)
    face, fold = lane_tables(quarter, faces)
    own_lane = per_lane(face, owner[...].astype(F32))
    target_lane = per_lane(face, targets(side[...], peer[...], slot, elements))
    products = dot_nt(states, coupling[...])
    places = lax.broadcasted_iota(jnp.int32, (3 * rows, lanes), 0).astype(F32)
    terms = jnp.sum(jnp.where(places == target_lane, products, 0.0), axis=0, keepdims=True)
    element = lax.broadcasted_iota(jnp.int32, (elements, lanes), 0).astype(F32)
    spread = jnp.where(element == own_lane, terms, 0.0)
    folded = dot_nt(two_parts(spread), fold)
    coupled = folded[0:elements] + folded[elements : 2 * elements]
    coupled = coupled + (kept[...] + left[rows:, 0:quarter] + right[rows:, 0:quarter])
    coupled = (coupled * mask).astype(BF16).astype(F32)
    if len(rest) == 2:
        weight = rest[0][...]
        for q in range(4):
            out[q, :, 128:640] = weight
    for q in range(4):
        out[q, :, 0:quarter] = coupled


def update(inv_diag, inv_off, base, gathered, mask, blk, wide):
    elements, quarter = base.shape
    for q in range(4):
        wide[:, q * quarter : (q + 1) * quarter] = gathered[q, :, 0:quarter]
    product = block_apply(inv_off, wide[...].astype(BF16), elements, quarter)
    own = gathered[blk, :, 0:quarter]
    return (base[...] - (inv_diag[...] * own + product)) * mask


def sweep_kernel(
    degree, owner, side, peer, coupling, inv_diag, inv_off, base, gathered, out, weight_out, wide
):
    elements, quarter = base.shape
    faces = owner.shape[1]
    slot = lax.axis_index("dom") % HALF
    blk = lax.axis_index("blk")
    mask = mask_of(degree[...], quarter, blk * quarter)
    adjoint = update(inv_diag, inv_off, base, gathered, mask, blk, wide)
    state = adjoint.astype(BF16).astype(F32)
    target = targets(side[...], peer[...], slot, elements)
    put_transposed(out, coupling[...], state, owner[...], target, elements, quarter, faces)
    weight_out[...] = (gathered[0, :, 128:640] + gathered[1, :, 128:640]) + (
        gathered[2, :, 128:640] + gathered[3, :, 128:640]
    )


def last_kernel(degree, inv_diag, inv_off, base, weight, gathered, adjoint_out, indicator, wide):
    elements, quarter = base.shape
    width = 4 * quarter
    blk = lax.axis_index("blk")
    mask = mask_of(degree[...], quarter, blk * quarter)
    adjoint_out[...] = update(inv_diag, inv_off, base, gathered, mask, blk, wide)
    dual = jnp.sum(weight[:, 0:width] * wide[...], axis=1, keepdims=True)
    indicator[...] = as_row(weight[:, 384:385] - dual, elements)


def call(body, shapes, *args, scratch=()):
    return pl.pallas_call(
        body,
        out_shape=shapes,
        scratch_shapes=scratch,
        compiler_params=pltpu.CompilerParams(vmem_limit_bytes=24 << 20),
    )(*args)


def hop(block, distance):
    count = lax.axis_size("dom")
    return lax.ppermute(block, "dom", [(i, (i + distance) % count) for i in range(count)])


def local(degree, face_elem, face_side, face_peer, coupling, inv_diag, inv_off, source, residual):
    elements, quarter = source.shape
    faces, _, width = coupling.shape
    doms = lax.axis_size("dom")
    groups = [
        [(first + i) * 4 + q for i in range(HALF) for q in range(4)] for first in range(0, doms, HALF)
    ]
    shape = lambda *dims: jax.ShapeDtypeStruct(dims, F32)
    degree = degree.reshape(1, elements)
    faces_of = [x.reshape(1, faces) for x in (face_elem, face_side, face_peer)]
    coupling = coupling.reshape(faces * quarter, width)
    inv_off = inv_off.reshape(elements * quarter, width)
    wide = [pltpu.VMEM((elements, width), F32)]
    across = lambda x: lax.all_to_all(x, "blk", 0, 0)
    group = lambda x: lax.all_to_all(x, ("dom", "blk"), 0, 0, axis_index_groups=groups)

    gathered = across(call(first_kernel, shape(4, elements, 128), degree, source))
    message_shape = shape(16, 4 * elements, 128)
    message, base, weight = call(
        base_kernel,
        (message_shape, shape(elements, quarter), shape(elements, 512)),
        degree, *faces_of, coupling, inv_diag, inv_off, source, residual, gathered,
        scratch=wide,
    )
    for sweep in range(SWEEPS):
        hop_shape = shape(HALF * elements + elements, 384)
        ahead, behind, kept = call(
            merge_kernel, (hop_shape, hop_shape, shape(elements, quarter)), group(message)
        )
        left = hop(ahead, HALF)
        right = hop(behind, -HALF)
        extra = (weight,) if sweep == 0 else ()
        coupled = call(
            couple_kernel,
            shape(4, elements, 640 if sweep == 0 else 128),
            degree, *faces_of, coupling, left, ahead, right, kept, *extra,
        )
        gathered = across(coupled)
        if sweep == 0:
            message, weight = call(
                sweep_kernel,
                (message_shape, shape(elements, 512)),
                degree, *faces_of, coupling, inv_diag, inv_off, base, gathered,
                scratch=wide,
            )
    adjoint, indicator = call(
        last_kernel,
        (shape(elements, quarter), shape(1, elements)),
        degree, inv_diag, inv_off, base, weight, gathered,
        scratch=wide,
    )
    return adjoint, indicator.reshape(elements)


def solution(mesh):
    in_specs = (
        P("dom"),
        P("dom"),
        P("dom"),
        P("dom"),
        P("dom", "blk", None),
        P("dom", "blk"),
        P("dom", "blk", None),
        P("dom", "blk"),
        P("dom", "blk"),
    )
    out_specs = (P("dom", "blk"), P("dom"))
    return jax.shard_map(local, mesh=mesh, in_specs=in_specs, out_specs=out_specs, check_vma=False)
```

time: 315 us -> 98.1 us (0.31)
  the two profiles are of different devices: /device:TPU:96 before, /device:TPU:32 now
where the time goes in v1:
time: 98.1 us; the launch traced here: 97.5 us
  blocking collectives  48.3 us (49%)
  starting transfers between devices  19.4 us (20%)
  waiting for transfers between devices  16.4 us (17%)
  local copies, waits for them, and re-layouts  7.32 us (7%)
  Pallas kernels  5.3 us (5%)
    all_to_all x3, blocking collectives, local(): across = lambda x: lax.all_to_all(x, 'blk', 0, 0)  25.5 us
    all_to_all x2, blocking collectives, local(): lax.all_to_all(x, ('dom', 'blk'), 0, 0, axis_index_groups=groups)  22.8 us
    ppermute x4, starting transfers between devices, hop(): lax.ppermute(block, 'dom', [(i, (i + distance) % count) for i in range(co...  19.4 us
    ppermute x4, waiting for transfers between devices, hop(): lax.ppermute(block, 'dom', [(i, (i + distance) % count) for i in range(co...  16.4 us
    unnamed x32, local copies, waits for them, and re-layouts  7.32 us
    pallas_call x8, Pallas kernels, call(): pl.pallas_call(body, out_shape=shapes, scratch_shapes=scratch, compiler_p...  5.3 us
  transfers between devices with their start and end apart: 4, of which 3 were waited for; matrix products, arithmetic and copies ran while one was open for 0% of the time, Pallas kernels for 0%

profile of v1, /device:TPU:32, one launch (start us, length us, event | category | flops | bytes accessed | tf_op | source)
XLA Modules:
  0.0 97.5 jit_solution(3104580917446356297)
XLA Ops:
  0.6 0.0 copy-start.7
  0.6 0.0 copy-start.12
  0.7 0.0 copy-start.10
  0.7 0.0 copy-start.6
  0.7 0.7 copy-done.6
  1.4 0.0 copy-start.8
  1.4 0.7 copy-done.8
  2.0 0.0 copy-start.14
  2.0 0.1 shard_map.104
  2.1 9.6 %all_to_all.25.gathered = f32[4,8,128]{2,1,0:T(8,128)S(1)} all-to-all(f32[4,8,128]{2,1,0:T(8,128)S(1)} %shard_map.104), channel_id=1, replica_groups=mesh['dom'=128,'blk'=4] {'blk'}, dimensions={0} | all-to-all | bytes 32768 | tf_op jit(solution)/shard_map/all_to_all | solution.py:263
  11.8 0.0 copy-start
  11.8 1.5 %copy-done = bf16[32,80,320]{2,1,0:T(8,128)(2,1)S(1)} copy-done((bf16[32,80,320]{2,1,0:T(8,128)(2,1)S(1)}, bf16[32,80,320]{2,1,0:T(8,128)(2,1)}, u32[]{:S(2)}) %copy-start) | copy-done | bytes 1638424
  13.3 0.0 copy-start.2
  13.3 1.0 %copy-done.2 = bf16[8,80,320]{2,1,0:T(8,128)(2,1)S(1)} copy-done((bf16[8,80,320]{2,1,0:T(8,128)(2,1)S(1)}, bf16[8,80,320]{2,1,0:T(8,128)(2,1)}, u32[]{:S(2)}) %copy-start.2) | copy-done | bytes 409624
  14.3 0.0 copy-start.4
  14.3 0.7 copy-done.4
  15.0 0.7 copy-done.9
  15.7 0.7 copy-done.11
  16.3 0.7 copy-done.13
  17.0 0.7 copy-done.15
  17.7 1.1 %shard_map.105 = (f32[16,32,128]{2,1,0:T(8,128)S(1)}, f32[8,80]{1,0:T(8,128)S(1)}, f32[8,512]{1,0:T(8,128)S(1)}) custom-call(s32[1,8]{1,0:T(1,128)S(1)} %bitcast.15, s32[1,32]{1,0:T(1,128)S(1)} %bitcast.20, s32[1,32]{1,0:T(1,128)S(1)} %bitcast.24, s32[1,32]{1,0:T(1,128)S(1)} %bitcast.28, bf16[2560,320]{1,0:T(8,128)(2,1)S(1)} %bitcast.7, ...), custom_call_target="tpu_custom_call" | custom-call | tf_op jit(solution)/shard_map/pallas_call | solution.py:237
  18.7 0.0 copy-start.3
  18.8 0.0 copy-start.5
  18.8 12.7 %all_to_all.26.message = f32[16,32,128]{2,1,0:T(8,128)S(1)} all-to-all(f32[16,32,128]{2,1,0:T(8,128)S(1)} %get-tuple-element.16), channel_id=1, replica_groups={{0,1,2,3,4,5,6,7,8,9,10,11,12,13,14,15},{16,17,18,19,20,21,22,23,24,25,..., dimensions={0} | all-to-all | bytes 524288 | tf_op jit(solution)/shard_map/all_to_all | solution.py:264
  31.4 0.1 shard_map.106
  31.5 10.7 %collective-permute-start.1 = (f32[40,384]{1,0:T(8,128)S(1)}, f32[40,384]{1,0:T(8,128)S(1)}, u32[]{:S(2)}, u32[]{:S(2)}) collective-permute-start(f32[40,384]{1,0:T(8,128)S(1)} %get-tuple-element.18), channel_id=1, source_target_pairs={{0,496},{4,500},{8,504},{12,508},{16,0},{20,4},{24,8},{28,12},{32,... | collective-permute-start | bytes 184328 | tf_op jit(solution)/shard_map/ppermute | solution.py:247
  42.2 1.9 %collective-permute-start = (f32[40,384]{1,0:T(8,128)S(1)}, f32[40,384]{1,0:T(8,128)S(1)}, u32[]{:S(2)}, u32[]{:S(2)}) collective-permute-start(f32[40,384]{1,0:T(8,128)S(1)} %get-tuple-element.17.middle), channel_id=1, source_target_pairs={{0,16},{4,20},{8,24},{12,28},{16,32},{20,36},{24,40},{28,44},{32,4... | collective-permute-start | bytes 184328 | tf_op jit(solution)/shard_map/ppermute | solution.py:247
  44.2 0.0 collective-permute-done.1.right
  44.2 9.5 %collective-permute-done.left = f32[40,384]{1,0:T(8,128)S(1)} collective-permute-done((f32[40,384]{1,0:T(8,128)S(1)}, f32[40,384]{1,0:T(8,128)S(1)}, u32[]{:S(2)}, u32[]{:S(2)}) %collective-permute-start) | collective-permute-done | bytes 61472 | tf_op jit(solution)/shard_map/ppermute | solution.py:247
  53.7 0.0 copy-done.7
  53.7 0.0 copy-done.12
  53.7 0.0 copy-done.10
  53.7 0.0 copy-done.14
  53.7 0.0 copy-done.1
  53.7 1.0 %shard_map.107 = f32[4,8,640]{2,1,0:T(8,128)S(1)} custom-call(s32[1,8]{1,0:T(1,128)S(1)} %bitcast.16, s32[1,32]{1,0:T(1,128)S(1)} %bitcast.21, s32[1,32]{1,0:T(1,128)S(1)} %bitcast.25, s32[1,32]{1,0:T(1,128)S(1)} %bitcast.29, bf16[2560,320]{1,0:T(8,128)(2,1)S(1)} %bitcast.8, f32[40,384]{1,0:T(8,128)S(1)} %collective-permute-done.left, ...), custom_call_target="tpu_custom_call" | custom-call | tf_op jit(solution)/shard_map/pallas_call | solution.py:237
  54.7 8.2 %all_to_all.27.gathered = f32[4,8,640]{2,1,0:T(8,128)S(1)} all-to-all(f32[4,8,640]{2,1,0:T(8,128)S(1)} %shard_map.107), channel_id=1, replica_groups=mesh['dom'=128,'blk'=4] {'blk'}, dimensions={0} | all-to-all | bytes 163840 | tf_op jit(solution)/shard_map/all_to_all | solution.py:263
  62.9 0.0 copy-done.3
  62.9 0.0 copy-done.5
  62.9 1.0 %shard_map.108 = (f32[16,32,128]{2,1,0:T(8,128)S(1)}, f32[8,512]{1,0:T(8,128)S(1)}) custom-call(s32[1,8]{1,0:T(1,128)S(1)} %bitcast.17, s32[1,32]{1,0:T(1,128)S(1)} %bitcast.22, s32[1,32]{1,0:T(1,128)S(1)} %bitcast.26, s32[1,32]{1,0:T(1,128)S(1)} %bitcast.30, bf16[2560,320]{1,0:T(8,128)(2,1)S(1)} %bitcast.9, f32[8,80]{1,0:T(8,128)S(1)} %copy-done.5, ...), custom_call_target="tpu_custom_call" | custom-call | tf_op jit(solution)/shard_map/pallas_call | solution.py:237
  63.9 10.1 %all_to_all.28.message = f32[16,32,128]{2,1,0:T(8,128)S(1)} all-to-all(f32[16,32,128]{2,1,0:T(8,128)S(1)} %get-tuple-element.22), channel_id=1, replica_groups={{0,1,2,3,4,5,6,7,8,9,10,11,12,13,14,15},{16,17,18,19,20,21,22,23,24,25,..., dimensions={0} | all-to-all | bytes 524288 | tf_op jit(solution)/shard_map/all_to_all | solution.py:264
  74.0 0.1 shard_map.109
  74.1 1.9 %collective-permute-start.3 = (f32[40,384]{1,0:T(8,128)S(1)}, f32[40,384]{1,0:T(8,128)S(1)}, u32[]{:S(2)}, u32[]{:S(2)}) collective-permute-start(f32[40,384]{1,0:T(8,128)S(1)} %get-tuple-element.24), channel_id=1, source_target_pairs={{0,496},{4,500},{8,504},{12,508},{16,0},{20,4},{24,8},{28,12},{32,... | collective-permute-start | bytes 184328 | tf_op jit(solution)/shard_map/ppermute | solution.py:247
  76.1 4.8 %collective-permute-start.2 = (f32[40,384]{1,0:T(8,128)S(1)}, f32[40,384]{1,0:T(8,128)S(1)}, u32[]{:S(2)}, u32[]{:S(2)}) collective-permute-start(f32[40,384]{1,0:T(8,128)S(1)} %get-tuple-element.23.middle), channel_id=1, source_target_pairs={{0,16},{4,20},{8,24},{12,28},{16,32},{20,36},{24,40},{28,44},{32,4... | collective-permute-start | bytes 184328 | tf_op jit(solution)/shard_map/ppermute | solution.py:247
  80.9 0.4 collective-permute-done.3.right
  81.3 6.5 %collective-permute-done.2.left = f32[40,384]{1,0:T(8,128)S(1)} collective-permute-done((f32[40,384]{1,0:T(8,128)S(1)}, f32[40,384]{1,0:T(8,128)S(1)}, u32[]{:S(2)}, u32[]{:S(2)}) %collective-permute-start.2) | collective-permute-done | bytes 61472 | tf_op jit(solution)/shard_map/ppermute | solution.py:247
  87.8 1.0 %shard_map.110 = f32[4,8,128]{2,1,0:T(8,128)S(1)} custom-call(s32[1,8]{1,0:T(1,128)S(1)} %bitcast.18, s32[1,32]{1,0:T(1,128)S(1)} %bitcast.23, s32[1,32]{1,0:T(1,128)S(1)} %bitcast.27, s32[1,32]{1,0:T(1,128)S(1)} %bitcast.31, bf16[2560,320]{1,0:T(8,128)(2,1)S(1)} %bitcast.10, f32[40,384]{1,0:T(8,128)S(1)} %collective-permute-done.2.left, ...), custom_call_target="tpu_custom_call" | custom-call | tf_op jit(solution)/shard_map/pallas_call | solution.py:237
  88.8 7.7 %all_to_all.29.gathered = f32[4,8,128]{2,1,0:T(8,128)S(1)} all-to-all(f32[4,8,128]{2,1,0:T(8,128)S(1)} %shard_map.110), channel_id=1, replica_groups=mesh['dom'=128,'blk'=4] {'blk'}, dimensions={0} | all-to-all | bytes 32768 | tf_op jit(solution)/shard_map/all_to_all | solution.py:263
  96.5 0.9 shard_map.111
  (5 shorter events, 0.0 us)
Async XLA Ops:
  0.6 53.0 %copy-start.7 = (s32[8]{0:T(128)S(1)}, s32[8]{0:T(128)}, u32[]{:S(2)}) copy-start(s32[8]{0:T(128)} %param.9) | copy-start | bytes 100
  0.6 53.0 %copy-start.12 = (s32[32]{0:T(128)S(1)}, s32[32]{0:T(128)}, u32[]{:S(2)}) copy-start(s32[32]{0:T(128)} %param.11) | copy-start | bytes 388
  0.7 53.0 %copy-start.10 = (s32[32]{0:T(128)S(1)}, s32[32]{0:T(128)}, u32[]{:S(2)}) copy-start(s32[32]{0:T(128)} %param.10) | copy-start | bytes 388
  0.7 0.7 copy-start.6
  1.4 0.7 copy-start.8
  2.0 51.6 %copy-start.14 = (s32[32]{0:T(128)S(1)}, s32[32]{0:T(128)}, u32[]{:S(2)}) copy-start(s32[32]{0:T(128)} %param.12) | copy-start | bytes 388
  11.8 1.5 %copy-start = (bf16[32,80,320]{2,1,0:T(8,128)(2,1)S(1)}, bf16[32,80,320]{2,1,0:T(8,128)(2,1)}, u32[]{:S(2)}) copy-start(bf16[32,80,320]{2,1,0:T(8,128)(2,1)} %param.13) | copy-start | bytes 4915204
  13.3 1.0 %copy-start.2 = (bf16[8,80,320]{2,1,0:T(8,128)(2,1)S(1)}, bf16[8,80,320]{2,1,0:T(8,128)(2,1)}, u32[]{:S(2)}) copy-start(bf16[8,80,320]{2,1,0:T(8,128)(2,1)} %param.15) | copy-start | bytes 1228804
  14.3 0.7 copy-start.4
  15.0 0.7 copy-start.9
  15.7 0.7 copy-start.11
  16.3 0.7 copy-start.13
  17.0 0.7 copy-start.15
  17.7 36.0 %copy-start.1 = (bf16[32,80,320]{2,1,0:T(8,128)(2,1)S(1)}, bf16[32,80,320]{2,1,0:T(8,128)(2,1)}, u32[]{:S(2)}) copy-start(bf16[32,80,320]{2,1,0:T(8,128)(2,1)} %param.13) | copy-start | bytes 4915204
  18.7 44.2 %copy-start.3 = (bf16[8,80,320]{2,1,0:T(8,128)(2,1)S(1)}, bf16[8,80,320]{2,1,0:T(8,128)(2,1)}, u32[]{:S(2)}) copy-start(bf16[8,80,320]{2,1,0:T(8,128)(2,1)} %param.15) | copy-start | bytes 1228804
  18.8 44.2 %copy-start.5 = (f32[8,80]{1,0:T(8,128)S(1)}, f32[8,80]{1,0:T(8,128)}, u32[]{:S(2)}) copy-start(f32[8,80]{1,0:T(8,128)} %inv_diag.5) | copy-start | bytes 7684
  31.5 12.7 %collective-permute-start.1 = (f32[40,384]{1,0:T(8,128)S(1)}, f32[40,384]{1,0:T(8,128)S(1)}, u32[]{:S(2)}, u32[]{:S(2)}) collective-permute-start(f32[40,384]{1,0:T(8,128)S(1)} %get-tuple-element.18), channel_id=1, source_target_pairs={{0,496},{4,500},{8,504},{12,508},{16,0},{20,4},{24,8},{28,12},{32,... | collective-permute-start | bytes 184328 | tf_op jit(solution)/shard_map/ppermute | solution.py:247
  42.2 11.4 %collective-permute-start = (f32[40,384]{1,0:T(8,128)S(1)}, f32[40,384]{1,0:T(8,128)S(1)}, u32[]{:S(2)}, u32[]{:S(2)}) collective-permute-start(f32[40,384]{1,0:T(8,128)S(1)} %get-tuple-element.17.middle), channel_id=1, source_target_pairs={{0,16},{4,20},{8,24},{12,28},{16,32},{20,36},{24,40},{28,44},{32,4... | collective-permute-start | bytes 184328 | tf_op jit(solution)/shard_map/ppermute | solution.py:247
  74.1 7.2 %collective-permute-start.3 = (f32[40,384]{1,0:T(8,128)S(1)}, f32[40,384]{1,0:T(8,128)S(1)}, u32[]{:S(2)}, u32[]{:S(2)}) collective-permute-start(f32[40,384]{1,0:T(8,128)S(1)} %get-tuple-element.24), channel_id=1, source_target_pairs={{0,496},{4,500},{8,504},{12,508},{16,0},{20,4},{24,8},{28,12},{32,... | collective-permute-start | bytes 184328 | tf_op jit(solution)/shard_map/ppermute | solution.py:247
  76.1 11.7 %collective-permute-start.2 = (f32[40,384]{1,0:T(8,128)S(1)}, f32[40,384]{1,0:T(8,128)S(1)}, u32[]{:S(2)}, u32[]{:S(2)}) collective-permute-start(f32[40,384]{1,0:T(8,128)S(1)} %get-tuple-element.23.middle), channel_id=1, source_target_pairs={{0,16},{4,20},{8,24},{12,28},{16,32},{20,36},{24,40},{28,44},{32,4... | collective-permute-start | bytes 184328 | tf_op jit(solution)/shard_map/ppermute | solution.py:247

commit v2 on v1

--- a/solution.py
+++ b/solution.py
@@ -74,6 +74,13 @@
     return ((HALF + slot + offset) * elements + peer).astype(F32)
 
 
+def fetch(pairs, arrived):
+    copies = [pltpu.make_async_copy(a, b, arrived.at[i]) for i, (a, b) in enumerate(pairs)]
+    for copy in copies:
+        copy.start()
+    return copies
+
+
 def block_apply(inv_off, vector, elements, quarter):
     row = lax.broadcasted_iota(jnp.int32, (elements, quarter), 0)
     total = jnp.zeros((elements, quarter), F32)
@@ -83,7 +90,7 @@
     return total
 
 
-def put_transposed(out, coupling, state, owner, target, elements, quarter, faces):
+def put_transposed(out, coupling, state, owner, target, elements, quarter, faces, ready=None):
     face, fold = lane_tables(quarter, faces)
     own_lane = per_lane(face, owner.astype(F32))
     target_lane = per_lane(face, target)
@@ -94,17 +101,21 @@
     count = 3 * HALF * elements
     places = lax.broadcasted_iota(jnp.int32, (count, lanes), 0).astype(F32)
     chosen = jnp.where(places == target_lane, spread, 0.0).astype(BF16)
-    transposed = dot(chosen, coupling)
-    for q in range(4):
-        part = transposed[:, q * quarter : (q + 1) * quarter]
+    if ready is not None:
+        ready.wait()
+    transposed = dot(chosen, coupling[...])
+    for q in range(4):
+        part = transposed[:, q * quarter : (q + 1) * quarter].astype(BF16)
         for r in range(HALF):
             for s in range(3):
                 at = (s * HALF + r) * elements
                 out[r * 4 + q, s * elements : (s + 1) * elements, 0:quarter] = part[at : at + elements]
-            out[r * 4 + q, 3 * elements : 4 * elements, 0:quarter] = state
-
-
-def first_kernel(degree, source, out):
+            out[r * 4 + q, 3 * elements : 4 * elements, 0:quarter] = state.astype(BF16)
+
+
+def first_kernel(degree_in, source_in, out, degree, source, arrived):
+    for copy in fetch([(degree_in, degree), (source_in, source)], arrived):
+        copy.wait()
     elements, quarter = source.shape
     first = lax.axis_index("blk") * quarter
     half = (source[...] * mask_of(degree[...], quarter, first)).astype(BF16).astype(F32)
@@ -112,25 +123,26 @@
         out[q, :, 0:quarter] = half
 
 
-def base_kernel(
-    degree, owner, side, peer, coupling, inv_diag, inv_off, source, residual, gathered,
-    out, base_out, weight_out, wide,
-):
+def base_kernel(*refs):
+    far, gathered, (out, base_out, weight_out), near = refs[0:9], refs[9], refs[10:13], refs[13:22]
+    wide, arrived = refs[22:24]
+    degree, owner, side, peer, inv_diag, source, residual, inv_off, coupling = near
+    copies = fetch(list(zip(far, near)), arrived)
     elements, quarter = source.shape
     faces = owner.shape[1]
     width = 4 * quarter
     slot = lax.axis_index("dom") % HALF
     blk = lax.axis_index("blk")
+    for q in range(4):
+        wide[:, q * quarter : (q + 1) * quarter] = gathered[q, :, 0:quarter]
+    for copy in copies[:-1]:
+        copy.wait()
     mask = mask_of(degree[...], quarter, blk * quarter)
-    for q in range(4):
-        wide[:, q * quarter : (q + 1) * quarter] = gathered[q, :, 0:quarter]
     own = (source[...] * mask).astype(BF16).astype(F32)
     product = block_apply(inv_off, wide[...].astype(BF16), elements, quarter)
     base = (inv_diag[...] * own + product) * mask
     base_out[...] = base
     state = base.astype(BF16).astype(F32)
-    target = targets(side[...], peer[...], slot, elements)
-    put_transposed(out, coupling[...], state, owner[...], target, elements, quarter, faces)
     weighted = residual[...] * mask
     parts = two_parts(weighted)
     row = lax.broadcasted_iota(jnp.int32, (elements, width), 0)
@@ -147,22 +159,27 @@
     weight_out[:, 384:512] = jnp.broadcast_to(
         jnp.sum(weighted * base, axis=1, keepdims=True), (elements, 128)
     )
+    target = targets(side[...], peer[...], slot, elements)
+    put_transposed(
+        out, coupling, state, owner[...], target, elements, quarter, faces, copies[-1]
+    )
 
 
 def merge_kernel(message, ahead, behind, kept):
     elements, quarter = kept.shape
-    total = message[0, 0 : 3 * elements, 0:quarter]
+    total = message[0, 0 : 3 * elements, 0:quarter].astype(F32)
     for i in range(1, 16):
-        total = total + message[i, 0 : 3 * elements, 0:quarter]
-    behind[HALF * elements :, 0:quarter] = total[0:elements]
+        total = total + message[i, 0 : 3 * elements, 0:quarter].astype(F32)
+    rows = HALF * elements
+    behind[rows:, 0:quarter] = two_parts(total[0:elements])
     kept[...] = total[elements : 2 * elements]
-    ahead[HALF * elements :, 0:quarter] = total[2 * elements : 3 * elements]
-    for r in range(HALF):
-        for q in range(4):
-            state = message[r * 4 + q, 3 * elements : 4 * elements, 0:quarter]
-            rows = slice(r * elements, (r + 1) * elements)
-            ahead[rows, q * quarter : (q + 1) * quarter] = state
-            behind[rows, q * quarter : (q + 1) * quarter] = state
+    ahead[rows:, 0:quarter] = two_parts(total[2 * elements : 3 * elements])
+    for q in range(4):
+        state = jnp.concatenate(
+            [message[r * 4 + q, 3 * elements :, 0:quarter].astype(F32) for r in range(HALF)], axis=0
+        ).astype(BF16)
+        ahead[0:rows, q * quarter : (q + 1) * quarter] = state
+        behind[0:rows, q * quarter : (q + 1) * quarter] = state
 
 
 def couple_kernel(degree, owner, side, peer, coupling, left, middle, right, kept, *rest):
@@ -176,7 +193,7 @@
     rows = HALF * elements
     states = jnp.concatenate(
         [left[0:rows, 0:width], middle[0:rows, 0:width], right[0:rows, 0:width]], axis=0
-    ).astype(BF16)
+    )
     face, fold = lane_tables(quarter, faces)
     own_lane = per_lane(face, owner[...].astype(F32))
     target_lane = per_lane(face, targets(side[...], peer[...], slot, elements))
@@ -187,7 +204,10 @@
     spread = jnp.where(element == own_lane, terms, 0.0)
     folded = dot_nt(two_parts(spread), fold)
     coupled = folded[0:elements] + folded[elements : 2 * elements]
-    coupled = coupled + (kept[...] + left[rows:, 0:quarter] + right[rows:, 0:quarter])
+    coupled = coupled + kept[...]
+    for sent in (left, right):
+        pair = sent[rows:, 0:quarter].astype(F32)
+        coupled = coupled + (pair[0:elements] + pair[elements : 2 * elements])
     coupled = (coupled * mask).astype(BF16).astype(F32)
     if len(rest) == 2:
         weight = rest[0][...]
@@ -217,7 +237,7 @@
     adjoint = update(inv_diag, inv_off, base, gathered, mask, blk, wide)
     state = adjoint.astype(BF16).astype(F32)
     target = targets(side[...], peer[...], slot, elements)
-    put_transposed(out, coupling[...], state, owner[...], target, elements, quarter, faces)
+    put_transposed(out, coupling, state, owner[...], target, elements, quarter, faces)
     weight_out[...] = (gathered[0, :, 128:640] + gathered[1, :, 128:640]) + (
         gathered[2, :, 128:640] + gathered[3, :, 128:640]
     )
@@ -233,13 +253,16 @@
     indicator[...] = as_row(weight[:, 384:385] - dual, elements)
 
 
-def call(body, shapes, *args, scratch=()):
+def call(body, shapes, *args, scratch=(), far=0):
+    space = lambda i: pl.BlockSpec(memory_space=pltpu.HBM if i < far else pltpu.VMEM)
+    near = [pltpu.VMEM(x.shape, x.dtype) for x in args[:far]]
     return pl.pallas_call(
         body,
         out_shape=shapes,
-        scratch_shapes=scratch,
+        in_specs=[space(i) for i in range(len(args))],
+        scratch_shapes=[*near, *scratch, *([pltpu.SemaphoreType.DMA((far,))] if far else [])],
         compiler_params=pltpu.CompilerParams(vmem_limit_bytes=24 << 20),
-    )(*args)
+    )(*[pltpu.with_memory_space_constraint(x, pltpu.HBM) for x in args[:far]], *args[far:])
 
 
 def hop(block, distance):
@@ -254,7 +277,7 @@
     groups = [
         [(first + i) * 4 + q for i in range(HALF) for q in range(4)] for first in range(0, doms, HALF)
     ]
-    shape = lambda *dims: jax.ShapeDtypeStruct(dims, F32)
+    shape = lambda *dims, kind=F32: jax.ShapeDtypeStruct(dims, kind)
     degree = degree.reshape(1, elements)
     faces_of = [x.reshape(1, faces) for x in (face_elem, face_side, face_peer)]
     coupling = coupling.reshape(faces * quarter, width)
@@ -263,16 +286,16 @@
     across = lambda x: lax.all_to_all(x, "blk", 0, 0)
     group = lambda x: lax.all_to_all(x, ("dom", "blk"), 0, 0, axis_index_groups=groups)
 
-    gathered = across(call(first_kernel, shape(4, elements, 128), degree, source))
-    message_shape = shape(16, 4 * elements, 128)
+    gathered = across(call(first_kernel, shape(4, elements, 128), degree, source, far=2))
+    message_shape = shape(16, 4 * elements, 128, kind=BF16)
     message, base, weight = call(
         base_kernel,
         (message_shape, shape(elements, quarter), shape(elements, 512)),
-        degree, *faces_of, coupling, inv_diag, inv_off, source, residual, gathered,
-        scratch=wide,
+        degree, *faces_of, inv_diag, source, residual, inv_off, coupling, gathered,
+        scratch=wide, far=9,
     )
     for sweep in range(SWEEPS):
-        hop_shape = shape(HALF * elements + elements, 384)
+        hop_shape = shape(HALF * elements + 2 * elements, 384, kind=BF16)
         ahead, behind, kept = call(
             merge_kernel, (hop_shape, hop_shape, shape(elements, quarter)), group(message)
         )

time: 98.1 us -> 88.1 us (0.90)
  local copies, waits for them, and re-layouts: 7.32 us -> 0.04 us
  waiting for transfers between devices: 16.4 us -> 13.6 us
  Pallas kernels: 5.3 us -> 7.56 us
  blocking collectives: 48.3 us -> 46.2 us
    unnamed x32 -> x14, local copies, waits for them, and re-layouts: 7.32 us -> 0.04 us
    ppermute x4, waiting for transfers between devices: 16.4 us -> 13.6 us  [hop(): lax.ppermute(block, 'dom', [(i, (i + distance) % count) for i in range(co...]
    all_to_all x2, blocking collectives: 22.8 us -> 20.4 us  [local(): lax.all_to_all(x, ('dom', 'blk'), 0, 0, axis_index_groups=groups)]
    pallas_call x8, Pallas kernels: 5.3 us -> 7.56 us  [call(): pl.pallas_call(body, out_shape=shapes, in_specs=[space(i) for i in range(...]
  transfers between devices with their start and end apart: 4 -> 4, of which waited for: 3 -> 2; matrix products, arithmetic and copies ran while one was open for 0% -> 0% of each run, Pallas kernels for 0% -> 0%
where the time goes in v2:
time: 88.1 us; the launch traced here: 87.7 us
  blocking collectives  46.2 us (52%)
  starting transfers between devices  19.5 us (22%)
  waiting for transfers between devices  13.6 us (15%)
  Pallas kernels  7.56 us (9%)
    all_to_all x3, blocking collectives, local(): across = lambda x: lax.all_to_all(x, 'blk', 0, 0)  25.8 us
    all_to_all x2, blocking collectives, local(): lax.all_to_all(x, ('dom', 'blk'), 0, 0, axis_index_groups=groups)  20.4 us
    ppermute x4, starting transfers between devices, hop(): lax.ppermute(block, 'dom', [(i, (i + distance) % count) for i in range(co...  19.5 us
    ppermute x4, waiting for transfers between devices, hop(): lax.ppermute(block, 'dom', [(i, (i + distance) % count) for i in range(co...  13.6 us
    pallas_call x8, Pallas kernels, call(): pl.pallas_call(body, out_shape=shapes, in_specs=[space(i) for i in range(...  7.56 us
  transfers between devices with their start and end apart: 4, of which 2 were waited for; matrix products, arithmetic and copies ran while one was open for 0% of the time, Pallas kernels for 0%

profile of v2, /device:TPU:32, one launch (start us, length us, event | category | flops | bytes accessed | tf_op | source)
XLA Modules:
  0.0 87.7 jit_solution(10955762093842577519)
XLA Ops:
  0.6 0.0 copy-start.3
  0.6 0.0 copy-start
  0.7 0.0 copy-start.6
  0.7 0.0 copy-start.5
  0.7 0.0 copy-start.4
  0.7 0.9 %shard_map.104 = f32[4,8,128]{2,1,0:T(8,128)S(1)} custom-call(s32[1,8]{1,0:T(1,128)} %bitcast.14, f32[8,80]{1,0:T(8,128)} %refs_5_.1), custom_call_target="tpu_custom_call" | custom-call | tf_op jit(solution)/shard_map/pallas_call | solution.py:259
  1.6 9.6 %all_to_all.25.refs_9_ = f32[4,8,128]{2,1,0:T(8,128)S(1)} all-to-all(f32[4,8,128]{2,1,0:T(8,128)S(1)} %shard_map.104), channel_id=1, replica_groups=mesh['dom'=128,'blk'=4] {'blk'}, dimensions={0} | all-to-all | bytes 32768 | tf_op jit(solution)/shard_map/all_to_all | solution.py:286
  11.3 2.5 %shard_map.105 = (bf16[16,32,128]{2,1,0:T(8,128)(2,1)S(1)}, f32[8,80]{1,0:T(8,128)S(1)}, f32[8,512]{1,0:T(8,128)S(1)}) custom-call(s32[1,8]{1,0:T(1,128)} %bitcast.15, s32[1,32]{1,0:T(1,128)} %bitcast.20, s32[1,32]{1,0:T(1,128)} %bitcast.24, s32[1,32]{1,0:T(1,128)} %bitcast.28, f32[8,80]{1,0:T(8,128)} %inv_diag.3, f32[8,80]{1,0:T(8,128)} %refs_5_.1, ...), custom_call_target="tpu_custom_call" | custom-call | tf_op jit(solution)/shard_map/pallas_call | solution.py:259
  13.7 0.0 copy-start.1
  13.7 0.0 copy-start.2
  13.8 11.4 %all_to_all.26.message = bf16[16,32,128]{2,1,0:T(8,128)(2,1)S(1)} all-to-all(bf16[16,32,128]{2,1,0:T(8,128)(2,1)S(1)} %get-tuple-element.16), channel_id=1, replica_groups={{0,1,2,3,4,5,6,7,8,9,10,11,12,13,14,15},{16,17,18,19,20,21,22,23,24,25,..., dimensions={0} | all-to-all | bytes 262144 | tf_op jit(solution)/shard_map/all_to_all | solution.py:287
  25.1 0.1 shard_map.106
  25.2 10.8 %collective-permute-start.1 = (bf16[48,384]{1,0:T(8,128)(2,1)S(1)}, bf16[48,384]{1,0:T(8,128)(2,1)S(1)}, u32[]{:S(2)}, u32[]{:S(2)}) collective-permute-start(bf16[48,384]{1,0:T(8,128)(2,1)S(1)} %get-tuple-element.18), channel_id=1, source_target_pairs={{0,496},{4,500},{8,504},{12,508},{16,0},{20,4},{24,8},{28,12},{32,... | collective-permute-start | bytes 110600 | tf_op jit(solution)/shard_map/ppermute | solution.py:270
  36.1 1.9 %collective-permute-start = (bf16[48,384]{1,0:T(8,128)(2,1)S(1)}, bf16[48,384]{1,0:T(8,128)(2,1)S(1)}, u32[]{:S(2)}, u32[]{:S(2)}) collective-permute-start(bf16[48,384]{1,0:T(8,128)(2,1)S(1)} %get-tuple-element.17.middle), channel_id=1, source_target_pairs={{0,16},{4,20},{8,24},{12,28},{16,32},{20,36},{24,40},{28,44},{32,4... | collective-permute-start | bytes 110600 | tf_op jit(solution)/shard_map/ppermute | solution.py:270
  38.0 0.0 collective-permute-done.1.right
  38.0 8.1 %collective-permute-done.left = bf16[48,384]{1,0:T(8,128)(2,1)S(1)} collective-permute-done((bf16[48,384]{1,0:T(8,128)(2,1)S(1)}, bf16[48,384]{1,0:T(8,128)(2,1)S(1)}, u32[]{:S(2)}, u32[]{:S(2)}) %collective-permute-start) | collective-permute-done | bytes 36896 | tf_op jit(solution)/shard_map/ppermute | solution.py:270
  46.1 0.0 copy-done.3
  46.1 0.0 copy-done
  46.1 0.0 copy-done.6
  46.1 0.0 copy-done.5
  46.1 0.0 copy-done.4
  46.2 1.0 %shard_map.107 = f32[4,8,640]{2,1,0:T(8,128)S(1)} custom-call(s32[1,8]{1,0:T(1,128)S(1)} %bitcast.16, s32[1,32]{1,0:T(1,128)S(1)} %bitcast.21, s32[1,32]{1,0:T(1,128)S(1)} %bitcast.25, s32[1,32]{1,0:T(1,128)S(1)} %bitcast.29, bf16[2560,320]{1,0:T(8,128)(2,1)S(1)} %bitcast.8, bf16[48,384]{1,0:T(8,128)(2,1)S(1)} %collective-permute-done.left, ...), custom_call_target="tpu_custom_call" | custom-call | tf_op jit(solution)/shard_map/pallas_call | solution.py:259
  47.2 8.3 %all_to_all.27.gathered = f32[4,8,640]{2,1,0:T(8,128)S(1)} all-to-all(f32[4,8,640]{2,1,0:T(8,128)S(1)} %shard_map.107), channel_id=1, replica_groups=mesh['dom'=128,'blk'=4] {'blk'}, dimensions={0} | all-to-all | bytes 163840 | tf_op jit(solution)/shard_map/all_to_all | solution.py:286
  55.5 0.0 copy-done.1
  55.5 0.0 copy-done.2
  55.5 1.0 %shard_map.108 = (bf16[16,32,128]{2,1,0:T(8,128)(2,1)S(1)}, f32[8,512]{1,0:T(8,128)S(1)}) custom-call(s32[1,8]{1,0:T(1,128)S(1)} %bitcast.17, s32[1,32]{1,0:T(1,128)S(1)} %bitcast.22, s32[1,32]{1,0:T(1,128)S(1)} %bitcast.26, s32[1,32]{1,0:T(1,128)S(1)} %bitcast.30, bf16[2560,320]{1,0:T(8,128)(2,1)S(1)} %bitcast.9, f32[8,80]{1,0:T(8,128)S(1)} %copy-done.2, ...), custom_call_target="tpu_custom_call" | custom-call | tf_op jit(solution)/shard_map/pallas_call | solution.py:259
  56.5 9.0 %all_to_all.28.message = bf16[16,32,128]{2,1,0:T(8,128)(2,1)S(1)} all-to-all(bf16[16,32,128]{2,1,0:T(8,128)(2,1)S(1)} %get-tuple-element.22), channel_id=1, replica_groups={{0,1,2,3,4,5,6,7,8,9,10,11,12,13,14,15},{16,17,18,19,20,21,22,23,24,25,..., dimensions={0} | all-to-all | bytes 262144 | tf_op jit(solution)/shard_map/all_to_all | solution.py:287
  65.5 0.1 shard_map.109
  65.6 1.9 %collective-permute-start.3 = (bf16[48,384]{1,0:T(8,128)(2,1)S(1)}, bf16[48,384]{1,0:T(8,128)(2,1)S(1)}, u32[]{:S(2)}, u32[]{:S(2)}) collective-permute-start(bf16[48,384]{1,0:T(8,128)(2,1)S(1)} %get-tuple-element.24), channel_id=1, source_target_pairs={{0,496},{4,500},{8,504},{12,508},{16,0},{20,4},{24,8},{28,12},{32,... | collective-permute-start | bytes 110600 | tf_op jit(solution)/shard_map/ppermute | solution.py:270
  67.5 4.8 %collective-permute-start.2 = (bf16[48,384]{1,0:T(8,128)(2,1)S(1)}, bf16[48,384]{1,0:T(8,128)(2,1)S(1)}, u32[]{:S(2)}, u32[]{:S(2)}) collective-permute-start(bf16[48,384]{1,0:T(8,128)(2,1)S(1)} %get-tuple-element.23.middle), channel_id=1, source_target_pairs={{0,16},{4,20},{8,24},{12,28},{16,32},{20,36},{24,40},{28,44},{32,4... | collective-permute-start | bytes 110600 | tf_op jit(solution)/shard_map/ppermute | solution.py:270
  72.3 0.0 collective-permute-done.3.right
  72.3 5.4 %collective-permute-done.2.left = bf16[48,384]{1,0:T(8,128)(2,1)S(1)} collective-permute-done((bf16[48,384]{1,0:T(8,128)(2,1)S(1)}, bf16[48,384]{1,0:T(8,128)(2,1)S(1)}, u32[]{:S(2)}, u32[]{:S(2)}) %collective-permute-start.2) | collective-permute-done | bytes 36896 | tf_op jit(solution)/shard_map/ppermute | solution.py:270
  77.8 1.0 %shard_map.110 = f32[4,8,128]{2,1,0:T(8,128)S(1)} custom-call(s32[1,8]{1,0:T(1,128)S(1)} %bitcast.18, s32[1,32]{1,0:T(1,128)S(1)} %bitcast.23, s32[1,32]{1,0:T(1,128)S(1)} %bitcast.27, s32[1,32]{1,0:T(1,128)S(1)} %bitcast.31, bf16[2560,320]{1,0:T(8,128)(2,1)S(1)} %bitcast.10, bf16[48,384]{1,0:T(8,128)(2,1)S(1)} %collective-permute-done.2.left, ...), custom_call_target="tpu_custom_call" | custom-call | tf_op jit(solution)/shard_map/pallas_call | solution.py:259
  78.8 7.9 %all_to_all.29.gathered = f32[4,8,128]{2,1,0:T(8,128)S(1)} all-to-all(f32[4,8,128]{2,1,0:T(8,128)S(1)} %shard_map.110), channel_id=1, replica_groups=mesh['dom'=128,'blk'=4] {'blk'}, dimensions={0} | all-to-all | bytes 32768 | tf_op jit(solution)/shard_map/all_to_all | solution.py:286
  86.7 0.9 %shard_map.111 = (f32[8,80]{1,0:T(8,128)}, f32[1,8]{1,0:T(1,128)}) custom-call(s32[1,8]{1,0:T(1,128)S(1)} %bitcast.19, f32[8,80]{1,0:T(8,128)S(1)} %copy-done.2, bf16[640,320]{1,0:T(8,128)(2,1)S(1)} %bitcast.13, f32[8,80]{1,0:T(8,128)S(1)} %get-tuple-element.15.base, f32[8,512]{1,0:T(8,128)S(1)} %get-tuple-element.21.weight, ...), custom_call_target="tpu_custom_call" | custom-call | tf_op jit(solution)/shard_map/pallas_call | solution.py:259
Async XLA Ops:
  0.6 45.5 %copy-start.3 = (s32[8]{0:T(128)S(1)}, s32[8]{0:T(128)}, u32[]{:S(2)}) copy-start(s32[8]{0:T(128)} %param.9) | copy-start | bytes 100
  0.6 45.5 %copy-start = (bf16[32,80,320]{2,1,0:T(8,128)(2,1)S(1)}, bf16[32,80,320]{2,1,0:T(8,128)(2,1)}, u32[]{:S(2)}) copy-start(bf16[32,80,320]{2,1,0:T(8,128)(2,1)} %param.13) | copy-start | bytes 4915204
  0.7 45.5 %copy-start.6 = (s32[32]{0:T(128)S(1)}, s32[32]{0:T(128)}, u32[]{:S(2)}) copy-start(s32[32]{0:T(128)} %param.12) | copy-start | bytes 388
  0.7 45.5 %copy-start.5 = (s32[32]{0:T(128)S(1)}, s32[32]{0:T(128)}, u32[]{:S(2)}) copy-start(s32[32]{0:T(128)} %param.11) | copy-start | bytes 388
  0.7 45.5 %copy-start.4 = (s32[32]{0:T(128)S(1)}, s32[32]{0:T(128)}, u32[]{:S(2)}) copy-start(s32[32]{0:T(128)} %param.10) | copy-start | bytes 388
  13.7 41.7 %copy-start.1 = (bf16[8,80,320]{2,1,0:T(8,128)(2,1)S(1)}, bf16[8,80,320]{2,1,0:T(8,128)(2,1)}, u32[]{:S(2)}) copy-start(bf16[8,80,320]{2,1,0:T(8,128)(2,1)} %param.15) | copy-start | bytes 1228804
  13.7 41.7 %copy-start.2 = (f32[8,80]{1,0:T(8,128)S(1)}, f32[8,80]{1,0:T(8,128)}, u32[]{:S(2)}) copy-start(f32[8,80]{1,0:T(8,128)} %inv_diag.3) | copy-start | bytes 7684
  25.2 12.8 %collective-permute-start.1 = (bf16[48,384]{1,0:T(8,128)(2,1)S(1)}, bf16[48,384]{1,0:T(8,128)(2,1)S(1)}, u32[]{:S(2)}, u32[]{:S(2)}) collective-permute-start(bf16[48,384]{1,0:T(8,128)(2,1)S(1)} %get-tuple-element.18), channel_id=1, source_target_pairs={{0,496},{4,500},{8,504},{12,508},{16,0},{20,4},{24,8},{28,12},{32,... | collective-permute-start | bytes 110600 | tf_op jit(solution)/shard_map/ppermute | solution.py:270
  36.1 10.1 %collective-permute-start = (bf16[48,384]{1,0:T(8,128)(2,1)S(1)}, bf16[48,384]{1,0:T(8,128)(2,1)S(1)}, u32[]{:S(2)}, u32[]{:S(2)}) collective-permute-start(bf16[48,384]{1,0:T(8,128)(2,1)S(1)} %get-tuple-element.17.middle), channel_id=1, source_target_pairs={{0,16},{4,20},{8,24},{12,28},{16,32},{20,36},{24,40},{28,44},{32,4... | collective-permute-start | bytes 110600 | tf_op jit(solution)/shard_map/ppermute | solution.py:270
  65.6 6.8 %collective-permute-start.3 = (bf16[48,384]{1,0:T(8,128)(2,1)S(1)}, bf16[48,384]{1,0:T(8,128)(2,1)S(1)}, u32[]{:S(2)}, u32[]{:S(2)}) collective-permute-start(bf16[48,384]{1,0:T(8,128)(2,1)S(1)} %get-tuple-element.24), channel_id=1, source_target_pairs={{0,496},{4,500},{8,504},{12,508},{16,0},{20,4},{24,8},{28,12},{32,... | collective-permute-start | bytes 110600 | tf_op jit(solution)/shard_map/ppermute | solution.py:270
  67.5 10.3 %collective-permute-start.2 = (bf16[48,384]{1,0:T(8,128)(2,1)S(1)}, bf16[48,384]{1,0:T(8,128)(2,1)S(1)}, u32[]{:S(2)}, u32[]{:S(2)}) collective-permute-start(bf16[48,384]{1,0:T(8,128)(2,1)S(1)} %get-tuple-element.23.middle), channel_id=1, source_target_pairs={{0,16},{4,20},{8,24},{12,28},{16,32},{20,36},{24,40},{28,44},{32,4... | collective-permute-start | bytes 110600 | tf_op jit(solution)/shard_map/ppermute | solution.py:270

commit v3 on v2

--- a/solution.py
+++ b/solution.py
@@ -1,5 +1,3 @@
-import functools
-
 import jax
 import jax.numpy as jnp
 from jax import lax
@@ -7,12 +5,14 @@
 from jax.experimental.pallas import tpu as pltpu
 from jax.sharding import PartitionSpec as P
 
+
 MODES = 64
 SWEEPS = 2
 NEIGH = 8
 HALF = NEIGH // 2
 F32 = jnp.float32
 BF16 = jnp.bfloat16
+COST = 20_000_000_000
 NT = (((1,), (1,)), ((), ()))
 
 
@@ -69,9 +69,16 @@
     return dot(wide, pick)[0:1]
 
 
-def targets(side, peer, slot, elements):
-    offset = jnp.where(side > HALF, HALF - side, side)
-    return ((HALF + slot + offset) * elements + peer).astype(F32)
+def place():
+    dom = lax.axis_index("dom")
+    return dom % HALF, 2 * ((dom // HALF) % 2) - 1
+
+
+def targets(side, peer, elements):
+    slot, sign = place()
+    spot = slot + jnp.where(side > HALF, HALF - side, side)
+    group = jnp.where(spot >= HALF, 1, jnp.where(spot < 0, -1, 0))
+    return (((1 + sign * group) * HALF + spot - HALF * group) * elements + peer).astype(F32)
 
 
 def fetch(pairs, arrived):
@@ -90,7 +97,7 @@
     return total
 
 
-def put_transposed(out, coupling, state, owner, target, elements, quarter, faces, ready=None):
+def put_transposed(out, coupling, state, owner, target, elements, quarter, faces):
     face, fold = lane_tables(quarter, faces)
     own_lane = per_lane(face, owner.astype(F32))
     target_lane = per_lane(face, target)
@@ -101,8 +108,6 @@
     count = 3 * HALF * elements
     places = lax.broadcasted_iota(jnp.int32, (count, lanes), 0).astype(F32)
     chosen = jnp.where(places == target_lane, spread, 0.0).astype(BF16)
-    if ready is not None:
-        ready.wait()
     transposed = dot(chosen, coupling[...])
     for q in range(4):
         part = transposed[:, q * quarter : (q + 1) * quarter].astype(BF16)
@@ -116,27 +121,23 @@
 def first_kernel(degree_in, source_in, out, degree, source, arrived):
     for copy in fetch([(degree_in, degree), (source_in, source)], arrived):
         copy.wait()
-    elements, quarter = source.shape
+    _, quarter = source.shape
     first = lax.axis_index("blk") * quarter
     half = (source[...] * mask_of(degree[...], quarter, first)).astype(BF16).astype(F32)
     for q in range(4):
         out[q, :, 0:quarter] = half
 
 
-def base_kernel(*refs):
-    far, gathered, (out, base_out, weight_out), near = refs[0:9], refs[9], refs[10:13], refs[13:22]
-    wide, arrived = refs[22:24]
-    degree, owner, side, peer, inv_diag, source, residual, inv_off, coupling = near
-    copies = fetch(list(zip(far, near)), arrived)
+def base_kernel(
+    degree, owner, side, peer, inv_diag, source, residual, inv_off, coupling, gathered,
+    out, base_out, weight_out, wide,
+):
     elements, quarter = source.shape
     faces = owner.shape[1]
     width = 4 * quarter
-    slot = lax.axis_index("dom") % HALF
     blk = lax.axis_index("blk")
     for q in range(4):
         wide[:, q * quarter : (q + 1) * quarter] = gathered[q, :, 0:quarter]
-    for copy in copies[:-1]:
-        copy.wait()
     mask = mask_of(degree[...], quarter, blk * quarter)
     own = (source[...] * mask).astype(BF16).astype(F32)
     product = block_apply(inv_off, wide[...].astype(BF16), elements, quarter)
@@ -159,44 +160,41 @@
     weight_out[:, 384:512] = jnp.broadcast_to(
         jnp.sum(weighted * base, axis=1, keepdims=True), (elements, 128)
     )
-    target = targets(side[...], peer[...], slot, elements)
-    put_transposed(
-        out, coupling, state, owner[...], target, elements, quarter, faces, copies[-1]
-    )
-
-
-def merge_kernel(message, ahead, behind, kept):
+    target = targets(side[...], peer[...], elements)
+    put_transposed(out, coupling, state, owner[...], target, elements, quarter, faces)
+
+
+def merge_kernel(message, first, second, kept):
     elements, quarter = kept.shape
     total = message[0, 0 : 3 * elements, 0:quarter].astype(F32)
     for i in range(1, 16):
         total = total + message[i, 0 : 3 * elements, 0:quarter].astype(F32)
     rows = HALF * elements
-    behind[rows:, 0:quarter] = two_parts(total[0:elements])
+    first[rows:, 0:quarter] = two_parts(total[0:elements])
     kept[...] = total[elements : 2 * elements]
-    ahead[rows:, 0:quarter] = two_parts(total[2 * elements : 3 * elements])
+    second[rows:, 0:quarter] = two_parts(total[2 * elements : 3 * elements])
     for q in range(4):
         state = jnp.concatenate(
             [message[r * 4 + q, 3 * elements :, 0:quarter].astype(F32) for r in range(HALF)], axis=0
         ).astype(BF16)
-        ahead[0:rows, q * quarter : (q + 1) * quarter] = state
-        behind[0:rows, q * quarter : (q + 1) * quarter] = state
-
-
-def couple_kernel(degree, owner, side, peer, coupling, left, middle, right, kept, *rest):
+        second[0:rows, q * quarter : (q + 1) * quarter] = state
+        first[0:rows, q * quarter : (q + 1) * quarter] = state
+
+
+def couple_kernel(degree, owner, side, peer, coupling, before, middle, after, kept, *rest):
     out = rest[-1]
     elements, quarter = kept.shape
     faces = owner.shape[1]
     width = 4 * quarter
     lanes = quarter * faces
-    slot = lax.axis_index("dom") % HALF
     mask = mask_of(degree[...], quarter, lax.axis_index("blk") * quarter)
     rows = HALF * elements
     states = jnp.concatenate(
-        [left[0:rows, 0:width], middle[0:rows, 0:width], right[0:rows, 0:width]], axis=0
+        [before[0:rows, 0:width], middle[0:rows, 0:width], after[0:rows, 0:width]], axis=0
     )
     face, fold = lane_tables(quarter, faces)
     own_lane = per_lane(face, owner[...].astype(F32))
-    target_lane = per_lane(face, targets(side[...], peer[...], slot, elements))
+    target_lane = per_lane(face, targets(side[...], peer[...], elements))
     products = dot_nt(states, coupling[...])
     places = lax.broadcasted_iota(jnp.int32, (3 * rows, lanes), 0).astype(F32)
     terms = jnp.sum(jnp.where(places == target_lane, products, 0.0), axis=0, keepdims=True)
@@ -205,7 +203,7 @@
     folded = dot_nt(two_parts(spread), fold)
     coupled = folded[0:elements] + folded[elements : 2 * elements]
     coupled = coupled + kept[...]
-    for sent in (left, right):
+    for sent in (before, after):
         pair = sent[rows:, 0:quarter].astype(F32)
         coupled = coupled + (pair[0:elements] + pair[elements : 2 * elements])
     coupled = (coupled * mask).astype(BF16).astype(F32)
@@ -231,12 +229,11 @@
 ):
     elements, quarter = base.shape
     faces = owner.shape[1]
-    slot = lax.axis_index("dom") % HALF
     blk = lax.axis_index("blk")
     mask = mask_of(degree[...], quarter, blk * quarter)
     adjoint = update(inv_diag, inv_off, base, gathered, mask, blk, wide)
     state = adjoint.astype(BF16).astype(F32)
-    target = targets(side[...], peer[...], slot, elements)
+    target = targets(side[...], peer[...], elements)
     put_transposed(out, coupling, state, owner[...], target, elements, quarter, faces)
     weight_out[...] = (gathered[0, :, 128:640] + gathered[1, :, 128:640]) + (
         gathered[2, :, 128:640] + gathered[3, :, 128:640]
@@ -253,7 +250,7 @@
     indicator[...] = as_row(weight[:, 384:385] - dual, elements)
 
 
-def call(body, shapes, *args, scratch=(), far=0):
+def call(body, shapes, *args, scratch=(), far=0, cost=None):
     space = lambda i: pl.BlockSpec(memory_space=pltpu.HBM if i < far else pltpu.VMEM)
     near = [pltpu.VMEM(x.shape, x.dtype) for x in args[:far]]
     return pl.pallas_call(
@@ -261,13 +258,15 @@
         out_shape=shapes,
         in_specs=[space(i) for i in range(len(args))],
         scratch_shapes=[*near, *scratch, *([pltpu.SemaphoreType.DMA((far,))] if far else [])],
+        cost_estimate=cost,
         compiler_params=pltpu.CompilerParams(vmem_limit_bytes=24 << 20),
     )(*[pltpu.with_memory_space_constraint(x, pltpu.HBM) for x in args[:far]], *args[far:])
 
 
-def hop(block, distance):
+def swap(block, odd):
     count = lax.axis_size("dom")
-    return lax.ppermute(block, "dom", [(i, (i + distance) % count) for i in range(count)])
+    step = lambda i: HALF if (i // HALF) % 2 == odd else -HALF
+    return lax.ppermute(block, "dom", [(i, (i + step(i)) % count) for i in range(count)])
 
 
 def local(degree, face_elem, face_side, face_peer, coupling, inv_diag, inv_off, source, residual):
@@ -286,26 +285,26 @@
     across = lambda x: lax.all_to_all(x, "blk", 0, 0)
     group = lambda x: lax.all_to_all(x, ("dom", "blk"), 0, 0, axis_index_groups=groups)
 
-    gathered = across(call(first_kernel, shape(4, elements, 128), degree, source, far=2))
+    gathered = across(call(first_kernel, shape(4, elements, 128), degree, source, far=2, cost=pl.CostEstimate(flops=COST, transcendentals=0, bytes_accessed=1 << 12)))
     message_shape = shape(16, 4 * elements, 128, kind=BF16)
     message, base, weight = call(
         base_kernel,
         (message_shape, shape(elements, quarter), shape(elements, 512)),
         degree, *faces_of, inv_diag, source, residual, inv_off, coupling, gathered,
-        scratch=wide, far=9,
+        scratch=wide,
     )
     for sweep in range(SWEEPS):
         hop_shape = shape(HALF * elements + 2 * elements, 384, kind=BF16)
-        ahead, behind, kept = call(
+        first, second, kept = call(
             merge_kernel, (hop_shape, hop_shape, shape(elements, quarter)), group(message)
         )
-        left = hop(ahead, HALF)
-        right = hop(behind, -HALF)
+        before = swap(first, 0)
+        after = swap(second, 1)
         extra = (weight,) if sweep == 0 else ()
         coupled = call(
             couple_kernel,
             shape(4, elements, 640 if sweep == 0 else 128),
-            degree, *faces_of, coupling, left, ahead, right, kept, *extra,
+            degree, *faces_of, coupling, before, first, after, kept, *extra,
         )
         gathered = across(coupled)
         if sweep == 0:
@@ -337,4 +336,6 @@
         P("dom", "blk"),
     )
     out_specs = (P("dom", "blk"), P("dom"))
-    return jax.shard_map(local, mesh=mesh, in_specs=in_specs, out_specs=out_specs, check_vma=False)
+    return jax.shard_map(
+        local, mesh=mesh, in_specs=in_specs, out_specs=out_specs, check_vma=False
+    )

time: 88.1 us -> 82.2 us (0.933)
  the two profiles are of different devices: /device:TPU:32 before, /device:TPU:8 now
where the time goes in v3:
time: 82.2 us; the launch traced here: 81.8 us
  blocking collectives  46.2 us (56%)
  starting transfers between devices  18.1 us (22%)
  waiting for transfers between devices  10.4 us (13%)
  Pallas kernels  6.14 us (7%)
  between operations  0.83 us (1%)
    all_to_all x3, blocking collectives, local(): across = lambda x: lax.all_to_all(x, 'blk', 0, 0)  28.3 us
    ppermute x4, starting transfers between devices, swap(): lax.ppermute(block, 'dom', [(i, (i + step(i)) % count) for i in range(cou...  18.1 us
    all_to_all x2, blocking collectives, local(): lax.all_to_all(x, ('dom', 'blk'), 0, 0, axis_index_groups=groups)  17.9 us
    ppermute x4, waiting for transfers between devices, swap(): lax.ppermute(block, 'dom', [(i, (i + step(i)) % count) for i in range(cou...  10.4 us
    pallas_call x8, Pallas kernels, call(): pl.pallas_call(body, out_shape=shapes, in_specs=[space(i) for i in range(...  6.14 us
  transfers between devices with their start and end apart: 4, of which 3 were waited for; matrix products, arithmetic and copies ran while one was open for 0% of the time, Pallas kernels for 0%

profile of v3, /device:TPU:8, one launch (start us, length us, event | category | flops | bytes accessed | tf_op | source)
XLA Modules:
  0.0 81.8 jit_solution(15027692578362359392)
XLA Ops:
  0.6 0.0 copy-start
  0.6 0.0 copy-start.1
  0.7 0.0 copy-start.2
  0.7 0.0 copy-start.3
  0.7 0.0 copy-start.4
  0.7 0.0 copy-start.5
  0.7 0.0 copy-start.6
  0.7 0.0 copy-start.7
  0.7 0.0 copy-start.8
  0.7 0.9 %shard_map.104 = f32[4,8,128]{2,1,0:T(8,128)S(1)} custom-call(s32[1,8]{1,0:T(1,128)} %bitcast.14, f32[8,80]{1,0:T(8,128)} %source.1), custom_call_target="tpu_custom_call" | custom-call | flops 20000000000 | bytes 4096 | tf_op jit(solution)/shard_map/pallas_call | solution.py:256
  1.7 12.0 %all_to_all.25.gathered = f32[4,8,128]{2,1,0:T(8,128)S(1)} all-to-all(f32[4,8,128]{2,1,0:T(8,128)S(1)} %shard_map.104), channel_id=1, replica_groups=mesh['dom'=128,'blk'=4] {'blk'}, dimensions={0} | all-to-all | bytes 32768 | tf_op jit(solution)/shard_map/all_to_all | solution.py:285
  13.7 0.0 copy-done
  13.7 0.0 copy-done.1
  13.7 0.0 copy-done.2
  13.7 0.0 copy-done.3
  13.7 0.0 copy-done.4
  13.8 0.0 copy-done.5
  13.8 0.0 copy-done.6
  13.8 0.0 copy-done.7
  13.8 0.0 copy-done.8
  13.8 1.0 %shard_map.105 = (bf16[16,32,128]{2,1,0:T(8,128)(2,1)S(1)}, f32[8,80]{1,0:T(8,128)S(1)}, f32[8,512]{1,0:T(8,128)S(1)}) custom-call(s32[1,8]{1,0:T(1,128)S(1)} %bitcast.15, s32[1,32]{1,0:T(1,128)S(1)} %bitcast.20, s32[1,32]{1,0:T(1,128)S(1)} %bitcast.24, s32[1,32]{1,0:T(1,128)S(1)} %bitcast.28, f32[8,80]{1,0:T(8,128)S(1)} %copy-done.2, ...), custom_call_target="tpu_custom_call" | custom-call | tf_op jit(solution)/shard_map/pallas_call | solution.py:256
  14.8 8.9 %all_to_all.26.message = bf16[16,32,128]{2,1,0:T(8,128)(2,1)S(1)} all-to-all(bf16[16,32,128]{2,1,0:T(8,128)(2,1)S(1)} %get-tuple-element.16), channel_id=1, replica_groups={{0,1,2,3,4,5,6,7,8,9,10,11,12,13,14,15},{16,17,18,19,20,21,22,23,24,25,..., dimensions={0} | all-to-all | bytes 262144 | tf_op jit(solution)/shard_map/all_to_all | solution.py:286
  23.8 0.1 shard_map.106
  23.9 10.8 %collective-permute-start.1 = (bf16[48,384]{1,0:T(8,128)(2,1)S(1)}, bf16[48,384]{1,0:T(8,128)(2,1)S(1)}, u32[]{:S(2)}, u32[]{:S(2)}) collective-permute-start(bf16[48,384]{1,0:T(8,128)(2,1)S(1)} %get-tuple-element.18), channel_id=1, source_target_pairs={{0,496},{4,500},{8,504},{12,508},{16,32},{20,36},{24,40},{28,44},{... | collective-permute-start | bytes 110600 | tf_op jit(solution)/shard_map/ppermute | solution.py:269
  34.7 1.9 %collective-permute-start = (bf16[48,384]{1,0:T(8,128)(2,1)S(1)}, bf16[48,384]{1,0:T(8,128)(2,1)S(1)}, u32[]{:S(2)}, u32[]{:S(2)}) collective-permute-start(bf16[48,384]{1,0:T(8,128)(2,1)S(1)} %get-tuple-element.17.middle), channel_id=1, source_target_pairs={{0,16},{4,20},{8,24},{12,28},{16,0},{20,4},{24,8},{28,12},{32,48},... | collective-permute-start | bytes 110600 | tf_op jit(solution)/shard_map/ppermute | solution.py:269
  36.6 0.0 collective-permute-done.1.after
  36.6 5.2 %collective-permute-done.before = bf16[48,384]{1,0:T(8,128)(2,1)S(1)} collective-permute-done((bf16[48,384]{1,0:T(8,128)(2,1)S(1)}, bf16[48,384]{1,0:T(8,128)(2,1)S(1)}, u32[]{:S(2)}, u32[]{:S(2)}) %collective-permute-start) | collective-permute-done | bytes 36896 | tf_op jit(solution)/shard_map/ppermute | solution.py:269
  41.8 1.0 %shard_map.107 = f32[4,8,640]{2,1,0:T(8,128)S(1)} custom-call(s32[1,8]{1,0:T(1,128)S(1)} %bitcast.16, s32[1,32]{1,0:T(1,128)S(1)} %bitcast.21, s32[1,32]{1,0:T(1,128)S(1)} %bitcast.25, s32[1,32]{1,0:T(1,128)S(1)} %bitcast.29, bf16[2560,320]{1,0:T(8,128)(2,1)S(1)} %bitcast.8, bf16[48,384]{1,0:T(8,128)(2,1)S(1)} %collective-permute-done.before, ...), custom_call_target="tpu_custom_call" | custom-call | tf_op jit(solution)/shard_map/pallas_call | solution.py:256
  42.9 8.3 %all_to_all.27.gathered = f32[4,8,640]{2,1,0:T(8,128)S(1)} all-to-all(f32[4,8,640]{2,1,0:T(8,128)S(1)} %shard_map.107), channel_id=1, replica_groups=mesh['dom'=128,'blk'=4] {'blk'}, dimensions={0} | all-to-all | bytes 163840 | tf_op jit(solution)/shard_map/all_to_all | solution.py:285
  51.2 1.0 %shard_map.108 = (bf16[16,32,128]{2,1,0:T(8,128)(2,1)S(1)}, f32[8,512]{1,0:T(8,128)S(1)}) custom-call(s32[1,8]{1,0:T(1,128)S(1)} %bitcast.17, s32[1,32]{1,0:T(1,128)S(1)} %bitcast.22, s32[1,32]{1,0:T(1,128)S(1)} %bitcast.26, s32[1,32]{1,0:T(1,128)S(1)} %bitcast.30, bf16[2560,320]{1,0:T(8,128)(2,1)S(1)} %bitcast.9, f32[8,80]{1,0:T(8,128)S(1)} %copy-done.2, ...), custom_call_target="tpu_custom_call" | custom-call | tf_op jit(solution)/shard_map/pallas_call | solution.py:256
  52.2 8.9 %all_to_all.28.message = bf16[16,32,128]{2,1,0:T(8,128)(2,1)S(1)} all-to-all(bf16[16,32,128]{2,1,0:T(8,128)(2,1)S(1)} %get-tuple-element.22), channel_id=1, replica_groups={{0,1,2,3,4,5,6,7,8,9,10,11,12,13,14,15},{16,17,18,19,20,21,22,23,24,25,..., dimensions={0} | all-to-all | bytes 262144 | tf_op jit(solution)/shard_map/all_to_all | solution.py:286
  61.2 0.1 shard_map.109
  61.2 3.4 %collective-permute-start.3 = (bf16[48,384]{1,0:T(8,128)(2,1)S(1)}, bf16[48,384]{1,0:T(8,128)(2,1)S(1)}, u32[]{:S(2)}, u32[]{:S(2)}) collective-permute-start(bf16[48,384]{1,0:T(8,128)(2,1)S(1)} %get-tuple-element.24), channel_id=1, source_target_pairs={{0,496},{4,500},{8,504},{12,508},{16,32},{20,36},{24,40},{28,44},{... | collective-permute-start | bytes 110600 | tf_op jit(solution)/shard_map/ppermute | solution.py:269
  64.7 1.9 %collective-permute-start.2 = (bf16[48,384]{1,0:T(8,128)(2,1)S(1)}, bf16[48,384]{1,0:T(8,128)(2,1)S(1)}, u32[]{:S(2)}, u32[]{:S(2)}) collective-permute-start(bf16[48,384]{1,0:T(8,128)(2,1)S(1)} %get-tuple-element.23.middle), channel_id=1, source_target_pairs={{0,16},{4,20},{8,24},{12,28},{16,0},{20,4},{24,8},{28,12},{32,48},... | collective-permute-start | bytes 110600 | tf_op jit(solution)/shard_map/ppermute | solution.py:269
  66.6 4.7 %collective-permute-done.3.after = bf16[48,384]{1,0:T(8,128)(2,1)S(1)} collective-permute-done((bf16[48,384]{1,0:T(8,128)(2,1)S(1)}, bf16[48,384]{1,0:T(8,128)(2,1)S(1)}, u32[]{:S(2)}, u32[]{:S(2)}) %collective-permute-start.3) | collective-permute-done | bytes 36896 | tf_op jit(solution)/shard_map/ppermute | solution.py:269
  71.3 0.5 collective-permute-done.2.before
  71.8 1.0 %shard_map.110 = f32[4,8,128]{2,1,0:T(8,128)S(1)} custom-call(s32[1,8]{1,0:T(1,128)S(1)} %bitcast.18, s32[1,32]{1,0:T(1,128)S(1)} %bitcast.23, s32[1,32]{1,0:T(1,128)S(1)} %bitcast.27, s32[1,32]{1,0:T(1,128)S(1)} %bitcast.31, bf16[2560,320]{1,0:T(8,128)(2,1)S(1)} %bitcast.10, bf16[48,384]{1,0:T(8,128)(2,1)S(1)} %collective-permute-done.2.before, ...), custom_call_target="tpu_custom_call" | custom-call | tf_op jit(solution)/shard_map/pallas_call | solution.py:256
  72.8 8.0 %all_to_all.29.gathered = f32[4,8,128]{2,1,0:T(8,128)S(1)} all-to-all(f32[4,8,128]{2,1,0:T(8,128)S(1)} %shard_map.110), channel_id=1, replica_groups=mesh['dom'=128,'blk'=4] {'blk'}, dimensions={0} | all-to-all | bytes 32768 | tf_op jit(solution)/shard_map/all_to_all | solution.py:285
  80.8 0.9 %shard_map.111 = (f32[8,80]{1,0:T(8,128)}, f32[1,8]{1,0:T(1,128)}) custom-call(s32[1,8]{1,0:T(1,128)S(1)} %bitcast.19, f32[8,80]{1,0:T(8,128)S(1)} %copy-done.2, bf16[640,320]{1,0:T(8,128)(2,1)S(1)} %bitcast.13, f32[8,80]{1,0:T(8,128)S(1)} %get-tuple-element.15.base, f32[8,512]{1,0:T(8,128)S(1)} %get-tuple-element.21.weight, ...), custom_call_target="tpu_custom_call" | custom-call | tf_op jit(solution)/shard_map/pallas_call | solution.py:256
Async XLA Ops:
  0.6 13.1 %copy-start = (bf16[32,80,320]{2,1,0:T(8,128)(2,1)S(1)}, bf16[32,80,320]{2,1,0:T(8,128)(2,1)}, u32[]{:S(2)}) copy-start(bf16[32,80,320]{2,1,0:T(8,128)(2,1)} %param.13) | copy-start | bytes 4915204
  0.6 13.1 %copy-start.1 = (bf16[8,80,320]{2,1,0:T(8,128)(2,1)S(1)}, bf16[8,80,320]{2,1,0:T(8,128)(2,1)}, u32[]{:S(2)}) copy-start(bf16[8,80,320]{2,1,0:T(8,128)(2,1)} %param.15) | copy-start | bytes 1228804
  0.7 13.1 %copy-start.2 = (f32[8,80]{1,0:T(8,128)S(1)}, f32[8,80]{1,0:T(8,128)}, u32[]{:S(2)}) copy-start(f32[8,80]{1,0:T(8,128)} %inv_diag.5) | copy-start | bytes 7684
  0.7 13.1 %copy-start.3 = (s32[8]{0:T(128)S(1)}, s32[8]{0:T(128)}, u32[]{:S(2)}) copy-start(s32[8]{0:T(128)} %param.9) | copy-start | bytes 100
  0.7 13.1 %copy-start.4 = (s32[32]{0:T(128)S(1)}, s32[32]{0:T(128)}, u32[]{:S(2)}) copy-start(s32[32]{0:T(128)} %param.10) | copy-start | bytes 388
  0.7 13.1 %copy-start.5 = (s32[32]{0:T(128)S(1)}, s32[32]{0:T(128)}, u32[]{:S(2)}) copy-start(s32[32]{0:T(128)} %param.11) | copy-start | bytes 388
  0.7 13.1 %copy-start.6 = (s32[32]{0:T(128)S(1)}, s32[32]{0:T(128)}, u32[]{:S(2)}) copy-start(s32[32]{0:T(128)} %param.12) | copy-start | bytes 388
  0.7 13.1 %copy-start.7 = (f32[8,80]{1,0:T(8,128)S(1)}, f32[8,80]{1,0:T(8,128)}, u32[]{:S(2)}) copy-start(f32[8,80]{1,0:T(8,128)} %source.1) | copy-start | bytes 7684
  0.7 13.1 %copy-start.8 = (f32[8,80]{1,0:T(8,128)S(1)}, f32[8,80]{1,0:T(8,128)}, u32[]{:S(2)}) copy-start(f32[8,80]{1,0:T(8,128)} %residual.1) | copy-start | bytes 7684
  23.9 12.8 %collective-permute-start.1 = (bf16[48,384]{1,0:T(8,128)(2,1)S(1)}, bf16[48,384]{1,0:T(8,128)(2,1)S(1)}, u32[]{:S(2)}, u32[]{:S(2)}) collective-permute-start(bf16[48,384]{1,0:T(8,128)(2,1)S(1)} %get-tuple-element.18), channel_id=1, source_target_pairs={{0,496},{4,500},{8,504},{12,508},{16,32},{20,36},{24,40},{28,44},{... | collective-permute-start | bytes 110600 | tf_op jit(solution)/shard_map/ppermute | solution.py:269
  34.7 7.1 %collective-permute-start = (bf16[48,384]{1,0:T(8,128)(2,1)S(1)}, bf16[48,384]{1,0:T(8,128)(2,1)S(1)}, u32[]{:S(2)}, u32[]{:S(2)}) collective-permute-start(bf16[48,384]{1,0:T(8,128)(2,1)S(1)} %get-tuple-element.17.middle), channel_id=1, source_target_pairs={{0,16},{4,20},{8,24},{12,28},{16,0},{20,4},{24,8},{28,12},{32,48},... | collective-permute-start | bytes 110600 | tf_op jit(solution)/shard_map/ppermute | solution.py:269
  61.2 10.1 %collective-permute-start.3 = (bf16[48,384]{1,0:T(8,128)(2,1)S(1)}, bf16[48,384]{1,0:T(8,128)(2,1)S(1)}, u32[]{:S(2)}, u32[]{:S(2)}) collective-permute-start(bf16[48,384]{1,0:T(8,128)(2,1)S(1)} %get-tuple-element.24), channel_id=1, source_target_pairs={{0,496},{4,500},{8,504},{12,508},{16,32},{20,36},{24,40},{28,44},{... | collective-permute-start | bytes 110600 | tf_op jit(solution)/shard_map/ppermute | solution.py:269
  64.7 7.1 %collective-permute-start.2 = (bf16[48,384]{1,0:T(8,128)(2,1)S(1)}, bf16[48,384]{1,0:T(8,128)(2,1)S(1)}, u32[]{:S(2)}, u32[]{:S(2)}) collective-permute-start(bf16[48,384]{1,0:T(8,128)(2,1)S(1)} %get-tuple-element.23.middle), channel_id=1, source_target_pairs={{0,16},{4,20},{8,24},{12,28},{16,0},{20,4},{24,8},{28,12},{32,48},... | collective-permute-start | bytes 110600 | tf_op jit(solution)/shard_map/ppermute | solution.py:269

commit v4 on v3

--- a/solution.py
+++ b/solution.py
@@ -62,11 +62,9 @@
 
 def per_lane(face, values):
     faces = values.shape[1]
-    lanes = face.shape[1]
-    row = lax.broadcasted_iota(jnp.int32, (faces, lanes), 0).astype(F32)
+    row = lax.broadcasted_iota(jnp.int32, (faces, face.shape[1]), 0).astype(F32)
     pick = jnp.where(row == face, 1.0, 0.0).astype(BF16)
-    wide = jnp.broadcast_to(values, (8, faces)).astype(BF16)
-    return dot(wide, pick)[0:1]
+    return dot(values.astype(BF16), pick)
 
 
 def place():
@@ -97,25 +95,22 @@
     return total
 
 
-def put_transposed(out, coupling, state, owner, target, elements, quarter, faces):
-    face, fold = lane_tables(quarter, faces)
-    own_lane = per_lane(face, owner.astype(F32))
-    target_lane = per_lane(face, target)
+def put_transposed(out, coupling, state, tables, fold, elements, quarter, faces):
     lanes = quarter * faces
     repeated = dot(state.astype(BF16), fold)
     rows = lax.broadcasted_iota(jnp.int32, (elements, lanes), 0).astype(F32)
-    spread = jnp.sum(jnp.where(rows == own_lane, repeated, 0.0), axis=0, keepdims=True)
+    spread = jnp.sum(jnp.where(rows == tables[0:1], repeated, 0.0), axis=0, keepdims=True)
     count = 3 * HALF * elements
     places = lax.broadcasted_iota(jnp.int32, (count, lanes), 0).astype(F32)
-    chosen = jnp.where(places == target_lane, spread, 0.0).astype(BF16)
+    chosen = jnp.where(places == tables[1:2], spread, 0.0).astype(BF16)
     transposed = dot(chosen, coupling[...])
     for q in range(4):
-        part = transposed[:, q * quarter : (q + 1) * quarter].astype(BF16)
+        part = transposed[:, q * quarter : (q + 1) * quarter]
         for r in range(HALF):
             for s in range(3):
                 at = (s * HALF + r) * elements
-                out[r * 4 + q, s * elements : (s + 1) * elements, 0:quarter] = part[at : at + elements]
-            out[r * 4 + q, 3 * elements : 4 * elements, 0:quarter] = state.astype(BF16)
+                out[r * 4 + q, :, s * quarter : (s + 1) * quarter] = part[at : at + elements].astype(BF16)
+            out[r * 4 + q, :, 3 * quarter : 4 * quarter] = state.astype(BF16)
 
 
 def first_kernel(degree_in, source_in, out, degree, source, arrived):
@@ -123,27 +118,34 @@
         copy.wait()
     _, quarter = source.shape
     first = lax.axis_index("blk") * quarter
-    half = (source[...] * mask_of(degree[...], quarter, first)).astype(BF16).astype(F32)
+    half = (source[...] * mask_of(degree[...], quarter, first)).astype(BF16)
     for q in range(4):
         out[q, :, 0:quarter] = half
 
 
 def base_kernel(
     degree, owner, side, peer, inv_diag, source, residual, inv_off, coupling, gathered,
-    out, base_out, weight_out, wide,
+    out, base_out, weight_out, tables_out, fold_out, wide,
 ):
     elements, quarter = source.shape
     faces = owner.shape[1]
     width = 4 * quarter
     blk = lax.axis_index("blk")
     for q in range(4):
-        wide[:, q * quarter : (q + 1) * quarter] = gathered[q, :, 0:quarter]
+        wide[:, q * quarter : (q + 1) * quarter] = gathered[q, :, 0:quarter].astype(F32)
     mask = mask_of(degree[...], quarter, blk * quarter)
     own = (source[...] * mask).astype(BF16).astype(F32)
     product = block_apply(inv_off, wide[...].astype(BF16), elements, quarter)
     base = (inv_diag[...] * own + product) * mask
     base_out[...] = base
     state = base.astype(BF16).astype(F32)
+    face, fold = lane_tables(quarter, faces)
+    target = targets(side[...], peer[...], elements)
+    index = lax.broadcasted_iota(jnp.int32, (8, faces), 0)
+    both = jnp.where(index == 0, owner[...].astype(F32), target)
+    tables = per_lane(face, both)
+    tables_out[...] = tables
+    fold_out[...] = fold
     weighted = residual[...] * mask
     parts = two_parts(weighted)
     row = lax.broadcasted_iota(jnp.int32, (elements, width), 0)
@@ -160,53 +162,48 @@
     weight_out[:, 384:512] = jnp.broadcast_to(
         jnp.sum(weighted * base, axis=1, keepdims=True), (elements, 128)
     )
-    target = targets(side[...], peer[...], elements)
-    put_transposed(out, coupling, state, owner[...], target, elements, quarter, faces)
+    put_transposed(out, coupling, state, tables, fold, elements, quarter, faces)
 
 
 def merge_kernel(message, first, second, kept):
     elements, quarter = kept.shape
-    total = message[0, 0 : 3 * elements, 0:quarter].astype(F32)
+    total = message[0].astype(F32)
     for i in range(1, 16):
-        total = total + message[i, 0 : 3 * elements, 0:quarter].astype(F32)
+        total = total + message[i].astype(F32)
     rows = HALF * elements
-    first[rows:, 0:quarter] = two_parts(total[0:elements])
-    kept[...] = total[elements : 2 * elements]
-    second[rows:, 0:quarter] = two_parts(total[2 * elements : 3 * elements])
+    first[rows:, 0:quarter] = two_parts(total[:, 0:quarter])
+    kept[...] = total[:, quarter : 2 * quarter]
+    second[rows:, 0:quarter] = two_parts(total[:, 2 * quarter : 3 * quarter])
     for q in range(4):
         state = jnp.concatenate(
-            [message[r * 4 + q, 3 * elements :, 0:quarter].astype(F32) for r in range(HALF)], axis=0
+            [message[r * 4 + q].astype(F32)[:, 3 * quarter : 4 * quarter] for r in range(HALF)], axis=0
         ).astype(BF16)
+        first[0:rows, q * quarter : (q + 1) * quarter] = state
         second[0:rows, q * quarter : (q + 1) * quarter] = state
-        first[0:rows, q * quarter : (q + 1) * quarter] = state
-
-
-def couple_kernel(degree, owner, side, peer, coupling, before, middle, after, kept, *rest):
+
+
+def couple_kernel(degree, tables, fold, coupling, before, middle, after, kept, *rest):
     out = rest[-1]
     elements, quarter = kept.shape
-    faces = owner.shape[1]
     width = 4 * quarter
-    lanes = quarter * faces
+    lanes = fold.shape[1]
     mask = mask_of(degree[...], quarter, lax.axis_index("blk") * quarter)
     rows = HALF * elements
     states = jnp.concatenate(
         [before[0:rows, 0:width], middle[0:rows, 0:width], after[0:rows, 0:width]], axis=0
     )
-    face, fold = lane_tables(quarter, faces)
-    own_lane = per_lane(face, owner[...].astype(F32))
-    target_lane = per_lane(face, targets(side[...], peer[...], elements))
     products = dot_nt(states, coupling[...])
     places = lax.broadcasted_iota(jnp.int32, (3 * rows, lanes), 0).astype(F32)
-    terms = jnp.sum(jnp.where(places == target_lane, products, 0.0), axis=0, keepdims=True)
+    terms = jnp.sum(jnp.where(places == tables[1:2, :], products, 0.0), axis=0, keepdims=True)
     element = lax.broadcasted_iota(jnp.int32, (elements, lanes), 0).astype(F32)
-    spread = jnp.where(element == own_lane, terms, 0.0)
-    folded = dot_nt(two_parts(spread), fold)
+    spread = jnp.where(element == tables[0:1, :], terms, 0.0)
+    folded = dot_nt(two_parts(spread), fold[...])
     coupled = folded[0:elements] + folded[elements : 2 * elements]
     coupled = coupled + kept[...]
     for sent in (before, after):
         pair = sent[rows:, 0:quarter].astype(F32)
         coupled = coupled + (pair[0:elements] + pair[elements : 2 * elements])
-    coupled = (coupled * mask).astype(BF16).astype(F32)
+    coupled = (coupled * mask).astype(BF16).astype(out.dtype)
     if len(rest) == 2:
         weight = rest[0][...]
         for q in range(4):
@@ -218,23 +215,22 @@
 def update(inv_diag, inv_off, base, gathered, mask, blk, wide):
     elements, quarter = base.shape
     for q in range(4):
-        wide[:, q * quarter : (q + 1) * quarter] = gathered[q, :, 0:quarter]
+        wide[:, q * quarter : (q + 1) * quarter] = gathered[q, :, 0:quarter].astype(F32)
     product = block_apply(inv_off, wide[...].astype(BF16), elements, quarter)
-    own = gathered[blk, :, 0:quarter]
+    own = gathered[blk, :, 0:quarter].astype(F32)
     return (base[...] - (inv_diag[...] * own + product)) * mask
 
 
 def sweep_kernel(
-    degree, owner, side, peer, coupling, inv_diag, inv_off, base, gathered, out, weight_out, wide
+    degree, tables, fold, coupling, inv_diag, inv_off, base, gathered, out, weight_out, wide
 ):
     elements, quarter = base.shape
-    faces = owner.shape[1]
+    faces = coupling.shape[0] // quarter
     blk = lax.axis_index("blk")
     mask = mask_of(degree[...], quarter, blk * quarter)
     adjoint = update(inv_diag, inv_off, base, gathered, mask, blk, wide)
     state = adjoint.astype(BF16).astype(F32)
-    target = targets(side[...], peer[...], elements)
-    put_transposed(out, coupling, state, owner[...], target, elements, quarter, faces)
+    put_transposed(out, coupling, state, tables[...], fold[...], elements, quarter, faces)
     weight_out[...] = (gathered[0, :, 128:640] + gathered[1, :, 128:640]) + (
         gathered[2, :, 128:640] + gathered[3, :, 128:640]
     )
@@ -285,11 +281,18 @@
     across = lambda x: lax.all_to_all(x, "blk", 0, 0)
     group = lambda x: lax.all_to_all(x, ("dom", "blk"), 0, 0, axis_index_groups=groups)
 
-    gathered = across(call(first_kernel, shape(4, elements, 128), degree, source, far=2, cost=pl.CostEstimate(flops=COST, transcendentals=0, bytes_accessed=1 << 12)))
-    message_shape = shape(16, 4 * elements, 128, kind=BF16)
-    message, base, weight = call(
+    gathered = across(call(first_kernel, shape(4, elements, 128, kind=BF16), degree, source, far=2, cost=pl.CostEstimate(flops=COST, transcendentals=0, bytes_accessed=1 << 12)))
+    message_shape = shape(16, elements, 384, kind=BF16)
+    lanes = faces * quarter
+    message, base, weight, tables, fold = call(
         base_kernel,
-        (message_shape, shape(elements, quarter), shape(elements, 512)),
+        (
+            message_shape,
+            shape(elements, quarter),
+            shape(elements, 512),
+            shape(8, lanes),
+            shape(quarter, lanes, kind=BF16),
+        ),
         degree, *faces_of, inv_diag, source, residual, inv_off, coupling, gathered,
         scratch=wide,
     )
@@ -303,15 +306,15 @@
         extra = (weight,) if sweep == 0 else ()
         coupled = call(
             couple_kernel,
-            shape(4, elements, 640 if sweep == 0 else 128),
-            degree, *faces_of, coupling, before, first, after, kept, *extra,
+            shape(4, elements, 640) if sweep == 0 else shape(4, elements, 128, kind=BF16),
+            degree, tables, fold, coupling, before, first, after, kept, *extra,
         )
         gathered = across(coupled)
         if sweep == 0:
             message, weight = call(
                 sweep_kernel,
                 (message_shape, shape(elements, 512)),
-                degree, *faces_of, coupling, inv_diag, inv_off, base, gathered,
+                degree, tables, fold, coupling, inv_diag, inv_off, base, gathered,
                 scratch=wide,
             )
     adjoint, indicator = call(

time: 82.2 us -> 81.4 us (level)
  no operation moved by 1% of the time
where the time goes in v4:
time: 81.4 us; the launch traced here: 81 us
  blocking collectives  45.5 us (56%)
  starting transfers between devices  18.1 us (22%)
  waiting for transfers between devices  10.4 us (13%)
  Pallas kernels  6.01 us (7%)
  between operations  0.83 us (1%)
    all_to_all x3, blocking collectives, local(): across = lambda x: lax.all_to_all(x, 'blk', 0, 0)  28.1 us
    ppermute x4, starting transfers between devices, swap(): lax.ppermute(block, 'dom', [(i, (i + step(i)) % count) for i in range(cou...  18.1 us
    all_to_all x2, blocking collectives, local(): lax.all_to_all(x, ('dom', 'blk'), 0, 0, axis_index_groups=groups)  17.4 us
    ppermute x4, waiting for transfers between devices, swap(): lax.ppermute(block, 'dom', [(i, (i + step(i)) % count) for i in range(cou...  10.4 us
    pallas_call x8, Pallas kernels, call(): pl.pallas_call(body, out_shape=shapes, in_specs=[space(i) for i in range(...  6.01 us
  transfers between devices with their start and end apart: 4, of which 3 were waited for; matrix products, arithmetic and copies ran while one was open for 0% of the time, Pallas kernels for 0%

profile of v4, /device:TPU:8, one launch (start us, length us, event | category | flops | bytes accessed | tf_op | source)
XLA Modules:
  0.0 81.0 jit_solution(17673506517699924235)
XLA Ops:
  0.6 0.0 copy-start
  0.6 0.0 copy-start.1
  0.7 0.0 copy-start.2
  0.7 0.0 copy-start.3
  0.7 0.0 copy-start.4
  0.7 0.0 copy-start.5
  0.7 0.0 copy-start.6
  0.7 0.0 copy-start.7
  0.7 0.0 copy-start.8
  0.7 0.9 %shard_map.104 = bf16[4,8,128]{2,1,0:T(8,128)(2,1)S(1)} custom-call(s32[1,8]{1,0:T(1,128)} %bitcast.14, f32[8,80]{1,0:T(8,128)} %source.1), custom_call_target="tpu_custom_call" | custom-call | flops 20000000000 | bytes 4096 | tf_op jit(solution)/shard_map/pallas_call | solution.py:252
  1.7 12.0 %all_to_all.25.gathered = bf16[4,8,128]{2,1,0:T(8,128)(2,1)S(1)} all-to-all(bf16[4,8,128]{2,1,0:T(8,128)(2,1)S(1)} %shard_map.104), channel_id=1, replica_groups=mesh['dom'=128,'blk'=4] {'blk'}, dimensions={0} | all-to-all | bytes 16384 | tf_op jit(solution)/shard_map/all_to_all | solution.py:281
  13.7 0.0 copy-done
  13.7 0.0 copy-done.1
  13.7 0.0 copy-done.2
  13.7 0.0 copy-done.3
  13.7 0.0 copy-done.4
  13.7 0.0 copy-done.5
  13.7 0.0 copy-done.6
  13.7 0.0 copy-done.7
  13.7 0.0 copy-done.8
  13.7 1.0 %shard_map.105 = (bf16[16,8,384]{2,1,0:T(8,128)(2,1)S(1)}, f32[8,80]{1,0:T(8,128)S(1)}, f32[8,512]{1,0:T(8,128)S(1)}, f32[8,2560]{1,0:T(8,128)S(1)}, bf16[80,2560]{1,0:T(8,128)(2,1)S(1)}) custom-call(s32[1,8]{1,0:T(1,128)S(1)} %bitcast.15, s32[1,32]{1,0:T(1,128)S(1)} %bitcast.20, s32[1,32]{1,0:T(1,128)S(1)} %bitcast.21, s32[1,32]{1,0:T(1,128)S(1)} %bitcast.22, ...), custom_call_target="tpu_custom_call" | custom-call | tf_op jit(solution)/shard_map/pallas_call | solution.py:252
  14.8 8.7 %all_to_all.26.message = bf16[16,8,384]{2,1,0:T(8,128)(2,1)S(1)} all-to-all(bf16[16,8,384]{2,1,0:T(8,128)(2,1)S(1)} %get-tuple-element.20), channel_id=1, replica_groups={{0,1,2,3,4,5,6,7,8,9,10,11,12,13,14,15},{16,17,18,19,20,21,22,23,24,25,..., dimensions={0} | all-to-all | bytes 196608 | tf_op jit(solution)/shard_map/all_to_all | solution.py:282
  23.5 0.1 shard_map.106
  23.6 10.9 %collective-permute-start.1 = (bf16[48,384]{1,0:T(8,128)(2,1)S(1)}, bf16[48,384]{1,0:T(8,128)(2,1)S(1)}, u32[]{:S(2)}, u32[]{:S(2)}) collective-permute-start(bf16[48,384]{1,0:T(8,128)(2,1)S(1)} %get-tuple-element.22), channel_id=1, source_target_pairs={{0,496},{4,500},{8,504},{12,508},{16,32},{20,36},{24,40},{28,44},{... | collective-permute-start | bytes 110600 | tf_op jit(solution)/shard_map/ppermute | solution.py:265
  34.4 1.9 %collective-permute-start = (bf16[48,384]{1,0:T(8,128)(2,1)S(1)}, bf16[48,384]{1,0:T(8,128)(2,1)S(1)}, u32[]{:S(2)}, u32[]{:S(2)}) collective-permute-start(bf16[48,384]{1,0:T(8,128)(2,1)S(1)} %get-tuple-element.21.middle), channel_id=1, source_target_pairs={{0,16},{4,20},{8,24},{12,28},{16,0},{20,4},{24,8},{28,12},{32,48},... | collective-permute-start | bytes 110600 | tf_op jit(solution)/shard_map/ppermute | solution.py:265
  36.4 0.0 collective-permute-done.1.after
  36.4 5.2 %collective-permute-done.before = bf16[48,384]{1,0:T(8,128)(2,1)S(1)} collective-permute-done((bf16[48,384]{1,0:T(8,128)(2,1)S(1)}, bf16[48,384]{1,0:T(8,128)(2,1)S(1)}, u32[]{:S(2)}, u32[]{:S(2)}) %collective-permute-start) | collective-permute-done | bytes 36896 | tf_op jit(solution)/shard_map/ppermute | solution.py:265
  41.6 1.0 %shard_map.107 = f32[4,8,640]{2,1,0:T(8,128)S(1)} custom-call(s32[1,8]{1,0:T(1,128)S(1)} %bitcast.16, f32[8,2560]{1,0:T(8,128)S(1)} %get-tuple-element.18.tables, bf16[80,2560]{1,0:T(8,128)(2,1)S(1)} %get-tuple-element.19.fold, bf16[2560,320]{1,0:T(8,128)(2,1)S(1)} %bitcast.8, bf16[48,384]{1,0:T(8,128)(2,1)S(1)} %collective-permute-done.before, ...), custom_call_target="tpu_custom_call" | custom-call | tf_op jit(solution)/shard_map/pallas_call | solution.py:252
  42.5 8.3 %all_to_all.27.gathered = f32[4,8,640]{2,1,0:T(8,128)S(1)} all-to-all(f32[4,8,640]{2,1,0:T(8,128)S(1)} %shard_map.107), channel_id=1, replica_groups=mesh['dom'=128,'blk'=4] {'blk'}, dimensions={0} | all-to-all | bytes 163840 | tf_op jit(solution)/shard_map/all_to_all | solution.py:281
  50.8 1.0 %shard_map.108 = (bf16[16,8,384]{2,1,0:T(8,128)(2,1)S(1)}, f32[8,512]{1,0:T(8,128)S(1)}) custom-call(s32[1,8]{1,0:T(1,128)S(1)} %bitcast.17, f32[8,2560]{1,0:T(8,128)S(1)} %get-tuple-element.18.tables, bf16[80,2560]{1,0:T(8,128)(2,1)S(1)} %get-tuple-element.19.fold, bf16[2560,320]{1,0:T(8,128)(2,1)S(1)} %bitcast.9, f32[8,80]{1,0:T(8,128)S(1)} %copy-done.2, ...), custom_call_target="tpu_custom_call" | custom-call | tf_op jit(solution)/shard_map/pallas_call | solution.py:252
  51.8 8.7 %all_to_all.28.message = bf16[16,8,384]{2,1,0:T(8,128)(2,1)S(1)} all-to-all(bf16[16,8,384]{2,1,0:T(8,128)(2,1)S(1)} %get-tuple-element.26), channel_id=1, replica_groups={{0,1,2,3,4,5,6,7,8,9,10,11,12,13,14,15},{16,17,18,19,20,21,22,23,24,25,..., dimensions={0} | all-to-all | bytes 196608 | tf_op jit(solution)/shard_map/all_to_all | solution.py:282
  60.5 0.1 shard_map.109
  60.6 3.4 %collective-permute-start.3 = (bf16[48,384]{1,0:T(8,128)(2,1)S(1)}, bf16[48,384]{1,0:T(8,128)(2,1)S(1)}, u32[]{:S(2)}, u32[]{:S(2)}) collective-permute-start(bf16[48,384]{1,0:T(8,128)(2,1)S(1)} %get-tuple-element.28), channel_id=1, source_target_pairs={{0,496},{4,500},{8,504},{12,508},{16,32},{20,36},{24,40},{28,44},{... | collective-permute-start | bytes 110600 | tf_op jit(solution)/shard_map/ppermute | solution.py:265
  64.0 1.9 %collective-permute-start.2 = (bf16[48,384]{1,0:T(8,128)(2,1)S(1)}, bf16[48,384]{1,0:T(8,128)(2,1)S(1)}, u32[]{:S(2)}, u32[]{:S(2)}) collective-permute-start(bf16[48,384]{1,0:T(8,128)(2,1)S(1)} %get-tuple-element.27.middle), channel_id=1, source_target_pairs={{0,16},{4,20},{8,24},{12,28},{16,0},{20,4},{24,8},{28,12},{32,48},... | collective-permute-start | bytes 110600 | tf_op jit(solution)/shard_map/ppermute | solution.py:265
  66.0 4.7 %collective-permute-done.3.after = bf16[48,384]{1,0:T(8,128)(2,1)S(1)} collective-permute-done((bf16[48,384]{1,0:T(8,128)(2,1)S(1)}, bf16[48,384]{1,0:T(8,128)(2,1)S(1)}, u32[]{:S(2)}, u32[]{:S(2)}) %collective-permute-start.3) | collective-permute-done | bytes 36896 | tf_op jit(solution)/shard_map/ppermute | solution.py:265
  70.7 0.5 collective-permute-done.2.before
  71.2 1.0 %shard_map.110 = bf16[4,8,128]{2,1,0:T(8,128)(2,1)S(1)} custom-call(s32[1,8]{1,0:T(1,128)S(1)} %bitcast.18, f32[8,2560]{1,0:T(8,128)S(1)} %get-tuple-element.18.tables, bf16[80,2560]{1,0:T(8,128)(2,1)S(1)} %get-tuple-element.19.fold, bf16[2560,320]{1,0:T(8,128)(2,1)S(1)} %bitcast.10, bf16[48,384]{1,0:T(8,128)(2,1)S(1)} %collective-permute-done.2.before, ...), custom_call_target="tpu_custom_call" | custom-call | tf_op jit(solution)/shard_map/pallas_call | solution.py:252
  72.2 7.9 %all_to_all.29.gathered = bf16[4,8,128]{2,1,0:T(8,128)(2,1)S(1)} all-to-all(bf16[4,8,128]{2,1,0:T(8,128)(2,1)S(1)} %shard_map.110), channel_id=1, replica_groups=mesh['dom'=128,'blk'=4] {'blk'}, dimensions={0} | all-to-all | bytes 16384 | tf_op jit(solution)/shard_map/all_to_all | solution.py:281
  80.0 0.9 %shard_map.111 = (f32[8,80]{1,0:T(8,128)}, f32[1,8]{1,0:T(1,128)}) custom-call(s32[1,8]{1,0:T(1,128)S(1)} %bitcast.19, f32[8,80]{1,0:T(8,128)S(1)} %copy-done.2, bf16[640,320]{1,0:T(8,128)(2,1)S(1)} %bitcast.13, f32[8,80]{1,0:T(8,128)S(1)} %get-tuple-element.17.base, f32[8,512]{1,0:T(8,128)S(1)} %get-tuple-element.25.weight, ...), custom_call_target="tpu_custom_call" | custom-call | tf_op jit(solution)/shard_map/pallas_call | solution.py:252
Async XLA Ops:
  0.6 13.0 %copy-start = (bf16[32,80,320]{2,1,0:T(8,128)(2,1)S(1)}, bf16[32,80,320]{2,1,0:T(8,128)(2,1)}, u32[]{:S(2)}) copy-start(bf16[32,80,320]{2,1,0:T(8,128)(2,1)} %param.13) | copy-start | bytes 4915204
  0.6 13.0 %copy-start.1 = (bf16[8,80,320]{2,1,0:T(8,128)(2,1)S(1)}, bf16[8,80,320]{2,1,0:T(8,128)(2,1)}, u32[]{:S(2)}) copy-start(bf16[8,80,320]{2,1,0:T(8,128)(2,1)} %param.15) | copy-start | bytes 1228804
  0.7 13.0 %copy-start.2 = (f32[8,80]{1,0:T(8,128)S(1)}, f32[8,80]{1,0:T(8,128)}, u32[]{:S(2)}) copy-start(f32[8,80]{1,0:T(8,128)} %inv_diag.5) | copy-start | bytes 7684
  0.7 13.0 %copy-start.3 = (s32[8]{0:T(128)S(1)}, s32[8]{0:T(128)}, u32[]{:S(2)}) copy-start(s32[8]{0:T(128)} %param.9) | copy-start | bytes 100
  0.7 13.0 %copy-start.4 = (f32[8,80]{1,0:T(8,128)S(1)}, f32[8,80]{1,0:T(8,128)}, u32[]{:S(2)}) copy-start(f32[8,80]{1,0:T(8,128)} %source.1) | copy-start | bytes 7684
  0.7 13.0 %copy-start.5 = (f32[8,80]{1,0:T(8,128)S(1)}, f32[8,80]{1,0:T(8,128)}, u32[]{:S(2)}) copy-start(f32[8,80]{1,0:T(8,128)} %residual.1) | copy-start | bytes 7684
  0.7 13.0 %copy-start.6 = (s32[32]{0:T(128)S(1)}, s32[32]{0:T(128)}, u32[]{:S(2)}) copy-start(s32[32]{0:T(128)} %param.10) | copy-start | bytes 388
  0.7 13.0 %copy-start.7 = (s32[32]{0:T(128)S(1)}, s32[32]{0:T(128)}, u32[]{:S(2)}) copy-start(s32[32]{0:T(128)} %param.11) | copy-start | bytes 388
  0.7 13.0 %copy-start.8 = (s32[32]{0:T(128)S(1)}, s32[32]{0:T(128)}, u32[]{:S(2)}) copy-start(s32[32]{0:T(128)} %param.12) | copy-start | bytes 388
  23.6 12.8 %collective-permute-start.1 = (bf16[48,384]{1,0:T(8,128)(2,1)S(1)}, bf16[48,384]{1,0:T(8,128)(2,1)S(1)}, u32[]{:S(2)}, u32[]{:S(2)}) collective-permute-start(bf16[48,384]{1,0:T(8,128)(2,1)S(1)} %get-tuple-element.22), channel_id=1, source_target_pairs={{0,496},{4,500},{8,504},{12,508},{16,32},{20,36},{24,40},{28,44},{... | collective-permute-start | bytes 110600 | tf_op jit(solution)/shard_map/ppermute | solution.py:265
  34.4 7.1 %collective-permute-start = (bf16[48,384]{1,0:T(8,128)(2,1)S(1)}, bf16[48,384]{1,0:T(8,128)(2,1)S(1)}, u32[]{:S(2)}, u32[]{:S(2)}) collective-permute-start(bf16[48,384]{1,0:T(8,128)(2,1)S(1)} %get-tuple-element.21.middle), channel_id=1, source_target_pairs={{0,16},{4,20},{8,24},{12,28},{16,0},{20,4},{24,8},{28,12},{32,48},... | collective-permute-start | bytes 110600 | tf_op jit(solution)/shard_map/ppermute | solution.py:265
  60.6 10.1 %collective-permute-start.3 = (bf16[48,384]{1,0:T(8,128)(2,1)S(1)}, bf16[48,384]{1,0:T(8,128)(2,1)S(1)}, u32[]{:S(2)}, u32[]{:S(2)}) collective-permute-start(bf16[48,384]{1,0:T(8,128)(2,1)S(1)} %get-tuple-element.28), channel_id=1, source_target_pairs={{0,496},{4,500},{8,504},{12,508},{16,32},{20,36},{24,40},{28,44},{... | collective-permute-start | bytes 110600 | tf_op jit(solution)/shard_map/ppermute | solution.py:265
  64.0 7.1 %collective-permute-start.2 = (bf16[48,384]{1,0:T(8,128)(2,1)S(1)}, bf16[48,384]{1,0:T(8,128)(2,1)S(1)}, u32[]{:S(2)}, u32[]{:S(2)}) collective-permute-start(bf16[48,384]{1,0:T(8,128)(2,1)S(1)} %get-tuple-element.27.middle), channel_id=1, source_target_pairs={{0,16},{4,20},{8,24},{12,28},{16,0},{20,4},{24,8},{28,12},{32,48},... | collective-permute-start | bytes 110600 | tf_op jit(solution)/shard_map/ppermute | solution.py:265

commit v5 on v4

--- a/solution.py
+++ b/solution.py
@@ -12,6 +12,7 @@
 HALF = NEIGH // 2
 F32 = jnp.float32
 BF16 = jnp.bfloat16
+ORDER = (1, 3, 0, 2)
 COST = 20_000_000_000
 NT = (((1,), (1,)), ((), ()))
 
@@ -69,7 +70,7 @@
 
 def place():
     dom = lax.axis_index("dom")
-    return dom % HALF, 2 * ((dom // HALF) % 2) - 1
+    return dom % HALF, 1
 
 
 def targets(side, peer, elements):
@@ -109,8 +110,8 @@
         for r in range(HALF):
             for s in range(3):
                 at = (s * HALF + r) * elements
-                out[r * 4 + q, :, s * quarter : (s + 1) * quarter] = part[at : at + elements].astype(BF16)
-            out[r * 4 + q, :, 3 * quarter : 4 * quarter] = state.astype(BF16)
+                out[ORDER.index(r) * 4 + q, :, s * quarter : (s + 1) * quarter] = part[at : at + elements].astype(BF16)
+            out[ORDER.index(r) * 4 + q, :, 3 * quarter : 4 * quarter] = state.astype(BF16)
 
 
 def first_kernel(degree_in, source_in, out, degree, source, arrived):
@@ -124,12 +125,11 @@
 
 
 def base_kernel(
-    degree, owner, side, peer, inv_diag, source, residual, inv_off, coupling, gathered,
-    out, base_out, weight_out, tables_out, fold_out, wide,
+    degree, owner, side, peer, inv_diag, source, inv_off, coupling, gathered,
+    out, base_out, tables_out, fold_out, wide,
 ):
     elements, quarter = source.shape
     faces = owner.shape[1]
-    width = 4 * quarter
     blk = lax.axis_index("blk")
     for q in range(4):
         wide[:, q * quarter : (q + 1) * quarter] = gathered[q, :, 0:quarter].astype(F32)
@@ -146,6 +146,50 @@
     tables = per_lane(face, both)
     tables_out[...] = tables
     fold_out[...] = fold
+    put_transposed(out, coupling, state, tables, fold, elements, quarter, faces)
+
+
+def merge_kernel(message, first, second, kept):
+    elements, quarter = kept.shape
+    total = message[0].astype(F32)
+    for i in range(1, 16):
+        total = total + message[i].astype(F32)
+    rows = HALF * elements
+    first[rows:, 0:quarter] = two_parts(total[:, 0:quarter])
+    kept[...] = total[:, quarter : 2 * quarter]
+    second[rows:, 0:quarter] = two_parts(total[:, 2 * quarter : 3 * quarter])
+    for q in range(4):
+        state = jnp.concatenate(
+            [message[ORDER.index(r) * 4 + q].astype(F32)[:, 3 * quarter : 4 * quarter] for r in range(HALF)], axis=0
+        ).astype(BF16)
+        first[0:rows, q * quarter : (q + 1) * quarter] = state
+        second[0:rows, q * quarter : (q + 1) * quarter] = state
+
+
+def local_sum(states, places, coupling, tables, fold, elements):
+    products = dot_nt(states, coupling[...])
+    terms = jnp.sum(jnp.where(places == tables[1:2, :], products, 0.0), axis=0, keepdims=True)
+    element = lax.broadcasted_iota(jnp.int32, (elements, fold.shape[1]), 0).astype(F32)
+    spread = jnp.where(element == tables[0:1, :], terms, 0.0)
+    folded = dot_nt(two_parts(spread), fold[...])
+    return folded[0:elements] + folded[elements : 2 * elements]
+
+
+def inner_kernel(tables, fold, coupling, middle, kept, out):
+    elements, quarter = kept.shape
+    rows = HALF * elements
+    places = lax.broadcasted_iota(jnp.int32, (rows, fold.shape[1]), 0) + rows
+    states = middle[0:rows, 0 : 4 * quarter]
+    out[...] = kept[...] + local_sum(
+        states, places.astype(F32), coupling, tables, fold, elements
+    )
+
+
+def weight_kernel(degree, inv_diag, inv_off, residual, base, weight_out, wide):
+    elements, quarter = base.shape
+    width = 4 * quarter
+    blk = lax.axis_index("blk")
+    mask = mask_of(degree[...], quarter, blk * quarter)
     weighted = residual[...] * mask
     parts = two_parts(weighted)
     row = lax.broadcasted_iota(jnp.int32, (elements, width), 0)
@@ -160,46 +204,20 @@
         wide[:, at] = wide[:, at] + jnp.where(blk == q, diagonal, 0.0)
     weight_out[:, 0:width] = wide[...]
     weight_out[:, 384:512] = jnp.broadcast_to(
-        jnp.sum(weighted * base, axis=1, keepdims=True), (elements, 128)
-    )
-    put_transposed(out, coupling, state, tables, fold, elements, quarter, faces)
-
-
-def merge_kernel(message, first, second, kept):
-    elements, quarter = kept.shape
-    total = message[0].astype(F32)
-    for i in range(1, 16):
-        total = total + message[i].astype(F32)
-    rows = HALF * elements
-    first[rows:, 0:quarter] = two_parts(total[:, 0:quarter])
-    kept[...] = total[:, quarter : 2 * quarter]
-    second[rows:, 0:quarter] = two_parts(total[:, 2 * quarter : 3 * quarter])
-    for q in range(4):
-        state = jnp.concatenate(
-            [message[r * 4 + q].astype(F32)[:, 3 * quarter : 4 * quarter] for r in range(HALF)], axis=0
-        ).astype(BF16)
-        first[0:rows, q * quarter : (q + 1) * quarter] = state
-        second[0:rows, q * quarter : (q + 1) * quarter] = state
-
-
-def couple_kernel(degree, tables, fold, coupling, before, middle, after, kept, *rest):
+        jnp.sum(weighted * base[...], axis=1, keepdims=True), (elements, 128)
+    )
+
+
+def couple_kernel(degree, tables, fold, coupling, before, after, inner, *rest):
     out = rest[-1]
-    elements, quarter = kept.shape
+    elements, quarter = inner.shape
     width = 4 * quarter
-    lanes = fold.shape[1]
     mask = mask_of(degree[...], quarter, lax.axis_index("blk") * quarter)
     rows = HALF * elements
-    states = jnp.concatenate(
-        [before[0:rows, 0:width], middle[0:rows, 0:width], after[0:rows, 0:width]], axis=0
-    )
-    products = dot_nt(states, coupling[...])
-    places = lax.broadcasted_iota(jnp.int32, (3 * rows, lanes), 0).astype(F32)
-    terms = jnp.sum(jnp.where(places == tables[1:2, :], products, 0.0), axis=0, keepdims=True)
-    element = lax.broadcasted_iota(jnp.int32, (elements, lanes), 0).astype(F32)
-    spread = jnp.where(element == tables[0:1, :], terms, 0.0)
-    folded = dot_nt(two_parts(spread), fold[...])
-    coupled = folded[0:elements] + folded[elements : 2 * elements]
-    coupled = coupled + kept[...]
+    states = jnp.concatenate([before[0:rows, 0:width], after[0:rows, 0:width]], axis=0)
+    index = lax.broadcasted_iota(jnp.int32, (2 * rows, fold.shape[1]), 0)
+    places = jnp.where(index >= rows, index + rows, index).astype(F32)
+    coupled = inner[...] + local_sum(states, places, coupling, tables, fold, elements)
     for sent in (before, after):
         pair = sent[rows:, 0:quarter].astype(F32)
         coupled = coupled + (pair[0:elements] + pair[elements : 2 * elements])
@@ -259,10 +277,9 @@
     )(*[pltpu.with_memory_space_constraint(x, pltpu.HBM) for x in args[:far]], *args[far:])
 
 
-def swap(block, odd):
+def hop(block, distance):
     count = lax.axis_size("dom")
-    step = lambda i: HALF if (i // HALF) % 2 == odd else -HALF
-    return lax.ppermute(block, "dom", [(i, (i + step(i)) % count) for i in range(count)])
+    return lax.ppermute(block, "dom", [(i, (i + distance) % count) for i in range(count)])
 
 
 def local(degree, face_elem, face_side, face_peer, coupling, inv_diag, inv_off, source, residual):
@@ -270,7 +287,7 @@
     faces, _, width = coupling.shape
     doms = lax.axis_size("dom")
     groups = [
-        [(first + i) * 4 + q for i in range(HALF) for q in range(4)] for first in range(0, doms, HALF)
+        [(first + i) * 4 + q for i in ORDER for q in range(4)] for first in range(0, doms, HALF)
     ]
     shape = lambda *dims, kind=F32: jax.ShapeDtypeStruct(dims, kind)
     degree = degree.reshape(1, elements)
@@ -284,16 +301,15 @@
     gathered = across(call(first_kernel, shape(4, elements, 128, kind=BF16), degree, source, far=2, cost=pl.CostEstimate(flops=COST, transcendentals=0, bytes_accessed=1 << 12)))
     message_shape = shape(16, elements, 384, kind=BF16)
     lanes = faces * quarter
-    message, base, weight, tables, fold = call(
+    message, base, tables, fold = call(
         base_kernel,
         (
             message_shape,
             shape(elements, quarter),
-            shape(elements, 512),
             shape(8, lanes),
             shape(quarter, lanes, kind=BF16),
         ),
-        degree, *faces_of, inv_diag, source, residual, inv_off, coupling, gathered,
+        degree, *faces_of, inv_diag, source, inv_off, coupling, gathered,
         scratch=wide,
     )
     for sweep in range(SWEEPS):
@@ -301,13 +317,19 @@
         first, second, kept = call(
             merge_kernel, (hop_shape, hop_shape, shape(elements, quarter)), group(message)
         )
-        before = swap(first, 0)
-        after = swap(second, 1)
+        before = hop(second, HALF)
+        after = hop(first, -HALF)
+        inner = call(inner_kernel, shape(elements, quarter), tables, fold, coupling, first, kept)
+        if sweep == 0:
+            weight = call(
+                weight_kernel, shape(elements, 512),
+                degree, inv_diag, inv_off, residual, base, scratch=wide,
+            )
         extra = (weight,) if sweep == 0 else ()
         coupled = call(
             couple_kernel,
             shape(4, elements, 640) if sweep == 0 else shape(4, elements, 128, kind=BF16),
-            degree, tables, fold, coupling, before, first, after, kept, *extra,
+            degree, tables, fold, coupling, before, after, inner, *extra,
         )
         gathered = across(coupled)
         if sweep == 0:

time: 81.4 us -> 79.1 us (0.972)
  waiting for transfers between devices: 10.4 us -> 1.04 us
  starting transfers between devices: 18.1 us -> 23.5 us
  Pallas kernels: 6.01 us -> 8.19 us
    ppermute x4, waiting for transfers between devices: 10.4 us -> 1.04 us  [hop(): lax.ppermute(block, 'dom', [(i, (i + distance) % count) for i in range(co...]
    ppermute x4, starting transfers between devices: 18.1 us -> 23.5 us  [hop(): lax.ppermute(block, 'dom', [(i, (i + distance) % count) for i in range(co...]
    pallas_call x8 -> x11, Pallas kernels: 6.01 us -> 8.19 us  [call(): pl.pallas_call(body, out_shape=shapes, in_specs=[space(i) for i in range(...]
    all_to_all x2, blocking collectives: 17.4 us -> 16.6 us  [local(): lax.all_to_all(x, ('dom', 'blk'), 0, 0, axis_index_groups=groups)]
  transfers between devices with their start and end apart: 4 -> 4, of which waited for: 3 -> 2; matrix products, arithmetic and copies ran while one was open for 0% -> 0% of each run, Pallas kernels for 0% -> 3%
where the time goes in v5:
time: 79.1 us; the launch traced here: 78.7 us
  blocking collectives  45.1 us (57%)
  starting transfers between devices  23.5 us (30%)
  Pallas kernels  8.19 us (10%)
  waiting for transfers between devices  1.04 us (1%)
  between operations  0.82 us (1%)
    all_to_all x3, blocking collectives, local(): across = lambda x: lax.all_to_all(x, 'blk', 0, 0)  28.6 us
    ppermute x4, starting transfers between devices, hop(): lax.ppermute(block, 'dom', [(i, (i + distance) % count) for i in range(co...  23.5 us
    all_to_all x2, blocking collectives, local(): lax.all_to_all(x, ('dom', 'blk'), 0, 0, axis_index_groups=groups)  16.6 us
    pallas_call x11, Pallas kernels, call(): pl.pallas_call(body, out_shape=shapes, in_specs=[space(i) for i in range(...  8.19 us
  transfers between devices with their start and end apart: 4, of which 2 were waited for; matrix products, arithmetic and copies ran while one was open for 0% of the time, Pallas kernels for 3%

profile of v5, /device:TPU:8, one launch (start us, length us, event | category | flops | bytes accessed | tf_op | source)
XLA Modules:
  0.0 78.7 jit_solution(15648573106673759703)
XLA Ops:
  0.6 0.0 copy-start
  0.6 0.0 copy-start.1
  0.7 0.0 copy-start.2
  0.7 0.0 copy-start.3
  0.7 0.0 copy-start.4
  0.7 0.0 copy-start.6
  0.7 0.0 copy-start.7
  0.7 0.0 copy-start.8
  0.7 0.9 %shard_map.104 = bf16[4,8,128]{2,1,0:T(8,128)(2,1)S(1)} custom-call(s32[1,8]{1,0:T(1,128)} %bitcast.17, f32[8,80]{1,0:T(8,128)} %source.1), custom_call_target="tpu_custom_call" | custom-call | flops 20000000000 | bytes 4096 | tf_op jit(solution)/shard_map/pallas_call | solution.py:270
  1.7 0.0 copy-start.5
  1.7 12.0 %all_to_all.25.gathered = bf16[4,8,128]{2,1,0:T(8,128)(2,1)S(1)} all-to-all(bf16[4,8,128]{2,1,0:T(8,128)(2,1)S(1)} %shard_map.104), channel_id=1, replica_groups=mesh['dom'=128,'blk'=4] {'blk'}, dimensions={0} | all-to-all | bytes 16384 | tf_op jit(solution)/shard_map/all_to_all | solution.py:298
  13.7 0.0 copy-done
  13.7 0.0 copy-done.1
  13.7 0.0 copy-done.2
  13.7 0.0 copy-done.3
  13.7 0.0 copy-done.4
  13.7 0.0 copy-done.6
  13.7 0.0 copy-done.7
  13.7 0.0 copy-done.8
  13.7 1.0 %shard_map.105 = (bf16[16,8,384]{2,1,0:T(8,128)(2,1)S(1)}, f32[8,80]{1,0:T(8,128)S(1)}, f32[8,2560]{1,0:T(8,128)S(1)}, bf16[80,2560]{1,0:T(8,128)(2,1)S(1)}) custom-call(s32[1,8]{1,0:T(1,128)S(1)} %bitcast.18, s32[1,32]{1,0:T(1,128)S(1)} %bitcast.24, s32[1,32]{1,0:T(1,128)S(1)} %bitcast.25, s32[1,32]{1,0:T(1,128)S(1)} %bitcast.26, f32[8,80]{1,0:T(8,128)S(1)} %copy-done.2, ...), custom_call_target="tpu_custom_call" | custom-call | tf_op jit(solution)/shard_map/pallas_call | solution.py:270
  14.7 8.3 %all_to_all.26.message = bf16[16,8,384]{2,1,0:T(8,128)(2,1)S(1)} all-to-all(bf16[16,8,384]{2,1,0:T(8,128)(2,1)S(1)} %get-tuple-element.19), channel_id=1, replica_groups={{4,5,6,7,12,13,14,15,0,1,2,3,8,9,10,11},{20,21,22,23,28,29,30,31,16,17,..., dimensions={0} | all-to-all | bytes 196608 | tf_op jit(solution)/shard_map/all_to_all | solution.py:299
  23.0 0.1 shard_map.106
  23.1 3.1 %collective-permute-start = (bf16[48,384]{1,0:T(8,128)(2,1)S(1)}, bf16[48,384]{1,0:T(8,128)(2,1)S(1)}, u32[]{:S(2)}, u32[]{:S(2)}) collective-permute-start(bf16[48,384]{1,0:T(8,128)(2,1)S(1)} %get-tuple-element.20), channel_id=1, source_target_pairs={{0,16},{4,20},{8,24},{12,28},{16,32},{20,36},{24,40},{28,44},{32,4... | collective-permute-start | bytes 110600 | tf_op jit(solution)/shard_map/ppermute | solution.py:282
  26.2 9.9 %collective-permute-start.1 = (bf16[48,384]{1,0:T(8,128)(2,1)S(1)}, bf16[48,384]{1,0:T(8,128)(2,1)S(1)}, u32[]{:S(2)}, u32[]{:S(2)}) collective-permute-start(bf16[48,384]{1,0:T(8,128)(2,1)S(1)} %get-tuple-element.21.middle), channel_id=1, source_target_pairs={{0,496},{4,500},{8,504},{12,508},{16,0},{20,4},{24,8},{28,12},{32,... | collective-permute-start | bytes 110600 | tf_op jit(solution)/shard_map/ppermute | solution.py:282
  36.1 0.0 copy-done.5
  36.1 0.3 shard_map.108.rest_0_
  36.4 0.9 %shard_map.107.inner = f32[8,80]{1,0:T(8,128)S(1)} custom-call(f32[8,2560]{1,0:T(8,128)S(1)} %get-tuple-element.17.tables, bf16[80,2560]{1,0:T(8,128)(2,1)S(1)} %get-tuple-element.18.fold, bf16[2560,320]{1,0:T(8,128)(2,1)S(1)} %bitcast.8, bf16[48,384]{1,0:T(8,128)(2,1)S(1)} %get-tuple-element.21.middle, f32[8,80]{1,0:T(8,128)S(1)} %get-tuple-element.22.kept), custom_call_target="tpu_custom_call" | custom-call | tf_op jit(solution)/shard_map/pallas_call | solution.py:270
  37.4 0.0 collective-permute-done.before
  37.4 0.4 collective-permute-done.1.after
  37.7 1.0 %shard_map.109 = f32[4,8,640]{2,1,0:T(8,128)S(1)} custom-call(s32[1,8]{1,0:T(1,128)S(1)} %bitcast.20, f32[8,2560]{1,0:T(8,128)S(1)} %get-tuple-element.17.tables, bf16[80,2560]{1,0:T(8,128)(2,1)S(1)} %get-tuple-element.18.fold, bf16[2560,320]{1,0:T(8,128)(2,1)S(1)} %bitcast.9, bf16[48,384]{1,0:T(8,128)(2,1)S(1)} %collective-permute-done.before, ...), custom_call_target="tpu_custom_call" | custom-call | tf_op jit(solution)/shard_map/pallas_call | solution.py:270
  38.7 8.5 %all_to_all.27.gathered = f32[4,8,640]{2,1,0:T(8,128)S(1)} all-to-all(f32[4,8,640]{2,1,0:T(8,128)S(1)} %shard_map.109), channel_id=1, replica_groups=mesh['dom'=128,'blk'=4] {'blk'}, dimensions={0} | all-to-all | bytes 163840 | tf_op jit(solution)/shard_map/all_to_all | solution.py:298
  47.2 1.0 %shard_map.110 = (bf16[16,8,384]{2,1,0:T(8,128)(2,1)S(1)}, f32[8,512]{1,0:T(8,128)S(1)}) custom-call(s32[1,8]{1,0:T(1,128)S(1)} %bitcast.21, f32[8,2560]{1,0:T(8,128)S(1)} %get-tuple-element.17.tables, bf16[80,2560]{1,0:T(8,128)(2,1)S(1)} %get-tuple-element.18.fold, bf16[2560,320]{1,0:T(8,128)(2,1)S(1)} %bitcast.10, f32[8,80]{1,0:T(8,128)S(1)} %copy-done.2, ...), custom_call_target="tpu_custom_call" | custom-call | tf_op jit(solution)/shard_map/pallas_call | solution.py:270
  48.2 8.3 %all_to_all.28.message = bf16[16,8,384]{2,1,0:T(8,128)(2,1)S(1)} all-to-all(bf16[16,8,384]{2,1,0:T(8,128)(2,1)S(1)} %get-tuple-element.24), channel_id=1, replica_groups={{4,5,6,7,12,13,14,15,0,1,2,3,8,9,10,11},{20,21,22,23,28,29,30,31,16,17,..., dimensions={0} | all-to-all | bytes 196608 | tf_op jit(solution)/shard_map/all_to_all | solution.py:299
  56.5 0.1 shard_map.111
  56.6 3.0 %collective-permute-start.2 = (bf16[48,384]{1,0:T(8,128)(2,1)S(1)}, bf16[48,384]{1,0:T(8,128)(2,1)S(1)}, u32[]{:S(2)}, u32[]{:S(2)}) collective-permute-start(bf16[48,384]{1,0:T(8,128)(2,1)S(1)} %get-tuple-element.25), channel_id=1, source_target_pairs={{0,16},{4,20},{8,24},{12,28},{16,32},{20,36},{24,40},{28,44},{32,4... | collective-permute-start | bytes 110600 | tf_op jit(solution)/shard_map/ppermute | solution.py:282
  59.6 7.5 %collective-permute-start.3 = (bf16[48,384]{1,0:T(8,128)(2,1)S(1)}, bf16[48,384]{1,0:T(8,128)(2,1)S(1)}, u32[]{:S(2)}, u32[]{:S(2)}) collective-permute-start(bf16[48,384]{1,0:T(8,128)(2,1)S(1)} %get-tuple-element.26.middle), channel_id=1, source_target_pairs={{0,496},{4,500},{8,504},{12,508},{16,0},{20,4},{24,8},{28,12},{32,... | collective-permute-start | bytes 110600 | tf_op jit(solution)/shard_map/ppermute | solution.py:282
  67.1 0.9 %shard_map.112.inner = f32[8,80]{1,0:T(8,128)S(1)} custom-call(f32[8,2560]{1,0:T(8,128)S(1)} %get-tuple-element.17.tables, bf16[80,2560]{1,0:T(8,128)(2,1)S(1)} %get-tuple-element.18.fold, bf16[2560,320]{1,0:T(8,128)(2,1)S(1)} %bitcast.11, bf16[48,384]{1,0:T(8,128)(2,1)S(1)} %get-tuple-element.26.middle, f32[8,80]{1,0:T(8,128)S(1)} %get-tuple-element.27.kept), custom_call_target="tpu_custom_call" | custom-call | tf_op jit(solution)/shard_map/pallas_call | solution.py:270
  68.0 0.0 collective-permute-done.2.before
  68.0 0.7 collective-permute-done.3.after
  68.7 1.0 %shard_map.113 = bf16[4,8,128]{2,1,0:T(8,128)(2,1)S(1)} custom-call(s32[1,8]{1,0:T(1,128)S(1)} %bitcast.22, f32[8,2560]{1,0:T(8,128)S(1)} %get-tuple-element.17.tables, bf16[80,2560]{1,0:T(8,128)(2,1)S(1)} %get-tuple-element.18.fold, bf16[2560,320]{1,0:T(8,128)(2,1)S(1)} %bitcast.12, bf16[48,384]{1,0:T(8,128)(2,1)S(1)} %collective-permute-done.2.before, ...), custom_call_target="tpu_custom_call" | custom-call | tf_op jit(solution)/shard_map/pallas_call | solution.py:270
  69.7 8.1 %all_to_all.29.gathered = bf16[4,8,128]{2,1,0:T(8,128)(2,1)S(1)} all-to-all(bf16[4,8,128]{2,1,0:T(8,128)(2,1)S(1)} %shard_map.113), channel_id=1, replica_groups=mesh['dom'=128,'blk'=4] {'blk'}, dimensions={0} | all-to-all | bytes 16384 | tf_op jit(solution)/shard_map/all_to_all | solution.py:298
  77.8 0.9 %shard_map.114 = (f32[8,80]{1,0:T(8,128)}, f32[1,8]{1,0:T(1,128)}) custom-call(s32[1,8]{1,0:T(1,128)S(1)} %bitcast.23, f32[8,80]{1,0:T(8,128)S(1)} %copy-done.2, bf16[640,320]{1,0:T(8,128)(2,1)S(1)} %bitcast.16, f32[8,80]{1,0:T(8,128)S(1)} %get-tuple-element.16.base, f32[8,512]{1,0:T(8,128)S(1)} %get-tuple-element.23.weight, ...), custom_call_target="tpu_custom_call" | custom-call | tf_op jit(solution)/shard_map/pallas_call | solution.py:270
Async XLA Ops:
  0.6 13.0 %copy-start = (bf16[32,80,320]{2,1,0:T(8,128)(2,1)S(1)}, bf16[32,80,320]{2,1,0:T(8,128)(2,1)}, u32[]{:S(2)}) copy-start(bf16[32,80,320]{2,1,0:T(8,128)(2,1)} %param.13) | copy-start | bytes 4915204
  0.6 13.0 %copy-start.1 = (bf16[8,80,320]{2,1,0:T(8,128)(2,1)S(1)}, bf16[8,80,320]{2,1,0:T(8,128)(2,1)}, u32[]{:S(2)}) copy-start(bf16[8,80,320]{2,1,0:T(8,128)(2,1)} %param.15) | copy-start | bytes 1228804
  0.7 13.0 %copy-start.2 = (f32[8,80]{1,0:T(8,128)S(1)}, f32[8,80]{1,0:T(8,128)}, u32[]{:S(2)}) copy-start(f32[8,80]{1,0:T(8,128)} %inv_diag.7) | copy-start | bytes 7684
  0.7 13.0 %copy-start.3 = (s32[8]{0:T(128)S(1)}, s32[8]{0:T(128)}, u32[]{:S(2)}) copy-start(s32[8]{0:T(128)} %param.9) | copy-start | bytes 100
  0.7 13.0 %copy-start.4 = (f32[8,80]{1,0:T(8,128)S(1)}, f32[8,80]{1,0:T(8,128)}, u32[]{:S(2)}) copy-start(f32[8,80]{1,0:T(8,128)} %source.1) | copy-start | bytes 7684
  0.7 13.0 %copy-start.6 = (s32[32]{0:T(128)S(1)}, s32[32]{0:T(128)}, u32[]{:S(2)}) copy-start(s32[32]{0:T(128)} %param.10) | copy-start | bytes 388
  0.7 13.0 %copy-start.7 = (s32[32]{0:T(128)S(1)}, s32[32]{0:T(128)}, u32[]{:S(2)}) copy-start(s32[32]{0:T(128)} %param.11) | copy-start | bytes 388
  0.7 13.0 %copy-start.8 = (s32[32]{0:T(128)S(1)}, s32[32]{0:T(128)}, u32[]{:S(2)}) copy-start(s32[32]{0:T(128)} %param.12) | copy-start | bytes 388
  1.7 34.5 %copy-start.5 = (f32[8,80]{1,0:T(8,128)S(1)}, f32[8,80]{1,0:T(8,128)}, u32[]{:S(2)}) copy-start(f32[8,80]{1,0:T(8,128)} %residual.1) | copy-start | bytes 7684
  23.1 14.3 %collective-permute-start = (bf16[48,384]{1,0:T(8,128)(2,1)S(1)}, bf16[48,384]{1,0:T(8,128)(2,1)S(1)}, u32[]{:S(2)}, u32[]{:S(2)}) collective-permute-start(bf16[48,384]{1,0:T(8,128)(2,1)S(1)} %get-tuple-element.20), channel_id=1, source_target_pairs={{0,16},{4,20},{8,24},{12,28},{16,32},{20,36},{24,40},{28,44},{32,4... | collective-permute-start | bytes 110600 | tf_op jit(solution)/shard_map/ppermute | solution.py:282
  26.2 11.5 %collective-permute-start.1 = (bf16[48,384]{1,0:T(8,128)(2,1)S(1)}, bf16[48,384]{1,0:T(8,128)(2,1)S(1)}, u32[]{:S(2)}, u32[]{:S(2)}) collective-permute-start(bf16[48,384]{1,0:T(8,128)(2,1)S(1)} %get-tuple-element.21.middle), channel_id=1, source_target_pairs={{0,496},{4,500},{8,504},{12,508},{16,0},{20,4},{24,8},{28,12},{32,... | collective-permute-start | bytes 110600 | tf_op jit(solution)/shard_map/ppermute | solution.py:282
  56.6 11.5 %collective-permute-start.2 = (bf16[48,384]{1,0:T(8,128)(2,1)S(1)}, bf16[48,384]{1,0:T(8,128)(2,1)S(1)}, u32[]{:S(2)}, u32[]{:S(2)}) collective-permute-start(bf16[48,384]{1,0:T(8,128)(2,1)S(1)} %get-tuple-element.25), channel_id=1, source_target_pairs={{0,16},{4,20},{8,24},{12,28},{16,32},{20,36},{24,40},{28,44},{32,4... | collective-permute-start | bytes 110600 | tf_op jit(solution)/shard_map/ppermute | solution.py:282
  59.6 9.1 %collective-permute-start.3 = (bf16[48,384]{1,0:T(8,128)(2,1)S(1)}, bf16[48,384]{1,0:T(8,128)(2,1)S(1)}, u32[]{:S(2)}, u32[]{:S(2)}) collective-permute-start(bf16[48,384]{1,0:T(8,128)(2,1)S(1)} %get-tuple-element.26.middle), channel_id=1, source_target_pairs={{0,496},{4,500},{8,504},{12,508},{16,0},{20,4},{24,8},{28,12},{32,... | collective-permute-start | bytes 110600 | tf_op jit(solution)/shard_map/ppermute | solution.py:282

commit v6 on v5

--- a/solution.py
+++ b/solution.py
@@ -51,14 +51,27 @@
     return jnp.where(modes.astype(F32) < limit, 1.0, 0.0)
 
 
-def lane_tables(quarter, faces):
-    lanes = quarter * faces
-    lane = lax.broadcasted_iota(jnp.int32, (1, lanes), 1).astype(F32)
-    face = jnp.floor((lane + 0.5) * (1.0 / quarter))
-    inside = lane - face * quarter
-    row = lax.broadcasted_iota(jnp.int32, (quarter, lanes), 0).astype(F32)
-    fold = jnp.where(row == inside, 1.0, 0.0).astype(BF16)
-    return face, fold
+def lane_face(quarter, faces):
+    lane = lax.broadcasted_iota(jnp.int32, (1, quarter * faces), 1).astype(F32)
+    return jnp.floor((lane + 0.5) * (1.0 / quarter))
+
+
+def repeat_lanes(values, faces, buffer):
+    quarter = values.shape[1]
+    for f in range(8):
+        buffer[:, f * quarter : (f + 1) * quarter] = values
+    return jnp.concatenate([buffer[...]] * (faces // 8), axis=1)
+
+
+def sum_faces(values, quarter):
+    block = 8 * quarter
+    total = values[:, 0:block]
+    for at in range(block, values.shape[1], block):
+        total = total + values[:, at : at + block]
+    result = total[:, 0:quarter]
+    for f in range(1, 8):
+        result = result + total[:, f * quarter : (f + 1) * quarter]
+    return result
 
 
 def per_lane(face, values):
@@ -96,9 +109,9 @@
     return total
 
 
-def put_transposed(out, coupling, state, tables, fold, elements, quarter, faces):
+def put_transposed(out, coupling, state, tables, buffer, elements, quarter, faces):
     lanes = quarter * faces
-    repeated = dot(state.astype(BF16), fold)
+    repeated = repeat_lanes(state, faces, buffer)
     rows = lax.broadcasted_iota(jnp.int32, (elements, lanes), 0).astype(F32)
     spread = jnp.sum(jnp.where(rows == tables[0:1], repeated, 0.0), axis=0, keepdims=True)
     count = 3 * HALF * elements
@@ -126,7 +139,7 @@
 
 def base_kernel(
     degree, owner, side, peer, inv_diag, source, inv_off, coupling, gathered,
-    out, base_out, tables_out, fold_out, wide,
+    out, base_out, tables_out, wide, buffer,
 ):
     elements, quarter = source.shape
     faces = owner.shape[1]
@@ -139,14 +152,12 @@
     base = (inv_diag[...] * own + product) * mask
     base_out[...] = base
     state = base.astype(BF16).astype(F32)
-    face, fold = lane_tables(quarter, faces)
     target = targets(side[...], peer[...], elements)
     index = lax.broadcasted_iota(jnp.int32, (8, faces), 0)
     both = jnp.where(index == 0, owner[...].astype(F32), target)
-    tables = per_lane(face, both)
+    tables = per_lane(lane_face(quarter, faces), both)
     tables_out[...] = tables
-    fold_out[...] = fold
-    put_transposed(out, coupling, state, tables, fold, elements, quarter, faces)
+    put_transposed(out, coupling, state, tables, buffer, elements, quarter, faces)
 
 
 def merge_kernel(message, first, second, kept):
@@ -166,22 +177,20 @@
         second[0:rows, q * quarter : (q + 1) * quarter] = state
 
 
-def local_sum(states, places, coupling, tables, fold, elements):
+def local_sum(states, places, coupling, tables, elements, quarter):
     products = dot_nt(states, coupling[...])
     terms = jnp.sum(jnp.where(places == tables[1:2, :], products, 0.0), axis=0, keepdims=True)
-    element = lax.broadcasted_iota(jnp.int32, (elements, fold.shape[1]), 0).astype(F32)
-    spread = jnp.where(element == tables[0:1, :], terms, 0.0)
-    folded = dot_nt(two_parts(spread), fold[...])
-    return folded[0:elements] + folded[elements : 2 * elements]
-
-
-def inner_kernel(tables, fold, coupling, middle, kept, out):
+    element = lax.broadcasted_iota(jnp.int32, (elements, terms.shape[1]), 0).astype(F32)
+    return sum_faces(jnp.where(element == tables[0:1, :], terms, 0.0), quarter)
+
+
+def inner_kernel(tables, coupling, middle, kept, out):
     elements, quarter = kept.shape
     rows = HALF * elements
-    places = lax.broadcasted_iota(jnp.int32, (rows, fold.shape[1]), 0) + rows
+    places = lax.broadcasted_iota(jnp.int32, (rows, tables.shape[1]), 0) + rows
     states = middle[0:rows, 0 : 4 * quarter]
     out[...] = kept[...] + local_sum(
-        states, places.astype(F32), coupling, tables, fold, elements
+        states, places.astype(F32), coupling, tables, elements, quarter
     )
 
 
@@ -208,16 +217,16 @@
     )
 
 
-def couple_kernel(degree, tables, fold, coupling, before, after, inner, *rest):
+def couple_kernel(degree, tables, coupling, before, after, inner, *rest):
     out = rest[-1]
     elements, quarter = inner.shape
     width = 4 * quarter
     mask = mask_of(degree[...], quarter, lax.axis_index("blk") * quarter)
     rows = HALF * elements
     states = jnp.concatenate([before[0:rows, 0:width], after[0:rows, 0:width]], axis=0)
-    index = lax.broadcasted_iota(jnp.int32, (2 * rows, fold.shape[1]), 0)
+    index = lax.broadcasted_iota(jnp.int32, (2 * rows, tables.shape[1]), 0)
     places = jnp.where(index >= rows, index + rows, index).astype(F32)
-    coupled = inner[...] + local_sum(states, places, coupling, tables, fold, elements)
+    coupled = inner[...] + local_sum(states, places, coupling, tables, elements, quarter)
     for sent in (before, after):
         pair = sent[rows:, 0:quarter].astype(F32)
         coupled = coupled + (pair[0:elements] + pair[elements : 2 * elements])
@@ -240,7 +249,7 @@
 
 
 def sweep_kernel(
-    degree, tables, fold, coupling, inv_diag, inv_off, base, gathered, out, weight_out, wide
+    degree, tables, coupling, inv_diag, inv_off, base, gathered, out, weight_out, wide, buffer
 ):
     elements, quarter = base.shape
     faces = coupling.shape[0] // quarter
@@ -248,7 +257,7 @@
     mask = mask_of(degree[...], quarter, blk * quarter)
     adjoint = update(inv_diag, inv_off, base, gathered, mask, blk, wide)
     state = adjoint.astype(BF16).astype(F32)
-    put_transposed(out, coupling, state, tables[...], fold[...], elements, quarter, faces)
+    put_transposed(out, coupling, state, tables, buffer, elements, quarter, faces)
     weight_out[...] = (gathered[0, :, 128:640] + gathered[1, :, 128:640]) + (
         gathered[2, :, 128:640] + gathered[3, :, 128:640]
     )
@@ -295,22 +304,22 @@
     coupling = coupling.reshape(faces * quarter, width)
     inv_off = inv_off.reshape(elements * quarter, width)
     wide = [pltpu.VMEM((elements, width), F32)]
+    buffer = [pltpu.VMEM((elements, 8 * quarter), F32)]
     across = lambda x: lax.all_to_all(x, "blk", 0, 0)
     group = lambda x: lax.all_to_all(x, ("dom", "blk"), 0, 0, axis_index_groups=groups)
 
     gathered = across(call(first_kernel, shape(4, elements, 128, kind=BF16), degree, source, far=2, cost=pl.CostEstimate(flops=COST, transcendentals=0, bytes_accessed=1 << 12)))
     message_shape = shape(16, elements, 384, kind=BF16)
     lanes = faces * quarter
-    message, base, tables, fold = call(
+    message, base, tables = call(
         base_kernel,
         (
             message_shape,
             shape(elements, quarter),
             shape(8, lanes),
-            shape(quarter, lanes, kind=BF16),
         ),
         degree, *faces_of, inv_diag, source, inv_off, coupling, gathered,
-        scratch=wide,
+        scratch=[*wide, *buffer],
     )
     for sweep in range(SWEEPS):
         hop_shape = shape(HALF * elements + 2 * elements, 384, kind=BF16)
@@ -319,7 +328,9 @@
         )
         before = hop(second, HALF)
         after = hop(first, -HALF)
-        inner = call(inner_kernel, shape(elements, quarter), tables, fold, coupling, first, kept)
+        inner = call(
+            inner_kernel, shape(elements, quarter), tables, coupling, first, kept
+        )
         if sweep == 0:
             weight = call(
                 weight_kernel, shape(elements, 512),
@@ -329,15 +340,15 @@
         coupled = call(
             couple_kernel,
             shape(4, elements, 640) if sweep == 0 else shape(4, elements, 128, kind=BF16),
-            degree, tables, fold, coupling, before, after, inner, *extra,
+            degree, tables, coupling, before, after, inner, *extra,
         )
         gathered = across(coupled)
         if sweep == 0:
             message, weight = call(
                 sweep_kernel,
                 (message_shape, shape(elements, 512)),
-                degree, tables, fold, coupling, inv_diag, inv_off, base, gathered,
-                scratch=wide,
+                degree, tables, coupling, inv_diag, inv_off, base, gathered,
+                scratch=[*wide, *buffer],
             )
     adjoint, indicator = call(
         last_kernel,

time: 79.1 us -> 78.8 us (level)
  transfers between devices with their start and end apart: 4 -> 4, of which waited for: 2 -> 2; matrix products, arithmetic and copies ran while one was open for 0% -> 0% of each run, Pallas kernels for 3% -> 2%
where the time goes in v6:
time: 78.8 us; the launch traced here: 78.4 us
  blocking collectives  45.1 us (57%)
  starting transfers between devices  23.5 us (30%)
  Pallas kernels  7.56 us (10%)
  waiting for transfers between devices  1.31 us (2%)
  between operations  0.84 us (1%)
    all_to_all x3, blocking collectives, local(): across = lambda x: lax.all_to_all(x, 'blk', 0, 0)  28.6 us
    ppermute x4, starting transfers between devices, hop(): lax.ppermute(block, 'dom', [(i, (i + distance) % count) for i in range(co...  23.5 us
    all_to_all x2, blocking collectives, local(): lax.all_to_all(x, ('dom', 'blk'), 0, 0, axis_index_groups=groups)  16.5 us
    pallas_call x11, Pallas kernels, call(): pl.pallas_call(body, out_shape=shapes, in_specs=[space(i) for i in range(...  7.56 us
  transfers between devices with their start and end apart: 4, of which 2 were waited for; matrix products, arithmetic and copies ran while one was open for 0% of the time, Pallas kernels for 2%

profile of v6, /device:TPU:8, one launch (start us, length us, event | category | flops | bytes accessed | tf_op | source)
XLA Modules:
  0.0 78.4 jit_solution(12181793845703222730)
XLA Ops:
  0.6 0.0 copy-start
  0.6 0.0 copy-start.1
  0.7 0.0 copy-start.2
  0.7 0.0 copy-start.3
  0.7 0.0 copy-start.4
  0.7 0.0 copy-start.6
  0.7 0.0 copy-start.7
  0.7 0.0 copy-start.8
  0.7 0.9 %shard_map.104 = bf16[4,8,128]{2,1,0:T(8,128)(2,1)S(1)} custom-call(s32[1,8]{1,0:T(1,128)} %bitcast.17, f32[8,80]{1,0:T(8,128)} %source.1), custom_call_target="tpu_custom_call" | custom-call | flops 20000000000 | bytes 4096 | tf_op jit(solution)/shard_map/pallas_call | solution.py:279
  1.7 0.0 copy-start.5
  1.7 12.0 %all_to_all.25.gathered = bf16[4,8,128]{2,1,0:T(8,128)(2,1)S(1)} all-to-all(bf16[4,8,128]{2,1,0:T(8,128)(2,1)S(1)} %shard_map.104), channel_id=1, replica_groups=mesh['dom'=128,'blk'=4] {'blk'}, dimensions={0} | all-to-all | bytes 16384 | tf_op jit(solution)/shard_map/all_to_all | solution.py:308
  13.7 0.0 copy-done
  13.7 0.0 copy-done.1
  13.7 0.0 copy-done.2
  13.7 0.0 copy-done.3
  13.7 0.0 copy-done.4
  13.7 0.0 copy-done.6
  13.7 0.0 copy-done.7
  13.7 0.0 copy-done.8
  13.7 1.0 %shard_map.105 = (bf16[16,8,384]{2,1,0:T(8,128)(2,1)S(1)}, f32[8,80]{1,0:T(8,128)S(1)}, f32[8,2560]{1,0:T(8,128)S(1)}) custom-call(s32[1,8]{1,0:T(1,128)S(1)} %bitcast.18, s32[1,32]{1,0:T(1,128)S(1)} %bitcast.24, s32[1,32]{1,0:T(1,128)S(1)} %bitcast.25, s32[1,32]{1,0:T(1,128)S(1)} %bitcast.26, f32[8,80]{1,0:T(8,128)S(1)} %copy-done.2, ...), custom_call_target="tpu_custom_call" | custom-call | tf_op jit(solution)/shard_map/pallas_call | solution.py:279
  14.7 8.3 %all_to_all.26.message = bf16[16,8,384]{2,1,0:T(8,128)(2,1)S(1)} all-to-all(bf16[16,8,384]{2,1,0:T(8,128)(2,1)S(1)} %get-tuple-element.17), channel_id=1, replica_groups={{4,5,6,7,12,13,14,15,0,1,2,3,8,9,10,11},{20,21,22,23,28,29,30,31,16,17,..., dimensions={0} | all-to-all | bytes 196608 | tf_op jit(solution)/shard_map/all_to_all | solution.py:309
  23.0 0.1 shard_map.106
  23.1 3.1 %collective-permute-start = (bf16[48,384]{1,0:T(8,128)(2,1)S(1)}, bf16[48,384]{1,0:T(8,128)(2,1)S(1)}, u32[]{:S(2)}, u32[]{:S(2)}) collective-permute-start(bf16[48,384]{1,0:T(8,128)(2,1)S(1)} %get-tuple-element.18), channel_id=1, source_target_pairs={{0,16},{4,20},{8,24},{12,28},{16,32},{20,36},{24,40},{28,44},{32,4... | collective-permute-start | bytes 110600 | tf_op jit(solution)/shard_map/ppermute | solution.py:291
  26.2 9.9 %collective-permute-start.1 = (bf16[48,384]{1,0:T(8,128)(2,1)S(1)}, bf16[48,384]{1,0:T(8,128)(2,1)S(1)}, u32[]{:S(2)}, u32[]{:S(2)}) collective-permute-start(bf16[48,384]{1,0:T(8,128)(2,1)S(1)} %get-tuple-element.19.middle), channel_id=1, source_target_pairs={{0,496},{4,500},{8,504},{12,508},{16,0},{20,4},{24,8},{28,12},{32,... | collective-permute-start | bytes 110600 | tf_op jit(solution)/shard_map/ppermute | solution.py:291
  36.1 0.0 copy-done.5
  36.1 0.3 shard_map.108.rest_0_
  36.4 0.8 %shard_map.107.inner = f32[8,80]{1,0:T(8,128)S(1)} custom-call(f32[8,2560]{1,0:T(8,128)S(1)} %get-tuple-element.16.tables, bf16[2560,320]{1,0:T(8,128)(2,1)S(1)} %bitcast.8, bf16[48,384]{1,0:T(8,128)(2,1)S(1)} %get-tuple-element.19.middle, f32[8,80]{1,0:T(8,128)S(1)} %get-tuple-element.20.kept), custom_call_target="tpu_custom_call" | custom-call | tf_op jit(solution)/shard_map/pallas_call | solution.py:279
  37.2 0.0 collective-permute-done.before
  37.2 0.5 collective-permute-done.1.after
  37.7 0.8 %shard_map.109 = f32[4,8,640]{2,1,0:T(8,128)S(1)} custom-call(s32[1,8]{1,0:T(1,128)S(1)} %bitcast.20, f32[8,2560]{1,0:T(8,128)S(1)} %get-tuple-element.16.tables, bf16[2560,320]{1,0:T(8,128)(2,1)S(1)} %bitcast.9, bf16[48,384]{1,0:T(8,128)(2,1)S(1)} %collective-permute-done.before, bf16[48,384]{1,0:T(8,128)(2,1)S(1)} %collective-permute-done.1.after, ...), custom_call_target="tpu_custom_call" | custom-call | tf_op jit(solution)/shard_map/pallas_call | solution.py:279
  38.6 8.5 %all_to_all.27.gathered = f32[4,8,640]{2,1,0:T(8,128)S(1)} all-to-all(f32[4,8,640]{2,1,0:T(8,128)S(1)} %shard_map.109), channel_id=1, replica_groups=mesh['dom'=128,'blk'=4] {'blk'}, dimensions={0} | all-to-all | bytes 163840 | tf_op jit(solution)/shard_map/all_to_all | solution.py:308
  47.0 1.0 %shard_map.110 = (bf16[16,8,384]{2,1,0:T(8,128)(2,1)S(1)}, f32[8,512]{1,0:T(8,128)S(1)}) custom-call(s32[1,8]{1,0:T(1,128)S(1)} %bitcast.21, f32[8,2560]{1,0:T(8,128)S(1)} %get-tuple-element.16.tables, bf16[2560,320]{1,0:T(8,128)(2,1)S(1)} %bitcast.10, f32[8,80]{1,0:T(8,128)S(1)} %copy-done.2, bf16[640,320]{1,0:T(8,128)(2,1)S(1)} %bitcast.15, ...), custom_call_target="tpu_custom_call" | custom-call | tf_op jit(solution)/shard_map/pallas_call | solution.py:279
  48.0 8.3 %all_to_all.28.message = bf16[16,8,384]{2,1,0:T(8,128)(2,1)S(1)} all-to-all(bf16[16,8,384]{2,1,0:T(8,128)(2,1)S(1)} %get-tuple-element.22), channel_id=1, replica_groups={{4,5,6,7,12,13,14,15,0,1,2,3,8,9,10,11},{20,21,22,23,28,29,30,31,16,17,..., dimensions={0} | all-to-all | bytes 196608 | tf_op jit(solution)/shard_map/all_to_all | solution.py:309
  56.3 0.1 shard_map.111
  56.4 2.9 %collective-permute-start.2 = (bf16[48,384]{1,0:T(8,128)(2,1)S(1)}, bf16[48,384]{1,0:T(8,128)(2,1)S(1)}, u32[]{:S(2)}, u32[]{:S(2)}) collective-permute-start(bf16[48,384]{1,0:T(8,128)(2,1)S(1)} %get-tuple-element.23), channel_id=1, source_target_pairs={{0,16},{4,20},{8,24},{12,28},{16,32},{20,36},{24,40},{28,44},{32,4... | collective-permute-start | bytes 110600 | tf_op jit(solution)/shard_map/ppermute | solution.py:291
  59.3 7.5 %collective-permute-start.3 = (bf16[48,384]{1,0:T(8,128)(2,1)S(1)}, bf16[48,384]{1,0:T(8,128)(2,1)S(1)}, u32[]{:S(2)}, u32[]{:S(2)}) collective-permute-start(bf16[48,384]{1,0:T(8,128)(2,1)S(1)} %get-tuple-element.24.middle), channel_id=1, source_target_pairs={{0,496},{4,500},{8,504},{12,508},{16,0},{20,4},{24,8},{28,12},{32,... | collective-permute-start | bytes 110600 | tf_op jit(solution)/shard_map/ppermute | solution.py:291
  66.9 0.8 %shard_map.112.inner = f32[8,80]{1,0:T(8,128)S(1)} custom-call(f32[8,2560]{1,0:T(8,128)S(1)} %get-tuple-element.16.tables, bf16[2560,320]{1,0:T(8,128)(2,1)S(1)} %bitcast.11, bf16[48,384]{1,0:T(8,128)(2,1)S(1)} %get-tuple-element.24.middle, f32[8,80]{1,0:T(8,128)S(1)} %get-tuple-element.25.kept), custom_call_target="tpu_custom_call" | custom-call | tf_op jit(solution)/shard_map/pallas_call | solution.py:279
  67.7 0.0 collective-permute-done.2.before
  67.7 0.8 %collective-permute-done.3.after = bf16[48,384]{1,0:T(8,128)(2,1)S(1)} collective-permute-done((bf16[48,384]{1,0:T(8,128)(2,1)S(1)}, bf16[48,384]{1,0:T(8,128)(2,1)S(1)}, u32[]{:S(2)}, u32[]{:S(2)}) %collective-permute-start.3) | collective-permute-done | bytes 36896 | tf_op jit(solution)/shard_map/ppermute | solution.py:291
  68.5 0.8 %shard_map.113 = bf16[4,8,128]{2,1,0:T(8,128)(2,1)S(1)} custom-call(s32[1,8]{1,0:T(1,128)S(1)} %bitcast.22, f32[8,2560]{1,0:T(8,128)S(1)} %get-tuple-element.16.tables, bf16[2560,320]{1,0:T(8,128)(2,1)S(1)} %bitcast.12, bf16[48,384]{1,0:T(8,128)(2,1)S(1)} %collective-permute-done.2.before, bf16[48,384]{1,0:T(8,128)(2,1)S(1)} %collective-permute-done.3.after, ...), custom_call_target="tpu_custom_call" | custom-call | tf_op jit(solution)/shard_map/pallas_call | solution.py:279
  69.3 8.1 %all_to_all.29.gathered = bf16[4,8,128]{2,1,0:T(8,128)(2,1)S(1)} all-to-all(bf16[4,8,128]{2,1,0:T(8,128)(2,1)S(1)} %shard_map.113), channel_id=1, replica_groups=mesh['dom'=128,'blk'=4] {'blk'}, dimensions={0} | all-to-all | bytes 16384 | tf_op jit(solution)/shard_map/all_to_all | solution.py:308
  77.4 0.9 %shard_map.114 = (f32[8,80]{1,0:T(8,128)}, f32[1,8]{1,0:T(1,128)}) custom-call(s32[1,8]{1,0:T(1,128)S(1)} %bitcast.23, f32[8,80]{1,0:T(8,128)S(1)} %copy-done.2, bf16[640,320]{1,0:T(8,128)(2,1)S(1)} %bitcast.16, f32[8,80]{1,0:T(8,128)S(1)} %get-tuple-element.15.base, f32[8,512]{1,0:T(8,128)S(1)} %get-tuple-element.21.weight, ...), custom_call_target="tpu_custom_call" | custom-call | tf_op jit(solution)/shard_map/pallas_call | solution.py:279
Async XLA Ops:
  0.6 13.0 %copy-start = (bf16[32,80,320]{2,1,0:T(8,128)(2,1)S(1)}, bf16[32,80,320]{2,1,0:T(8,128)(2,1)}, u32[]{:S(2)}) copy-start(bf16[32,80,320]{2,1,0:T(8,128)(2,1)} %param.13) | copy-start | bytes 4915204
  0.6 13.0 %copy-start.1 = (bf16[8,80,320]{2,1,0:T(8,128)(2,1)S(1)}, bf16[8,80,320]{2,1,0:T(8,128)(2,1)}, u32[]{:S(2)}) copy-start(bf16[8,80,320]{2,1,0:T(8,128)(2,1)} %param.15) | copy-start | bytes 1228804
  0.7 13.0 %copy-start.2 = (f32[8,80]{1,0:T(8,128)S(1)}, f32[8,80]{1,0:T(8,128)}, u32[]{:S(2)}) copy-start(f32[8,80]{1,0:T(8,128)} %inv_diag.7) | copy-start | bytes 7684
  0.7 13.0 %copy-start.3 = (s32[8]{0:T(128)S(1)}, s32[8]{0:T(128)}, u32[]{:S(2)}) copy-start(s32[8]{0:T(128)} %param.9) | copy-start | bytes 100
  0.7 13.0 %copy-start.4 = (f32[8,80]{1,0:T(8,128)S(1)}, f32[8,80]{1,0:T(8,128)}, u32[]{:S(2)}) copy-start(f32[8,80]{1,0:T(8,128)} %source.1) | copy-start | bytes 7684
  0.7 13.0 %copy-start.6 = (s32[32]{0:T(128)S(1)}, s32[32]{0:T(128)}, u32[]{:S(2)}) copy-start(s32[32]{0:T(128)} %param.10) | copy-start | bytes 388
  0.7 13.0 %copy-start.7 = (s32[32]{0:T(128)S(1)}, s32[32]{0:T(128)}, u32[]{:S(2)}) copy-start(s32[32]{0:T(128)} %param.11) | copy-start | bytes 388
  0.7 13.0 %copy-start.8 = (s32[32]{0:T(128)S(1)}, s32[32]{0:T(128)}, u32[]{:S(2)}) copy-start(s32[32]{0:T(128)} %param.12) | copy-start | bytes 388
  1.7 34.4 %copy-start.5 = (f32[8,80]{1,0:T(8,128)S(1)}, f32[8,80]{1,0:T(8,128)}, u32[]{:S(2)}) copy-start(f32[8,80]{1,0:T(8,128)} %residual.1) | copy-start | bytes 7684
  23.1 14.1 %collective-permute-start = (bf16[48,384]{1,0:T(8,128)(2,1)S(1)}, bf16[48,384]{1,0:T(8,128)(2,1)S(1)}, u32[]{:S(2)}, u32[]{:S(2)}) collective-permute-start(bf16[48,384]{1,0:T(8,128)(2,1)S(1)} %get-tuple-element.18), channel_id=1, source_target_pairs={{0,16},{4,20},{8,24},{12,28},{16,32},{20,36},{24,40},{28,44},{32,4... | collective-permute-start | bytes 110600 | tf_op jit(solution)/shard_map/ppermute | solution.py:291
  26.2 11.5 %collective-permute-start.1 = (bf16[48,384]{1,0:T(8,128)(2,1)S(1)}, bf16[48,384]{1,0:T(8,128)(2,1)S(1)}, u32[]{:S(2)}, u32[]{:S(2)}) collective-permute-start(bf16[48,384]{1,0:T(8,128)(2,1)S(1)} %get-tuple-element.19.middle), channel_id=1, source_target_pairs={{0,496},{4,500},{8,504},{12,508},{16,0},{20,4},{24,8},{28,12},{32,... | collective-permute-start | bytes 110600 | tf_op jit(solution)/shard_map/ppermute | solution.py:291
  56.4 11.3 %collective-permute-start.2 = (bf16[48,384]{1,0:T(8,128)(2,1)S(1)}, bf16[48,384]{1,0:T(8,128)(2,1)S(1)}, u32[]{:S(2)}, u32[]{:S(2)}) collective-permute-start(bf16[48,384]{1,0:T(8,128)(2,1)S(1)} %get-tuple-element.23), channel_id=1, source_target_pairs={{0,16},{4,20},{8,24},{12,28},{16,32},{20,36},{24,40},{28,44},{32,4... | collective-permute-start | bytes 110600 | tf_op jit(solution)/shard_map/ppermute | solution.py:291
  59.3 9.2 %collective-permute-start.3 = (bf16[48,384]{1,0:T(8,128)(2,1)S(1)}, bf16[48,384]{1,0:T(8,128)(2,1)S(1)}, u32[]{:S(2)}, u32[]{:S(2)}) collective-permute-start(bf16[48,384]{1,0:T(8,128)(2,1)S(1)} %get-tuple-element.24.middle), channel_id=1, source_target_pairs={{0,496},{4,500},{8,504},{12,508},{16,0},{20,4},{24,8},{28,12},{32,... | collective-permute-start | bytes 110600 | tf_op jit(solution)/shard_map/ppermute | solution.py:291
